TPU v7x, 32 devices: a whole 2x2x4 slice. The times are simulated.
32 devices in a mesh: row: 4 (over z), col: 8 (over y, x, core).
Axes of the slice: x: 2, y: 2, z: 4, core: 2. Of those that a mesh axis runs over, the one named last changes fastest.
Arguments:
- precision_diag: float32 [32, 256, 256], P(('row', 'col')), may hold values from -0.1 to 4.6, as said below
- precision_pairs: float32 [32, 7, 256, 256], P(('row', 'col')), may hold values from -0.024 to 0.024
- pattern_cols: int32 [32, 7], P(('row', 'col')), may hold values from -1 to 31, as said below
- newton_diag: float32 [32, 256, 256], P(('row', 'col')), may hold values from -0.1 to 0.1, as said below
- newton_pairs: float32 [32, 7, 256, 256], P(('row', 'col')), may hold values from -0.006 to 0.006
- warm_start: float32 [32, 96, 256], P(('row', 'col')), may hold values from -15 to 15
- target_rows: int32 [96], replicated, may hold values from 0 to 8191, as said below
Outputs:
- inverse_panel: float32 [32, 96, 256], P(('row', 'col'))
- hessian_block: float32 [96, 96], P('row', 'col')
Inputs may be any that keep to these rules, and one draw needn't show every extreme that they name: `pattern_cols`: each row lists its live entries first and -1 for the rest; it has 4 to 7 live entries, some row exactly 7 and some fewer. The live entries of block row I are distinct, differ from I, and lie in the group of 8 consecutive block rows that holds I (groups start at multiples of 8). `precision_diag`: each tile is symmetric, and X is positive definite. `newton_diag`: each tile is symmetric. `target_rows`: the 96 entries are distinct rows of X.
All inputs are finite; a program needn't handle non-finite values.
Results may differ from a plain program's by a relative error of at most 0.0003.
Values sent between devices are 32-bit elements; how exact they have to be, the bound alone decides.
No kernel may reach another device: no remote copies, remote signals or barrier semaphores. Data moves between devices by JAX's collectives and lax.ppermute only.
A program may use at most 64 MiB of HBM per device.

v0:
```python
import functools

import jax
import jax.numpy as jnp
from jax import lax
from jax.experimental import pallas as pl
from jax.experimental.pallas import tpu as pltpu
from jax.sharding import Mesh, PartitionSpec as P


F32 = jnp.float32
BF16 = jnp.bfloat16
ALL = ("row", "chip", "core")
GRANT = 24 << 20
LANES = 128
HALF = 64

NT = (((1,), (1,)), ((), ()))
NN = (((1,), (0,)), ((), ()))


def split(value):
    high = value.astype(BF16)
    low = (value - high.astype(F32)).astype(BF16)
    return high, low


def dot3(left, right, dims):
    rows = left[0].shape[0]
    both = jnp.concatenate(left, axis=0)
    first = lax.dot_general(both, right[0], dims, preferred_element_type=F32)
    second = lax.dot_general(left[0], right[1], dims, preferred_element_type=F32)
    return first[:rows] + first[rows:] + second


def dot_full(left, right, dims):
    return lax.dot_general(
        left, right, dims, precision=lax.Precision.HIGHEST, preferred_element_type=F32
    )


def row_sums(product):
    return dot_full(jnp.ones((8, product.shape[1]), F32), product, NT)[0:1]


def column_of(row):
    n = row.shape[1]
    eye = lax.broadcasted_iota(jnp.int32, (n, n), 0) == lax.broadcasted_iota(
        jnp.int32, (n, n), 1
    )
    return jnp.sum(jnp.where(eye, row, 0.0), axis=1, keepdims=True)


class Far:
    def __init__(self, array, anywhere=False):
        self.stacked = isinstance(array, (tuple, list))
        self.arrays = list(array) if self.stacked else [array]
        if not anywhere:
            self.arrays = [
                pltpu.with_memory_space_constraint(a, pltpu.HBM) for a in self.arrays
            ]
        first = self.arrays[0]
        self.shape = (len(self.arrays),) * self.stacked + first.shape
        self.pieces = self.shape[0] if len(self.shape) == 3 else 1
        self.dtype = first.dtype

    def copies(self, refs, buffer, sems):
        for k in range(self.pieces):
            if self.stacked:
                source, target = refs[k], buffer.at[k]
            elif len(self.shape) == 3:
                source, target = refs[0].at[k], buffer.at[k]
            else:
                source, target = refs[0], buffer
            yield pltpu.make_async_copy(source, target, sems.at[k])


class Fetched:
    def __init__(self, copies, ref):
        self.copies, self.ref, self.shape = copies, ref, ref.shape

    def wait(self):
        for copy in self.copies:
            copy.wait()
        self.copies = []
        return self.ref

    def all(self):
        return self.wait()[...]


def call(body, outs, scalars, operands, scratch=(), flops=0):
    flat, plan = [], []
    for one in operands:
        arrays = one.arrays if isinstance(one, Far) else one
        if not isinstance(arrays, (tuple, list)):
            arrays = [arrays]
        plan.append((one, len(flat), len(arrays)))
        flat.extend(arrays)
    fars = [one for one, _, _ in plan if isinstance(one, Far)]
    smem = pl.BlockSpec(memory_space=pltpu.SMEM)
    vmem = pl.BlockSpec(memory_space=pltpu.VMEM)
    specs = [smem] * len(scalars)
    for one, _, length in plan:
        specs += [pl.BlockSpec(memory_space=pl.ANY) if isinstance(one, Far) else vmem] * length

    def kernel(*refs):
        given, refs = refs[: len(scalars)], refs[len(scalars) :]
        arrays, refs = refs[: len(flat)], refs[len(flat) :]
        out, refs = refs[: len(outs)], refs[len(outs) :]
        mine, refs = refs[: len(scratch)], refs[len(scratch) :]
        buffers, sems = refs[: len(fars)], refs[len(fars) :]
        seen, at = [], 0
        for one, first, length in plan:
            if isinstance(one, Far):
                copies = list(
                    one.copies(arrays[first : first + length], buffers[at], sems[at])
                )
                for copy in copies:
                    copy.start()
                seen.append(Fetched(copies, buffers[at]))
                at += 1
            elif isinstance(one, (tuple, list)):
                seen.append(arrays[first : first + length])
            else:
                seen.append(arrays[first])
        body(*given, *seen, *out, *mine)

    outs = [o if isinstance(o, jax.ShapeDtypeStruct) else jax.ShapeDtypeStruct(o, F32) for o in outs]
    scratch = [o if isinstance(o, jax.ShapeDtypeStruct) else jax.ShapeDtypeStruct(o, F32) for o in scratch]
    return pl.pallas_call(
        kernel,
        out_shape=outs,
        in_specs=specs,
        out_specs=[vmem] * len(outs),
        scratch_shapes=[pltpu.VMEM(o.shape, o.dtype) for o in scratch]
        + [pltpu.VMEM(one.shape, one.dtype) for one in fars]
        + [pltpu.SemaphoreType.DMA((one.pieces,)) for one in fars],
        cost_estimate=pl.CostEstimate(
            flops=flops,
            bytes_accessed=sum(a.size * a.dtype.itemsize for a in flat),
            transcendentals=0,
        ),
        compiler_params=pltpu.CompilerParams(vmem_limit_bytes=GRANT),
    )(*scalars, *flat)


class Way:
    def __init__(self, chips):
        self.chips, self.power = chips, chips & (chips - 1) == 0

    def pairs(self, k):
        n = self.chips
        return [(i, i ^ k if self.power else (i + k) % n) for i in range(n)]

    def to(self, here, there):
        n = self.chips
        return there ^ here if self.power else lax.rem(there - here + n, n)

    def source(self, k):
        return k if self.power else (self.chips - k) % self.chips


def seats(way, meta, count):
    chip, core = meta[count], meta[count + 1]
    found = []
    for k in range(count):
        slot = jnp.maximum(meta[k], 0)
        kind = jnp.where(slot % 2 == core, 0, way.chips)
        found.append(
            jnp.where(meta[k] >= 0, kind + way.to(chip, slot // 2), 2 * way.chips)
        )
    return found


def contributions(way, meta, pairs, panel, work, keep, send):
    chips = way.chips
    work[0 : 2 * chips] = jnp.zeros((2 * chips,) + work.shape[1:], F32)
    for seat, pair in zip(seats(way, meta, len(pairs)), pairs):
        work[seat] = dot3(panel, pair(), NN)
    keep[...] = work[0:chips]
    send[...] = work[chips : 2 * chips]


def hold(gathered, held):
    for k, block in enumerate(gathered):
        high, low = split(block[...])
        rows = high.shape[0]
        held[k, 0:rows] = high
        held[k, rows : 2 * rows] = low
    held[len(gathered)] = jnp.zeros(held.shape[1:], BF16)


def off_diagonal(way, meta, pairs, held):
    rows = held.shape[1] // 2
    first = second = None
    for seat, pair in zip(seats(way, meta, len(pairs)), pairs):
        both, (high, low) = held[seat], pair()
        one = lax.dot_general(both, high, NT, preferred_element_type=F32)
        two = lax.dot_general(both[:rows], low, NT, preferred_element_type=F32)
        first = one if first is None else first + one
        second = two if second is None else second + two
    return first[:rows] + (first[rows:] + second)


def held_pairs(split_tiles):
    return [
        functools.partial(lambda k: (split_tiles[0, k], split_tiles[1, k]), k)
        for k in range(split_tiles.shape[1])
    ]


def fresh_pairs(tiles):
    return [
        functools.partial(lambda k: split(tiles.ref[k]), k)
        for k in range(tiles.shape[0])
    ]


def first_kernel(way, meta, panel, tiles, keep, send, work):
    tiles.wait()
    contributions(way, meta, fresh_pairs(tiles), split(panel[...]), work, keep, send)


def prepare_kernel(panel, diag, tiles, image, split_tiles):
    image[...] = dot_full(panel[...], diag.all(), NT)
    tiles.wait()
    for k in range(tiles.shape[0]):
        split_tiles[0, k], split_tiles[1, k] = split(tiles.ref[k])


def residual_kernel(
    way, meta, base, target, gathered, split_tiles, added, residual, keep, send, work, held
):
    pairs = held_pairs(split_tiles)
    hold(gathered, held)
    total = base[...] + off_diagonal(way, meta, pairs, held)
    for block in added:
        total = total + block[...]
    rows, size = residual.shape
    unit = target[...] == lax.broadcasted_iota(jnp.int32, (rows, size), 1)
    value = unit.astype(F32) - total
    residual[...] = value
    contributions(way, meta, pairs, split(value), work, keep, send)


def image_kernel(way, meta, panel, base, gathered, split_tiles, added, image, sums, held):
    hold(gathered, held)
    total = base[...] + off_diagonal(way, meta, held_pairs(split_tiles), held)
    for block in added:
        total = total + block[...]
    image[...] = total
    value = panel[...]
    sums[0:1] = row_sums(value * value)
    sums[1:2] = row_sums(value * total)
    sums[2:3] = row_sums(total * total)


def middle_kernel(
    way,
    parts_rows,
    parts_cols,
    meta,
    sums,
    images,
    starts,
    residuals,
    split_tiles,
    diag,
    newton_diag,
    newton_tiles,
    x_out,
    d_out,
    norm_out,
    keep,
    send,
    held,
    packed,
    order,
    blocks,
    pieces,
):
    n = split_tiles.shape[1]
    totals = sums[0]
    for device in range(1, sums.shape[0]):
        totals = totals + sums[device]
    rr, rq, qq = totals[0:1], totals[1:2], totals[2:3]
    step = rr / rq
    norm = rr - 2.0 * step * rq + step * step * qq
    norm_out[...] = norm
    step_col = column_of(step)
    grow = 1.0 + column_of(norm / rr)
    count, _ = x_out.shape
    starts.wait()
    residuals.wait()
    for k, image in enumerate(images):
        r = residuals.ref[k]
        x = starts.ref[k] + step_col * r
        d = grow * r - step_col * image[...]
        if k == 0:
            x_out[...] = x
            d_out[...] = d
        held[k, 0:count], held[k, 3 * count : 4 * count] = split(x)
        held[k, count : 2 * count], held[k, 2 * count : 3 * count] = split(d)
    held[len(images)] = jnp.zeros(held.shape[1:], BF16)
    x1, d1 = x_out[...], d_out[...]
    found = seats(way, meta, n)

    def product(rows, tile):
        return lax.dot_general(rows, tile, NT, preferred_element_type=F32)

    high, low = split(diag.all() * 0.5)
    own = held[0]
    first = product(own[count : 3 * count], high)
    second = product(own[count : 2 * count], low)
    for k in range(n):
        block = held[found[k]]
        first += product(block[count : 3 * count], split_tiles[0, k])
        second += product(block[count : 2 * count], split_tiles[1, k])
    half_d = first[:count] + (first[count:] + second)
    curvature = 2.0 * row_sums(d1 * half_d)
    high, low = split(newton_diag.all() * 0.5)
    first = product(own, high)
    second = product(own[: 2 * count], low)
    newton_tiles.wait()
    for k in range(n):
        block = held[found[k]]
        high, low = split(newton_tiles.ref[k])
        first += product(block, high)
        second += product(block[: 2 * count], low)
    ux = first[:count] + (first[3 * count :] + second[:count])
    ud = first[count : 2 * count] + (first[2 * count : 3 * count] + second[count:])
    hr, hc = count // parts_rows, count // parts_cols
    for r_index in range(parts_rows):
        for kind, pair in enumerate(((x1, ux), (d1, ud))):
            at = (2 * r_index + kind) * hr
            for side in range(2):
                order[side, at : at + hr] = pair[side][
                    r_index * hr : (r_index + 1) * hr
                ]
    blocks[...] = dot_full(
        jnp.concatenate([x1, d1], axis=0), order[1], NT
    ) + dot_full(jnp.concatenate([ux, ud], axis=0), order[0], NT)
    core = meta[n + 1]
    for r_index in range(parts_rows):
        lanes = slice(2 * r_index * hr, 2 * (r_index + 1) * hr)
        pieces[:, 0 : 2 * hr] = blocks[0:count, lanes]
        pieces[:, HALF : HALF + 2 * hr] = blocks[count : 2 * count, lanes]
        for c_index in range(parts_cols):
            at = r_index * (parts_cols // 2) + c_index // 2
            target = packed.at[c_index % 2, at]
            target[0:hc] = pieces[c_index * hc : (c_index + 1) * hc]
            target[hc : hc + 1, 0:count] = curvature
    keep[...] = packed[core]
    send[...] = packed[1 - core]


def last_kernel(parts_rows, parts_cols, n, meta, received, norm, x1, d1, x_out, hessian):
    total = received[0]
    for device in range(1, received.shape[0]):
        total = total + received[device]
    count = x1.shape[0]
    hr, hc = count // parts_rows, count // parts_cols
    step = norm[...] / total[hc : hc + 1, 0:count]
    step_col = column_of(step)
    x_out[...] = x1[...] + step_col * d1[...]
    row_at, col_at = meta[n + 2] * hr, (meta[n] * 2 + meta[n + 1]) * hc
    wanted = lax.broadcasted_iota(jnp.int32, (count, hr), 0) == row_at + (
        lax.broadcasted_iota(jnp.int32, (count, hr), 1)
    )
    of_rows = jnp.sum(jnp.where(wanted, step_col, 0.0), axis=0, keepdims=True)
    wanted = lax.broadcasted_iota(jnp.int32, (hc, count), 1) == col_at + (
        lax.broadcasted_iota(jnp.int32, (hc, count), 0)
    )
    of_cols = jnp.sum(jnp.where(wanted, step, 0.0), axis=1, keepdims=True)
    xx = total[0:hc, 0:hr]
    dx = total[0:hc, hr : 2 * hr]
    xd = total[0:hc, HALF : HALF + hr]
    dd = total[0:hc, HALF + hr : HALF + 2 * hr]
    hessian[...] = xx + of_rows * dx + of_cols * (xd + of_rows * dd)


def on_device(
    precision_diag,
    precision_pairs,
    pattern_cols,
    newton_diag,
    newton_pairs,
    warm_start,
    target_rows,
):
    groups = lax.axis_size("row")
    chips = lax.axis_size("chip")
    columns = chips * 2
    devices = groups * columns
    row, chip, core = (lax.axis_index(a).astype(jnp.int32) for a in ALL)
    block = row * columns + chip * 2 + core
    count, size = warm_start.shape[1:]
    n = precision_pairs.shape[1]
    spot = jnp.arange(n + 3, dtype=jnp.int32)
    slots = jnp.where(pattern_cols >= 0, pattern_cols - row * columns, -1)[0]
    meta = jnp.where(spot == n, chip, jnp.where(spot == n + 1, core, row))
    meta = jnp.where(spot < n, jnp.pad(slots, (0, 3)), meta)
    target = (target_rows - block * size).astype(jnp.int32)[:, None]
    tiles, diag = precision_pairs[0], precision_diag[0]
    ntiles, ndiag = newton_pairs[0], newton_diag[0]
    panel = (count, size)
    stack = (chips, count, size)
    swap = [(0, 1), (1, 0)]
    way = Way(chips)
    unit = 2 * count * size * size * 3
    parts = jax.ShapeDtypeStruct((2, n, size, size), BF16)
    work = (2 * chips + 1,) + panel
    held = jax.ShapeDtypeStruct((2 * chips + 1, 2 * count, size), BF16)

    def gather(value):
        same = [value] + [None] * (chips - 1)
        for k in range(1, chips):
            same[way.source(k)] = lax.ppermute(value, "chip", way.pairs(k))
        return same

    def forward(same):
        return list(same) + [lax.ppermute(block, "core", swap) for block in same]

    def scatter(keep, send):
        received = lax.ppermute(send, "core", swap)
        sums = [keep[k] + received[k] for k in range(chips)]
        return [sums[0]] + [lax.ppermute(sums[k], "chip", way.pairs(k)) for k in range(1, chips)]

    def prepare(value):
        return call(
            prepare_kernel,
            [panel, parts],
            [],
            [value, Far(diag), Far(tiles)],
            flops=4 * unit,
        )

    start = warm_start[0]
    starts = gather(start)
    keep, send = call(
        functools.partial(first_kernel, way),
        [stack, stack],
        [meta],
        [start, Far(tiles)],
        scratch=[work],
        flops=n * unit,
    )
    added = scatter(keep, send)
    starts = forward(starts)
    base, split_tiles = prepare(start)
    residual, keep, send = call(
        functools.partial(residual_kernel, way),
        [panel, stack, stack],
        [meta],
        [base, target, starts, split_tiles, added],
        scratch=[work, held],
        flops=2 * n * unit,
    )
    residuals = gather(residual)
    added = scatter(keep, send)
    residuals = forward(residuals)
    base, split_tiles = prepare(residual)
    image, sums = call(
        functools.partial(image_kernel, way),
        [panel, (3, count)],
        [meta],
        [residual, base, residuals, split_tiles, added],
        scratch=[held],
        flops=n * unit,
    )
    images = gather(image)
    all_sums = lax.all_to_all(
        jnp.broadcast_to(sums[None], (devices,) + sums.shape), ALL, 0, 0, tiled=True
    )
    images = forward(images)
    _, split_tiles = prepare(image)
    hr, hc = count // groups, count // columns
    depth = -(-(hc + 1) // 8) * 8
    share = (devices // 2, depth, LANES)
    x1, d1, norm, keep, send = call(
        functools.partial(middle_kernel, way, groups, columns),
        [panel, panel, (1, count), share, share],
        [meta],
        [
            all_sums,
            images,
            Far(starts, anywhere=True),
            Far(residuals, anywhere=True),
            split_tiles,
            Far(diag),
            Far(ndiag),
            Far(ntiles),
        ],
        scratch=[
            jax.ShapeDtypeStruct((2 * chips + 1, 4 * count, size), BF16),
            (2,) + share,
            (2, 2 * count, size),
            (2 * count, 2 * count),
            (count, LANES),
        ],
        flops=4 * n * unit,
    )
    received = lax.ppermute(send, "core", swap)
    received = lax.all_to_all(keep + received, ("row", "chip"), 0, 0, tiled=True)
    solved, hessian = call(
        functools.partial(last_kernel, groups, columns, n),
        [panel, (hc, hr)],
        [meta],
        [received, norm, x1, d1],
        flops=unit // 100,
    )
    return solved[None], hessian.T


def solution(mesh):
    rows, columns = mesh.devices.shape
    fine = Mesh(mesh.devices.reshape(rows, columns // 2, 2), ALL)
    placed = (
        P(ALL, None, None),
        P(ALL, None, None, None),
        P(ALL, None),
        P(ALL, None, None),
        P(ALL, None, None, None),
        P(ALL, None, None),
        P(),
    )
    return jax.shard_map(
        on_device,
        mesh=fine,
        in_specs=placed,
        out_specs=(P(ALL, None, None), P("row", ("chip", "core"))),
        check_vma=False,
    )
```

profile of v0, /device:TPU:0, one launch (start us, length us, event | category | flops | bytes accessed | tf_op | source)
XLA Modules:
  0.0 87.4 jit_solution(12307304276641686500)
XLA Ops:
  1.3 3.0 %shard_map.87 = (f32[4,96,256]{2,1,0:T(8,128)S(1)}, f32[4,96,256]{2,1,0:T(8,128)S(1)}) custom-call(s32[10]{0:T(128)S(1)} %compare_select_fusion.3.refs_0_, f32[96,256]{1,0:T(8,128)} %bitcast.1.refs_0_.refs_1_.refs_3_.refs_10_, f32[7,256,256]{2,1,0:T(8,128)} %bitcast.27), custom_call_target="tpu_custom_call" | custom-call | flops 264241152 | bytes 1933312 | tf_op jit(solution)/shard_map/pallas_call | solution.py:131
  4.8 3.5 %collective-permute-start.2 = (f32[96,256]{1,0:T(8,128)}, f32[96,256]{1,0:T(8,128)S(1)}, u32[]{:S(2)}, u32[]{:S(2)}) collective-permute-start(f32[96,256]{1,0:T(8,128)} %bitcast.1.refs_0_.refs_1_.refs_3_.refs_10_), channel_id=1, source_target_pairs={{0,6},{2,4},{4,2},{6,0},{1,7},{3,5},{5,3},{7,1},{8,14},{10,12},{12... | collective-permute-start | bytes 294920 | tf_op jit(solution)/shard_map/ppermute | solution.py:419
  9.0 3.0 %collective-permute-done.2.refs_6_.refs_13_ = f32[96,256]{1,0:T(8,128)S(1)} collective-permute-done((f32[96,256]{1,0:T(8,128)}, f32[96,256]{1,0:T(8,128)S(1)}, u32[]{:S(2)}, u32[]{:S(2)}) %collective-permute-start.2) | collective-permute-done | bytes 98336 | tf_op jit(solution)/shard_map/ppermute | solution.py:419
  12.0 2.0 %collective-permute-done.1.refs_5_.refs_12_ = f32[96,256]{1,0:T(8,128)S(1)} collective-permute-done((f32[96,256]{1,0:T(8,128)}, f32[96,256]{1,0:T(8,128)S(1)}, u32[]{:S(2)}, u32[]{:S(2)}) %collective-permute-start.1) | collective-permute-done | bytes 98336 | tf_op jit(solution)/shard_map/ppermute | solution.py:419
  14.6 1.8 %collective-permute-start.10 = (f32[96,256]{1,0:T(8,128)S(1)}, f32[96,256]{1,0:T(8,128)S(1)}, u32[]{:S(2)}, u32[]{:S(2)}) collective-permute-start(f32[96,256]{1,0:T(8,128)S(1)} %get-tuple-element.44), channel_id=1, source_target_pairs={{0,6},{2,4},{4,2},{6,0},{1,7},{3,5},{5,3},{7,1},{8,14},{10,12},{12... | collective-permute-start | bytes 294920 | tf_op jit(solution)/shard_map/ppermute | solution.py:428
  18.3 3.1 %shard_map.86 = (f32[96,256]{1,0:T(8,128)S(1)}, bf16[2,7,256,256]{3,2,1,0:T(8,128)(2,1)S(1)}) custom-call(f32[96,256]{1,0:T(8,128)} %bitcast.1.refs_0_.refs_1_.refs_3_.refs_10_, f32[256,256]{1,0:T(8,128)} %bitcast.31, f32[7,256,256]{2,1,0:T(8,128)} %bitcast.28), custom_call_target="tpu_custom_call" | custom-call | flops 150994944 | bytes 2195456 | tf_op jit(solution)/shard_map/pallas_call | solution.py:131
  22.7 2.6 %shard_map.88 = (f32[96,256]{1,0:T(8,128)S(1)}, f32[4,96,256]{2,1,0:T(8,128)S(1)}, f32[4,96,256]{2,1,0:T(8,128)S(1)}) custom-call(s32[10]{0:T(128)S(1)} %compare_select_fusion.3.refs_0_, f32[96,256]{1,0:T(8,128)S(1)} %get-tuple-element.21.refs_1_, s32[96,1]{1,0:T(8,128)S(1)} %copy.9.refs_2_, f32[96,256]{1,0:T(8,128)} %bitcast.1.refs_0_.refs_1_.refs_3_.refs_10_, ...), custom_call_target="tpu_custom_call" | custom-call | flops 528482304 | bytes 3113344 | tf_op jit(solution)/shard_map/pallas_call | solution.py:131
  25.4 1.6 %collective-permute-start.13 = (f32[96,256]{1,0:T(8,128)S(1)}, f32[96,256]{1,0:T(8,128)S(1)}, u32[]{:S(2)}, u32[]{:S(2)}) collective-permute-start(f32[96,256]{1,0:T(8,128)S(1)} %get-tuple-element.25.refs_0_.refs_1_.refs_3_.refs_18_), channel_id=1, source_target_pairs={{0,6},{2,4},{4,2},{6,0},{1,7},{3,5},{5,3},{7,1},{8,14},{10,12},{12... | collective-permute-start | bytes 294920 | tf_op jit(solution)/shard_map/ppermute | solution.py:419
  27.0 1.5 %collective-permute-start.12 = (f32[96,256]{1,0:T(8,128)S(1)}, f32[96,256]{1,0:T(8,128)S(1)}, u32[]{:S(2)}, u32[]{:S(2)}) collective-permute-start(f32[96,256]{1,0:T(8,128)S(1)} %get-tuple-element.25.refs_0_.refs_1_.refs_3_.refs_18_), channel_id=1, source_target_pairs={{0,4},{2,6},{4,0},{6,2},{1,5},{3,7},{5,1},{7,3},{8,12},{10,14},{12... | collective-permute-start | bytes 294920 | tf_op jit(solution)/shard_map/ppermute | solution.py:419
  29.0 3.1 %collective-permute-done.13.refs_6_.refs_21_ = f32[96,256]{1,0:T(8,128)S(1)} collective-permute-done((f32[96,256]{1,0:T(8,128)S(1)}, f32[96,256]{1,0:T(8,128)S(1)}, u32[]{:S(2)}, u32[]{:S(2)}) %collective-permute-start.13) | collective-permute-done | bytes 98336 | tf_op jit(solution)/shard_map/ppermute | solution.py:419
  32.0 1.6 %collective-permute-done.12.refs_5_.refs_20_ = f32[96,256]{1,0:T(8,128)S(1)} collective-permute-done((f32[96,256]{1,0:T(8,128)S(1)}, f32[96,256]{1,0:T(8,128)S(1)}, u32[]{:S(2)}, u32[]{:S(2)}) %collective-permute-start.12) | collective-permute-done | bytes 98336 | tf_op jit(solution)/shard_map/ppermute | solution.py:419
  34.2 1.6 %collective-permute-start.21 = (f32[96,256]{1,0:T(8,128)S(1)}, f32[96,256]{1,0:T(8,128)S(1)}, u32[]{:S(2)}, u32[]{:S(2)}) collective-permute-start(f32[96,256]{1,0:T(8,128)S(1)} %get-tuple-element.40), channel_id=1, source_target_pairs={{0,6},{2,4},{4,2},{6,0},{1,7},{3,5},{5,3},{7,1},{8,14},{10,12},{12... | collective-permute-start | bytes 294920 | tf_op jit(solution)/shard_map/ppermute | solution.py:428
  35.7 1.5 %collective-permute-start.20 = (f32[96,256]{1,0:T(8,128)S(1)}, f32[96,256]{1,0:T(8,128)S(1)}, u32[]{:S(2)}, u32[]{:S(2)}) collective-permute-start(f32[96,256]{1,0:T(8,128)S(1)} %get-tuple-element.41), channel_id=1, source_target_pairs={{0,4},{2,6},{4,0},{6,2},{1,5},{3,7},{5,1},{7,3},{8,12},{10,14},{12... | collective-permute-start | bytes 294920 | tf_op jit(solution)/shard_map/ppermute | solution.py:428
  37.7 2.2 %shard_map.89 = (f32[96,256]{1,0:T(8,128)S(1)}, bf16[2,7,256,256]{3,2,1,0:T(8,128)(2,1)S(1)}) custom-call(f32[96,256]{1,0:T(8,128)S(1)} %get-tuple-element.25.refs_0_.refs_1_.refs_3_.refs_18_, f32[256,256]{1,0:T(8,128)} %bitcast.32, f32[7,256,256]{2,1,0:T(8,128)} %bitcast.29), custom_call_target="tpu_custom_call" | custom-call | flops 150994944 | bytes 2195456 | tf_op jit(solution)/shard_map/pallas_call | solution.py:131
  40.5 1.5 %collective-permute-done.20.refs_14_ = f32[96,256]{1,0:T(8,128)S(1)} collective-permute-done((f32[96,256]{1,0:T(8,128)S(1)}, f32[96,256]{1,0:T(8,128)S(1)}, u32[]{:S(2)}, u32[]{:S(2)}) %collective-permute-start.20) | collective-permute-done | bytes 98336 | tf_op jit(solution)/shard_map/ppermute | solution.py:428
  42.0 1.8 %shard_map.90 = (f32[96,256]{1,0:T(8,128)S(1)}, f32[3,96]{1,0:T(4,128)S(1)}) custom-call(s32[10]{0:T(128)S(1)} %compare_select_fusion.3.refs_0_, f32[96,256]{1,0:T(8,128)S(1)} %get-tuple-element.25.refs_0_.refs_1_.refs_3_.refs_18_, f32[96,256]{1,0:T(8,128)S(1)} %get-tuple-element.26.refs_2_, ...), custom_call_target="tpu_custom_call" | custom-call | flops 264241152 | bytes 3211264 | tf_op jit(solution)/shard_map/pallas_call | solution.py:131
  43.8 1.5 %collective-permute-start.24 = (f32[96,256]{1,0:T(8,128)S(1)}, f32[96,256]{1,0:T(8,128)}, u32[]{:S(2)}, u32[]{:S(2)}) collective-permute-start(f32[96,256]{1,0:T(8,128)S(1)} %get-tuple-element.31.refs_0_.refs_2_), channel_id=1, source_target_pairs={{0,6},{2,4},{4,2},{6,0},{1,7},{3,5},{5,3},{7,1},{8,14},{10,12},{12... | collective-permute-start | bytes 294920 | tf_op jit(solution)/shard_map/ppermute | solution.py:419
  47.4 2.8 %collective-permute-done.24.refs_5_ = f32[96,256]{1,0:T(8,128)} collective-permute-done((f32[96,256]{1,0:T(8,128)S(1)}, f32[96,256]{1,0:T(8,128)}, u32[]{:S(2)}, u32[]{:S(2)}) %collective-permute-start.24) | collective-permute-done | bytes 98336 | tf_op jit(solution)/shard_map/ppermute | solution.py:419
  50.2 1.5 %collective-permute-done.23.refs_4_ = f32[96,256]{1,0:T(8,128)} collective-permute-done((f32[96,256]{1,0:T(8,128)S(1)}, f32[96,256]{1,0:T(8,128)}, u32[]{:S(2)}, u32[]{:S(2)}) %collective-permute-start.23) | collective-permute-done | bytes 98336 | tf_op jit(solution)/shard_map/ppermute | solution.py:419
  52.8 5.1 %all-to-all-start = ((f32[32,3,96]{2,1,0:T(4,128)}), f32[32,3,96]{2,1,0:T(4,128)S(1)}, u32[]{:S(2)}, u32[]{:S(2)}) async-start(f32[32,3,96]{2,1,0:T(4,128)} %broadcast_in_dim.33), calls=%async_computation | async-start | bytes 131072 | tf_op jit(solution)/shard_map/all_to_all | solution.py:473
  57.9 2.5 %shard_map.91 = (f32[96,256]{1,0:T(8,128)}, bf16[2,7,256,256]{3,2,1,0:T(8,128)(2,1)S(1)}) custom-call(f32[96,256]{1,0:T(8,128)S(1)} %get-tuple-element.31.refs_0_.refs_2_, f32[256,256]{1,0:T(8,128)} %bitcast.33, f32[7,256,256]{2,1,0:T(8,128)} %bitcast.30), custom_call_target="tpu_custom_call" | custom-call | flops 150994944 | bytes 2195456 | tf_op jit(solution)/shard_map/pallas_call | solution.py:131
  60.4 4.9 %all-to-all-done.refs_1_ = f32[32,3,96]{2,1,0:T(4,128)S(1)} async-done(((f32[32,3,96]{2,1,0:T(4,128)}), f32[32,3,96]{2,1,0:T(4,128)S(1)}, u32[]{:S(2)}, u32[]{:S(2)}) %all-to-all-start) | async-done | bytes 36896 | tf_op jit(solution)/shard_map/all_to_all | solution.py:473
  65.3 8.5 %shard_map.92 = (f32[96,256]{1,0:T(8,128)S(1)}, f32[96,256]{1,0:T(8,128)S(1)}, f32[1,96]{1,0:T(1,128)S(1)}, f32[16,16,128]{2,1,0:T(8,128)S(1)}, f32[16,16,128]{2,1,0:T(8,128)S(1)}) custom-call(s32[10]{0:T(128)S(1)} %compare_select_fusion.3.refs_0_, f32[32,3,96]{2,1,0:T(4,128)S(1)} %all-to-all-done.refs_1_, f32[96,256]{1,0:T(8,128)S(1)} %get-tuple-element.31.refs_0_.refs_2_, ...), custom_call_target="tpu_custom_call" | custom-call | flops 1056964608 | bytes 6590464 | tf_op jit(solution)/shard_map/pallas_call | solution.py:131
  75.3 10.6 %all_to_all.10.refs_1_ = f32[16,16,128]{2,1,0:T(8,128)S(1)} all-to-all(f32[16,16,128]{2,1,0:T(8,128)S(1)} %add.75), channel_id=1, replica_groups=mesh['row'=4,'chip'=4,'core'=2] {'row','chip'}, dimensions={0} | all-to-all | bytes 262144 | tf_op jit(solution)/shard_map/all_to_all | solution.py:505
  (57 shorter events, 13.8 us)
Async XLA Ops:
  4.3 10.3 %collective-permute-start.7 = (f32[4,96,256]{2,1,0:T(8,128)S(1)}, f32[4,96,256]{2,1,0:T(8,128)S(1)}, u32[]{:S(2)}, u32[]{:S(2)}) collective-permute-start(f32[4,96,256]{2,1,0:T(8,128)S(1)} %get-tuple-element.24), channel_id=1, source_target_pairs={{0,1},{1,0},{2,3},{3,2},{4,5},{5,4},{6,7},{7,6},{8,9},{9,8},{10,11... | collective-permute-start | bytes 1179656 | tf_op jit(solution)/shard_map/ppermute | solution.py:426
  4.8 7.2 %collective-permute-start.2 = (f32[96,256]{1,0:T(8,128)}, f32[96,256]{1,0:T(8,128)S(1)}, u32[]{:S(2)}, u32[]{:S(2)}) collective-permute-start(f32[96,256]{1,0:T(8,128)} %bitcast.1.refs_0_.refs_1_.refs_3_.refs_10_), channel_id=1, source_target_pairs={{0,6},{2,4},{4,2},{6,0},{1,7},{3,5},{5,3},{7,1},{8,14},{10,12},{12... | collective-permute-start | bytes 294920 | tf_op jit(solution)/shard_map/ppermute | solution.py:419
  8.4 5.7 %collective-permute-start.1 = (f32[96,256]{1,0:T(8,128)}, f32[96,256]{1,0:T(8,128)S(1)}, u32[]{:S(2)}, u32[]{:S(2)}) collective-permute-start(f32[96,256]{1,0:T(8,128)} %bitcast.1.refs_0_.refs_1_.refs_3_.refs_10_), channel_id=1, source_target_pairs={{0,4},{2,6},{4,0},{6,2},{1,5},{3,7},{5,1},{7,3},{8,12},{10,14},{12... | collective-permute-start | bytes 294920 | tf_op jit(solution)/shard_map/ppermute | solution.py:419
  9.0 7.5 %collective-permute-start.3 = (f32[96,256]{1,0:T(8,128)}, f32[96,256]{1,0:T(8,128)S(1)}, u32[]{:S(2)}, u32[]{:S(2)}) collective-permute-start(f32[96,256]{1,0:T(8,128)} %bitcast.1.refs_0_.refs_1_.refs_3_.refs_10_), channel_id=1, source_target_pairs={{0,1},{1,0},{2,3},{3,2},{4,5},{5,4},{6,7},{7,6},{8,9},{9,8},{10,11... | collective-permute-start | bytes 294920 | tf_op jit(solution)/shard_map/ppermute | solution.py:423
  12.0 5.8 %collective-permute-start.6 = (f32[96,256]{1,0:T(8,128)S(1)}, f32[96,256]{1,0:T(8,128)S(1)}, u32[]{:S(2)}, u32[]{:S(2)}) collective-permute-start(f32[96,256]{1,0:T(8,128)S(1)} %collective-permute-done.2.refs_6_.refs_13_), channel_id=1, source_target_pairs={{0,1},{1,0},{2,3},{3,2},{4,5},{5,4},{6,7},{7,6},{8,9},{9,8},{10,11... | collective-permute-start | bytes 294920 | tf_op jit(solution)/shard_map/ppermute | solution.py:423
  14.1 7.3 %collective-permute-start.5 = (f32[96,256]{1,0:T(8,128)S(1)}, f32[96,256]{1,0:T(8,128)S(1)}, u32[]{:S(2)}, u32[]{:S(2)}) collective-permute-start(f32[96,256]{1,0:T(8,128)S(1)} %collective-permute-done.1.refs_5_.refs_12_), channel_id=1, source_target_pairs={{0,1},{1,0},{2,3},{3,2},{4,5},{5,4},{6,7},{7,6},{8,9},{9,8},{10,11... | collective-permute-start | bytes 294920 | tf_op jit(solution)/shard_map/ppermute | solution.py:423
  14.3 7.1 %collective-permute-start.4 = (f32[96,256]{1,0:T(8,128)S(1)}, f32[96,256]{1,0:T(8,128)S(1)}, u32[]{:S(2)}, u32[]{:S(2)}) collective-permute-start(f32[96,256]{1,0:T(8,128)S(1)} %collective-permute-done.refs_4_.refs_11_), channel_id=1, source_target_pairs={{0,1},{1,0},{2,3},{3,2},{4,5},{5,4},{6,7},{7,6},{8,9},{9,8},{10,11... | collective-permute-start | bytes 294920 | tf_op jit(solution)/shard_map/ppermute | solution.py:423
  14.6 6.8 %collective-permute-start.10 = (f32[96,256]{1,0:T(8,128)S(1)}, f32[96,256]{1,0:T(8,128)S(1)}, u32[]{:S(2)}, u32[]{:S(2)}) collective-permute-start(f32[96,256]{1,0:T(8,128)S(1)} %get-tuple-element.44), channel_id=1, source_target_pairs={{0,6},{2,4},{4,2},{6,0},{1,7},{3,5},{5,3},{7,1},{8,14},{10,12},{12... | collective-permute-start | bytes 294920 | tf_op jit(solution)/shard_map/ppermute | solution.py:428
  16.4 6.2 %collective-permute-start.9 = (f32[96,256]{1,0:T(8,128)S(1)}, f32[96,256]{1,0:T(8,128)S(1)}, u32[]{:S(2)}, u32[]{:S(2)}) collective-permute-start(f32[96,256]{1,0:T(8,128)S(1)} %get-tuple-element.45), channel_id=1, source_target_pairs={{0,4},{2,6},{4,0},{6,2},{1,5},{3,7},{5,1},{7,3},{8,12},{10,14},{12... | collective-permute-start | bytes 294920 | tf_op jit(solution)/shard_map/ppermute | solution.py:428
  25.3 8.8 %collective-permute-start.18 = (f32[4,96,256]{2,1,0:T(8,128)S(1)}, f32[4,96,256]{2,1,0:T(8,128)S(1)}, u32[]{:S(2)}, u32[]{:S(2)}) collective-permute-start(f32[4,96,256]{2,1,0:T(8,128)S(1)} %get-tuple-element.29), channel_id=1, source_target_pairs={{0,1},{1,0},{2,3},{3,2},{4,5},{5,4},{6,7},{7,6},{8,9},{9,8},{10,11... | collective-permute-start | bytes 1179656 | tf_op jit(solution)/shard_map/ppermute | solution.py:426
  25.4 6.6 %collective-permute-start.13 = (f32[96,256]{1,0:T(8,128)S(1)}, f32[96,256]{1,0:T(8,128)S(1)}, u32[]{:S(2)}, u32[]{:S(2)}) collective-permute-start(f32[96,256]{1,0:T(8,128)S(1)} %get-tuple-element.25.refs_0_.refs_1_.refs_3_.refs_18_), channel_id=1, source_target_pairs={{0,6},{2,4},{4,2},{6,0},{1,7},{3,5},{5,3},{7,1},{8,14},{10,12},{12... | collective-permute-start | bytes 294920 | tf_op jit(solution)/shard_map/ppermute | solution.py:419
  27.0 6.6 %collective-permute-start.12 = (f32[96,256]{1,0:T(8,128)S(1)}, f32[96,256]{1,0:T(8,128)S(1)}, u32[]{:S(2)}, u32[]{:S(2)}) collective-permute-start(f32[96,256]{1,0:T(8,128)S(1)} %get-tuple-element.25.refs_0_.refs_1_.refs_3_.refs_18_), channel_id=1, source_target_pairs={{0,4},{2,6},{4,0},{6,2},{1,5},{3,7},{5,1},{7,3},{8,12},{10,14},{12... | collective-permute-start | bytes 294920 | tf_op jit(solution)/shard_map/ppermute | solution.py:419
  29.0 6.8 %collective-permute-start.14 = (f32[96,256]{1,0:T(8,128)S(1)}, f32[96,256]{1,0:T(8,128)S(1)}, u32[]{:S(2)}, u32[]{:S(2)}) collective-permute-start(f32[96,256]{1,0:T(8,128)S(1)} %get-tuple-element.25.refs_0_.refs_1_.refs_3_.refs_18_), channel_id=1, source_target_pairs={{0,1},{1,0},{2,3},{3,2},{4,5},{5,4},{6,7},{7,6},{8,9},{9,8},{10,11... | collective-permute-start | bytes 294920 | tf_op jit(solution)/shard_map/ppermute | solution.py:423
  33.6 6.3 %collective-permute-start.16 = (f32[96,256]{1,0:T(8,128)S(1)}, f32[96,256]{1,0:T(8,128)S(1)}, u32[]{:S(2)}, u32[]{:S(2)}) collective-permute-start(f32[96,256]{1,0:T(8,128)S(1)} %collective-permute-done.12.refs_5_.refs_20_), channel_id=1, source_target_pairs={{0,1},{1,0},{2,3},{3,2},{4,5},{5,4},{6,7},{7,6},{8,9},{9,8},{10,11... | collective-permute-start | bytes 294920 | tf_op jit(solution)/shard_map/ppermute | solution.py:423
  33.6 6.3 %collective-permute-start.15 = (f32[96,256]{1,0:T(8,128)S(1)}, f32[96,256]{1,0:T(8,128)S(1)}, u32[]{:S(2)}, u32[]{:S(2)}) collective-permute-start(f32[96,256]{1,0:T(8,128)S(1)} %collective-permute-done.11.refs_4_.refs_19_), channel_id=1, source_target_pairs={{0,1},{1,0},{2,3},{3,2},{4,5},{5,4},{6,7},{7,6},{8,9},{9,8},{10,11... | collective-permute-start | bytes 294920 | tf_op jit(solution)/shard_map/ppermute | solution.py:423
  34.2 6.3 %collective-permute-start.21 = (f32[96,256]{1,0:T(8,128)S(1)}, f32[96,256]{1,0:T(8,128)S(1)}, u32[]{:S(2)}, u32[]{:S(2)}) collective-permute-start(f32[96,256]{1,0:T(8,128)S(1)} %get-tuple-element.40), channel_id=1, source_target_pairs={{0,6},{2,4},{4,2},{6,0},{1,7},{3,5},{5,3},{7,1},{8,14},{10,12},{12... | collective-permute-start | bytes 294920 | tf_op jit(solution)/shard_map/ppermute | solution.py:428
  35.7 6.2 %collective-permute-start.20 = (f32[96,256]{1,0:T(8,128)S(1)}, f32[96,256]{1,0:T(8,128)S(1)}, u32[]{:S(2)}, u32[]{:S(2)}) collective-permute-start(f32[96,256]{1,0:T(8,128)S(1)} %get-tuple-element.41), channel_id=1, source_target_pairs={{0,4},{2,6},{4,0},{6,2},{1,5},{3,7},{5,1},{7,3},{8,12},{10,14},{12... | collective-permute-start | bytes 294920 | tf_op jit(solution)/shard_map/ppermute | solution.py:428
  43.8 6.4 %collective-permute-start.24 = (f32[96,256]{1,0:T(8,128)S(1)}, f32[96,256]{1,0:T(8,128)}, u32[]{:S(2)}, u32[]{:S(2)}) collective-permute-start(f32[96,256]{1,0:T(8,128)S(1)} %get-tuple-element.31.refs_0_.refs_2_), channel_id=1, source_target_pairs={{0,6},{2,4},{4,2},{6,0},{1,7},{3,5},{5,3},{7,1},{8,14},{10,12},{12... | collective-permute-start | bytes 294920 | tf_op jit(solution)/shard_map/ppermute | solution.py:419
  45.4 6.3 %collective-permute-start.23 = (f32[96,256]{1,0:T(8,128)S(1)}, f32[96,256]{1,0:T(8,128)}, u32[]{:S(2)}, u32[]{:S(2)}) collective-permute-start(f32[96,256]{1,0:T(8,128)S(1)} %get-tuple-element.31.refs_0_.refs_2_), channel_id=1, source_target_pairs={{0,4},{2,6},{4,0},{6,2},{1,5},{3,7},{5,1},{7,3},{8,12},{10,14},{12... | collective-permute-start | bytes 294920 | tf_op jit(solution)/shard_map/ppermute | solution.py:419
  47.4 18.0 %collective-permute-start.25 = (f32[96,256]{1,0:T(8,128)S(1)}, f32[96,256]{1,0:T(8,128)}, u32[]{:S(2)}, u32[]{:S(2)}) collective-permute-start(f32[96,256]{1,0:T(8,128)S(1)} %get-tuple-element.31.refs_0_.refs_2_), channel_id=1, source_target_pairs={{0,1},{1,0},{2,3},{3,2},{4,5},{5,4},{6,7},{7,6},{8,9},{9,8},{10,11... | collective-permute-start | bytes 294920 | tf_op jit(solution)/shard_map/ppermute | solution.py:423
  50.2 15.1 %collective-permute-start.28 = (f32[96,256]{1,0:T(8,128)}, f32[96,256]{1,0:T(8,128)}, u32[]{:S(2)}, u32[]{:S(2)}) collective-permute-start(f32[96,256]{1,0:T(8,128)} %collective-permute-done.24.refs_5_), channel_id=1, source_target_pairs={{0,1},{1,0},{2,3},{3,2},{4,5},{5,4},{6,7},{7,6},{8,9},{9,8},{10,11... | collective-permute-start | bytes 294920 | tf_op jit(solution)/shard_map/ppermute | solution.py:423
  51.7 13.6 %collective-permute-start.27 = (f32[96,256]{1,0:T(8,128)}, f32[96,256]{1,0:T(8,128)}, u32[]{:S(2)}, u32[]{:S(2)}) collective-permute-start(f32[96,256]{1,0:T(8,128)} %collective-permute-done.23.refs_4_), channel_id=1, source_target_pairs={{0,1},{1,0},{2,3},{3,2},{4,5},{5,4},{6,7},{7,6},{8,9},{9,8},{10,11... | collective-permute-start | bytes 294920 | tf_op jit(solution)/shard_map/ppermute | solution.py:423
  51.7 13.6 %collective-permute-start.26 = (f32[96,256]{1,0:T(8,128)}, f32[96,256]{1,0:T(8,128)}, u32[]{:S(2)}, u32[]{:S(2)}) collective-permute-start(f32[96,256]{1,0:T(8,128)} %collective-permute-done.22.refs_3_), channel_id=1, source_target_pairs={{0,1},{1,0},{2,3},{3,2},{4,5},{5,4},{6,7},{7,6},{8,9},{9,8},{10,11... | collective-permute-start | bytes 294920 | tf_op jit(solution)/shard_map/ppermute | solution.py:423
  52.8 12.5 %all-to-all-start = ((f32[32,3,96]{2,1,0:T(4,128)}), f32[32,3,96]{2,1,0:T(4,128)S(1)}, u32[]{:S(2)}, u32[]{:S(2)}) async-start(f32[32,3,96]{2,1,0:T(4,128)} %broadcast_in_dim.33), calls=%async_computation | async-start | bytes 131072 | tf_op jit(solution)/shard_map/all_to_all | solution.py:473
  (8 other events, 49.3 us)
where the time goes:
time: 87.8 us; the launch traced here: 87.4 us
  starting transfers between devices  25.5 us (29%)
  Pallas kernels  25.1 us (29%)
  waiting for transfers between devices  23.8 us (27%)
  blocking collectives  10.6 us (12%)
    pallas_call x8, Pallas kernels, call(): pl.pallas_call(kernel, out_shape=outs, in_specs=specs, out_specs=[vmem] *...  25.1 us
    ppermute x9, waiting for transfers between devices, gather(): same[way.source(k)] = lax.ppermute(value, 'chip', way.pairs(k))  14.3 us
    ppermute x9, starting transfers between devices, gather(): same[way.source(k)] = lax.ppermute(value, 'chip', way.pairs(k))  11.2 us
    all_to_all x1, blocking collectives, on_device(): lax.all_to_all(keep + received, ('row', 'chip'), 0, 0, tiled=True)  10.6 us
    ppermute x6, starting transfers between devices, scatter(): lax.ppermute(sums[k], 'chip', way.pairs(k))  7.11 us
    all_to_all x1, starting transfers between devices, on_device(): lax.all_to_all(jnp.broadcast_to(sums[None], (devices,) + sums.shape), ALL...  5.07 us
    all_to_all x1, waiting for transfers between devices, on_device(): lax.all_to_all(jnp.broadcast_to(sums[None], (devices,) + sums.shape), ALL...  4.87 us
    ppermute x6, waiting for transfers between devices, scatter(): lax.ppermute(sums[k], 'chip', way.pairs(k))  3.35 us
  transfers between devices with their start and end apart: 31, of which 12 were waited for; matrix products, arithmetic and copies ran while one was open for 1% of the time, Pallas kernels for 9%

commit v1 on v0

--- a/solution.py
+++ b/solution.py
@@ -52,37 +52,29 @@
 
 
 class Far:
-    def __init__(self, array, anywhere=False):
-        self.stacked = isinstance(array, (tuple, list))
-        self.arrays = list(array) if self.stacked else [array]
-        if not anywhere:
-            self.arrays = [
-                pltpu.with_memory_space_constraint(a, pltpu.HBM) for a in self.arrays
-            ]
-        first = self.arrays[0]
-        self.shape = (len(self.arrays),) * self.stacked + first.shape
-        self.pieces = self.shape[0] if len(self.shape) == 3 else 1
-        self.dtype = first.dtype
-
-    def copies(self, refs, buffer, sems):
-        for k in range(self.pieces):
-            if self.stacked:
-                source, target = refs[k], buffer.at[k]
-            elif len(self.shape) == 3:
-                source, target = refs[0].at[k], buffer.at[k]
-            else:
-                source, target = refs[0], buffer
-            yield pltpu.make_async_copy(source, target, sems.at[k])
+    def __init__(self, array, space=pltpu.VMEM):
+        self.arrays = [pltpu.with_memory_space_constraint(array, pltpu.HBM)]
+        self.pieces = array.shape[0] if array.ndim == 3 else 1
+        self.buffer = space(array.shape, array.dtype)
+
+    def copies(self, ref, buffer, sems):
+        if self.pieces == 1:
+            return [pltpu.make_async_copy(ref, buffer, sems.at[0])]
+        return [
+            pltpu.make_async_copy(ref.at[k], buffer.at[k], sems.at[k])
+            for k in range(self.pieces)
+        ]
 
 
 class Fetched:
     def __init__(self, copies, ref):
-        self.copies, self.ref, self.shape = copies, ref, ref.shape
-
-    def wait(self):
-        for copy in self.copies:
-            copy.wait()
-        self.copies = []
+        self.copies, self.ref, self.shape, self.done = copies, ref, ref.shape, 0
+
+    def wait(self, upto=None):
+        upto = len(self.copies) if upto is None else upto
+        for k in range(self.done, upto):
+            self.copies[k].wait()
+        self.done = max(self.done, upto)
         return self.ref
 
     def all(self):
@@ -113,9 +105,7 @@
         seen, at = [], 0
         for one, first, length in plan:
             if isinstance(one, Far):
-                copies = list(
-                    one.copies(arrays[first : first + length], buffers[at], sems[at])
-                )
+                copies = one.copies(arrays[first], buffers[at], sems[at])
                 for copy in copies:
                     copy.start()
                 seen.append(Fetched(copies, buffers[at]))
@@ -134,7 +124,7 @@
         in_specs=specs,
         out_specs=[vmem] * len(outs),
         scratch_shapes=[pltpu.VMEM(o.shape, o.dtype) for o in scratch]
-        + [pltpu.VMEM(one.shape, one.dtype) for one in fars]
+        + [one.buffer for one in fars]
         + [pltpu.SemaphoreType.DMA((one.pieces,)) for one in fars],
         cost_estimate=pl.CostEstimate(
             flops=flops,
@@ -161,22 +151,23 @@
         return k if self.power else (self.chips - k) % self.chips
 
 
-def seats(way, meta, count):
-    chip, core = meta[count], meta[count + 1]
+def seats(way, cols):
+    chip, core = lax.axis_index("chip"), lax.axis_index("core")
+    first = lax.axis_index("row") * (2 * way.chips)
     found = []
-    for k in range(count):
-        slot = jnp.maximum(meta[k], 0)
-        kind = jnp.where(slot % 2 == core, 0, way.chips)
+    for k in range(cols.shape[0]):
+        slot = jnp.maximum(cols[k] - first, 0)
+        kind = jnp.where(lax.rem(slot, 2) == core, 0, way.chips)
         found.append(
-            jnp.where(meta[k] >= 0, kind + way.to(chip, slot // 2), 2 * way.chips)
+            jnp.where(cols[k] >= 0, kind + way.to(chip, slot // 2), 2 * way.chips)
         )
     return found
 
 
-def contributions(way, meta, pairs, panel, work, keep, send):
+def contributions(way, cols, pairs, panel, work, keep, send):
     chips = way.chips
     work[0 : 2 * chips] = jnp.zeros((2 * chips,) + work.shape[1:], F32)
-    for seat, pair in zip(seats(way, meta, len(pairs)), pairs):
+    for seat, pair in zip(seats(way, cols), pairs):
         work[seat] = dot3(panel, pair(), NN)
     keep[...] = work[0:chips]
     send[...] = work[chips : 2 * chips]
@@ -191,10 +182,10 @@
     held[len(gathered)] = jnp.zeros(held.shape[1:], BF16)
 
 
-def off_diagonal(way, meta, pairs, held):
+def off_diagonal(way, cols, pairs, held):
     rows = held.shape[1] // 2
     first = second = None
-    for seat, pair in zip(seats(way, meta, len(pairs)), pairs):
+    for seat, pair in zip(seats(way, cols), pairs):
         both, (high, low) = held[seat], pair()
         one = lax.dot_general(both, high, NT, preferred_element_type=F32)
         two = lax.dot_general(both[:rows], low, NT, preferred_element_type=F32)
@@ -211,60 +202,84 @@
 
 
 def fresh_pairs(tiles):
-    return [
-        functools.partial(lambda k: split(tiles.ref[k]), k)
-        for k in range(tiles.shape[0])
-    ]
-
-
-def first_kernel(way, meta, panel, tiles, keep, send, work):
-    tiles.wait()
-    contributions(way, meta, fresh_pairs(tiles), split(panel[...]), work, keep, send)
+    n = tiles.shape[0]
+    half = (n + 1) // 2
+
+    def pair(k):
+        if k in (0, half):
+            tiles.wait(half if k == 0 else n)
+        return split(tiles.ref[k])
+
+    return [functools.partial(pair, k) for k in range(n)]
+
+
+def first_kernel(way, cols, panel, tiles, keep, send, work):
+    cols = cols.wait()
+    contributions(way, cols, fresh_pairs(tiles), split(panel.all()), work, keep, send)
 
 
 def prepare_kernel(panel, diag, tiles, image, split_tiles):
-    image[...] = dot_full(panel[...], diag.all(), NT)
+    image[...] = dot_full(panel.all(), diag.all(), NT)
     tiles.wait()
     for k in range(tiles.shape[0]):
         split_tiles[0, k], split_tiles[1, k] = split(tiles.ref[k])
 
 
+def diag_kernel(panel, diag, image):
+    image[...] = dot_full(panel[...], diag.all(), NT)
+
+
 def residual_kernel(
-    way, meta, base, target, gathered, split_tiles, added, residual, keep, send, work, held
+    way, cols, base, target, gathered, split_tiles, added, residual, keep, send, work, held
 ):
     pairs = held_pairs(split_tiles)
     hold(gathered, held)
-    total = base[...] + off_diagonal(way, meta, pairs, held)
+    total = base[...] + off_diagonal(way, cols, pairs, held)
     for block in added:
         total = total + block[...]
     rows, size = residual.shape
-    unit = target[...] == lax.broadcasted_iota(jnp.int32, (rows, size), 1)
+    chips = way.chips
+    block = (lax.axis_index("row") * chips + lax.axis_index("chip")) * 2
+    block = block + lax.axis_index("core")
+    at = column_of((target[...] - block * size).astype(F32))
+    unit = at == lax.broadcasted_iota(jnp.int32, (rows, size), 1).astype(F32)
     value = unit.astype(F32) - total
     residual[...] = value
-    contributions(way, meta, pairs, split(value), work, keep, send)
-
-
-def image_kernel(way, meta, panel, base, gathered, split_tiles, added, image, sums, held):
+    contributions(way, cols, pairs, split(value), work, keep, send)
+
+
+def image_kernel(way, cols, panel, base, gathered, split_tiles, added, image, sums, held):
     hold(gathered, held)
-    total = base[...] + off_diagonal(way, meta, held_pairs(split_tiles), held)
+    total = base[...] + off_diagonal(way, cols, held_pairs(split_tiles), held)
     for block in added:
         total = total + block[...]
     image[...] = total
     value = panel[...]
-    sums[0:1] = row_sums(value * value)
-    sums[1:2] = row_sums(value * total)
-    sums[2:3] = row_sums(total * total)
+    found = jnp.concatenate(
+        [row_sums(value * value), row_sums(value * total), row_sums(total * total)], 0
+    )
+    sums[...] = jnp.broadcast_to(found[None], sums.shape)
+
+
+def steps(sums):
+    totals = sums[0]
+    for device in range(1, sums.shape[0]):
+        totals = totals + sums[device]
+    rr, rq, qq = totals[0:1], totals[1:2], totals[2:3]
+    step = rr / rq
+    norm = rr - 2.0 * step * rq + step * step * qq
+    return norm, column_of(step), 1.0 + column_of(norm / rr)
 
 
 def middle_kernel(
     way,
     parts_rows,
     parts_cols,
-    meta,
+    cols,
     sums,
-    images,
     starts,
     residuals,
+    images,
     split_tiles,
     diag,
     newton_diag,
@@ -275,28 +290,17 @@
     keep,
     send,
     held,
-    packed,
     order,
     blocks,
     pieces,
 ):
-    n = split_tiles.shape[1]
-    totals = sums[0]
-    for device in range(1, sums.shape[0]):
-        totals = totals + sums[device]
-    rr, rq, qq = totals[0:1], totals[1:2], totals[2:3]
-    step = rr / rq
-    norm = rr - 2.0 * step * rq + step * step * qq
-    norm_out[...] = norm
-    step_col = column_of(step)
-    grow = 1.0 + column_of(norm / rr)
-    count, _ = x_out.shape
-    starts.wait()
-    residuals.wait()
+    n = newton_tiles.shape[0]
+    norm_out[...], step, grow = steps(sums)
+    count = d_out.shape[0]
     for k, image in enumerate(images):
-        r = residuals.ref[k]
-        x = starts.ref[k] + step_col * r
-        d = grow * r - step_col * image[...]
+        r = residuals[k][...]
+        x = starts[k][...] + step * r
+        d = grow * r - step * image[...]
         if k == 0:
             x_out[...] = x
             d_out[...] = d
@@ -304,7 +308,7 @@
         held[k, count : 2 * count], held[k, 2 * count : 3 * count] = split(d)
     held[len(images)] = jnp.zeros(held.shape[1:], BF16)
     x1, d1 = x_out[...], d_out[...]
-    found = seats(way, meta, n)
+    found = seats(way, cols)
 
     def product(rows, tile):
         return lax.dot_general(rows, tile, NT, preferred_element_type=F32)
@@ -322,10 +326,8 @@
     high, low = split(newton_diag.all() * 0.5)
     first = product(own, high)
     second = product(own[: 2 * count], low)
-    newton_tiles.wait()
-    for k in range(n):
-        block = held[found[k]]
-        high, low = split(newton_tiles.ref[k])
+    for seat, pair in zip(found, fresh_pairs(newton_tiles)):
+        block, (high, low) = held[seat], pair()
         first += product(block, high)
         second += product(block[: 2 * count], low)
     ux = first[:count] + (first[3 * count :] + second[:count])
@@ -333,29 +335,42 @@
     hr, hc = count // parts_rows, count // parts_cols
     for r_index in range(parts_rows):
         for kind, pair in enumerate(((x1, ux), (d1, ud))):
-            at = (2 * r_index + kind) * hr
+            at = r_index * HALF + kind * hr
             for side in range(2):
                 order[side, at : at + hr] = pair[side][
                     r_index * hr : (r_index + 1) * hr
                 ]
+        at = r_index * HALF + 2 * hr
+        order[:, at : (r_index + 1) * HALF] = jnp.zeros(
+            (2, HALF - 2 * hr, x1.shape[1]), F32
+        )
     blocks[...] = dot_full(
         jnp.concatenate([x1, d1], axis=0), order[1], NT
     ) + dot_full(jnp.concatenate([ux, ud], axis=0), order[0], NT)
-    core = meta[n + 1]
+    depth = keep.shape[1]
+    left = lax.broadcasted_iota(jnp.int32, (count, LANES), 1) < HALF
+    wide = jnp.concatenate([curvature, jnp.zeros((1, LANES - count), F32)], axis=1)
+    spot = lax.broadcasted_iota(jnp.int32, (depth, LANES), 0) == hc
+    first_core = lax.axis_index("core") == 0
     for r_index in range(parts_rows):
-        lanes = slice(2 * r_index * hr, 2 * (r_index + 1) * hr)
-        pieces[:, 0 : 2 * hr] = blocks[0:count, lanes]
-        pieces[:, HALF : HALF + 2 * hr] = blocks[count : 2 * count, lanes]
-        for c_index in range(parts_cols):
-            at = r_index * (parts_cols // 2) + c_index // 2
-            target = packed.at[c_index % 2, at]
-            target[0:hc] = pieces[c_index * hc : (c_index + 1) * hc]
-            target[hc : hc + 1, 0:count] = curvature
-    keep[...] = packed[core]
-    send[...] = packed[1 - core]
-
-
-def last_kernel(parts_rows, parts_cols, n, meta, received, norm, x1, d1, x_out, hessian):
+        lanes = slice(r_index // 2 * LANES, (r_index // 2 + 1) * LANES)
+        top, bottom = blocks[0:count, lanes], blocks[count : 2 * count, lanes]
+        if r_index % 2:
+            top = pltpu.roll(top, HALF, 1)
+        else:
+            bottom = pltpu.roll(bottom, HALF, 1)
+        pieces[r_index, 0:count] = jnp.where(left, top, bottom)
+        for pair in range(parts_cols // 2):
+            one, two = (
+                jnp.where(spot, wide, pieces[r_index, c * hc : c * hc + depth])
+                for c in (2 * pair, 2 * pair + 1)
+            )
+            at = r_index * (parts_cols // 2) + pair
+            keep[at] = jnp.where(first_core, one, two)
+            send[at] = jnp.where(first_core, two, one)
+
+
+def last_kernel(parts_rows, parts_cols, received, norm, x1, d1, x_out, hessian):
     total = received[0]
     for device in range(1, received.shape[0]):
         total = total + received[device]
@@ -364,7 +379,8 @@
     step = norm[...] / total[hc : hc + 1, 0:count]
     step_col = column_of(step)
     x_out[...] = x1[...] + step_col * d1[...]
-    row_at, col_at = meta[n + 2] * hr, (meta[n] * 2 + meta[n + 1]) * hc
+    row_at = lax.axis_index("row") * hr
+    col_at = (lax.axis_index("chip") * 2 + lax.axis_index("core")) * hc
     wanted = lax.broadcasted_iota(jnp.int32, (count, hr), 0) == row_at + (
         lax.broadcasted_iota(jnp.int32, (count, hr), 1)
     )
@@ -392,16 +408,10 @@
     groups = lax.axis_size("row")
     chips = lax.axis_size("chip")
     columns = chips * 2
-    devices = groups * columns
-    row, chip, core = (lax.axis_index(a).astype(jnp.int32) for a in ALL)
-    block = row * columns + chip * 2 + core
     count, size = warm_start.shape[1:]
     n = precision_pairs.shape[1]
-    spot = jnp.arange(n + 3, dtype=jnp.int32)
-    slots = jnp.where(pattern_cols >= 0, pattern_cols - row * columns, -1)[0]
-    meta = jnp.where(spot == n, chip, jnp.where(spot == n + 1, core, row))
-    meta = jnp.where(spot < n, jnp.pad(slots, (0, 3)), meta)
-    target = (target_rows - block * size).astype(jnp.int32)[:, None]
+    cols = pattern_cols[0]
+    target = target_rows[None]
     tiles, diag = precision_pairs[0], precision_diag[0]
     ntiles, ndiag = newton_pairs[0], newton_diag[0]
     panel = (count, size)
@@ -427,32 +437,29 @@
         sums = [keep[k] + received[k] for k in range(chips)]
         return [sums[0]] + [lax.ppermute(sums[k], "chip", way.pairs(k)) for k in range(1, chips)]
 
-    def prepare(value):
-        return call(
-            prepare_kernel,
-            [panel, parts],
-            [],
-            [value, Far(diag), Far(tiles)],
-            flops=4 * unit,
-        )
-
     start = warm_start[0]
     starts = gather(start)
     keep, send = call(
         functools.partial(first_kernel, way),
         [stack, stack],
-        [meta],
-        [start, Far(tiles)],
+        [],
+        [Far(cols, pltpu.SMEM), Far(start), Far(tiles)],
         scratch=[work],
         flops=n * unit,
     )
     added = scatter(keep, send)
     starts = forward(starts)
-    base, split_tiles = prepare(start)
+    base, split_tiles = call(
+        prepare_kernel,
+        [panel, parts],
+        [],
+        [Far(start), Far(diag), Far(tiles)],
+        flops=4 * unit,
+    )
     residual, keep, send = call(
         functools.partial(residual_kernel, way),
         [panel, stack, stack],
-        [meta],
+        [cols],
         [base, target, starts, split_tiles, added],
         scratch=[work, held],
         flops=2 * n * unit,
@@ -460,33 +467,32 @@
     residuals = gather(residual)
     added = scatter(keep, send)
     residuals = forward(residuals)
-    base, split_tiles = prepare(residual)
+    (base,) = call(
+        diag_kernel, [panel], [], [residual, Far(diag)], flops=2 * unit
+    )
     image, sums = call(
         functools.partial(image_kernel, way),
-        [panel, (3, count)],
-        [meta],
+        [panel, (groups * columns, 3, count)],
+        [cols],
         [residual, base, residuals, split_tiles, added],
         scratch=[held],
         flops=n * unit,
     )
     images = gather(image)
-    all_sums = lax.all_to_all(
-        jnp.broadcast_to(sums[None], (devices,) + sums.shape), ALL, 0, 0, tiled=True
-    )
+    sums = lax.all_to_all(sums, ALL, 0, 0, tiled=True)
     images = forward(images)
-    _, split_tiles = prepare(image)
     hr, hc = count // groups, count // columns
     depth = -(-(hc + 1) // 8) * 8
-    share = (devices // 2, depth, LANES)
+    share = (groups * chips, depth, LANES)
     x1, d1, norm, keep, send = call(
         functools.partial(middle_kernel, way, groups, columns),
         [panel, panel, (1, count), share, share],
-        [meta],
+        [cols],
         [
-            all_sums,
+            sums,
+            starts,
+            residuals,
             images,
-            Far(starts, anywhere=True),
-            Far(residuals, anywhere=True),
             split_tiles,
             Far(diag),
             Far(ndiag),
@@ -494,19 +500,18 @@
         ],
         scratch=[
             jax.ShapeDtypeStruct((2 * chips + 1, 4 * count, size), BF16),
-            (2,) + share,
-            (2, 2 * count, size),
-            (2 * count, 2 * count),
-            (count, LANES),
+            (2, groups * HALF, size),
+            (2 * count, groups * HALF),
+            (groups, count + depth, LANES),
         ],
         flops=4 * n * unit,
     )
     received = lax.ppermute(send, "core", swap)
     received = lax.all_to_all(keep + received, ("row", "chip"), 0, 0, tiled=True)
     solved, hessian = call(
-        functools.partial(last_kernel, groups, columns, n),
+        functools.partial(last_kernel, groups, columns),
         [panel, (hc, hr)],
-        [meta],
+        [],
         [received, norm, x1, d1],
         flops=unit // 100,
     )

time: 87.8 us -> 81.8 us (0.932)
  blocking collectives: 10.6 us -> 22.9 us
  Pallas kernels: 25.1 us -> 16.8 us
  starting transfers between devices: 25.5 us -> 20.5 us
  waiting for transfers between devices: 23.8 us -> 20.4 us
    all_to_all x0 -> x1, blocking collectives: none -> 12.3 us  [on_device(): sums = lax.all_to_all(sums, ALL, 0, 0, tiled=True)]
    pallas_call x8 -> x7, Pallas kernels: 25.1 us -> 16.8 us  [call(): pl.pallas_call(kernel, out_shape=outs, in_specs=specs, out_specs=[vmem] *...]
    all_to_all x1 -> x0, starting transfers between devices: 5.07 us -> none  [on_device(): lax.all_to_all(jnp.broadcast_to(sums[None], (devices,) + sums.shape), ALL...]
    all_to_all x1 -> x0, waiting for transfers between devices: 4.87 us -> none  [on_device(): lax.all_to_all(jnp.broadcast_to(sums[None], (devices,) + sums.shape), ALL...]
    ppermute x6, waiting for transfers between devices: 3.35 us -> 5.15 us  [scatter(): lax.ppermute(sums[k], 'chip', way.pairs(k))]
  transfers between devices with their start and end apart: 31 -> 30, of which waited for: 12 -> 12; matrix products, arithmetic and copies ran while one was open for 1% -> 0% of each run, Pallas kernels for 9% -> 4%
where the time goes in v1:
time: 81.8 us; the launch traced here: 81.5 us
  blocking collectives  22.9 us (28%)
  starting transfers between devices  20.5 us (25%)
  waiting for transfers between devices  20.4 us (25%)
  Pallas kernels  16.8 us (21%)
    pallas_call x7, Pallas kernels, call(): pl.pallas_call(kernel, out_shape=outs, in_specs=specs, out_specs=[vmem] *...  16.8 us
    ppermute x9, waiting for transfers between devices, gather(): same[way.source(k)] = lax.ppermute(value, 'chip', way.pairs(k))  13.9 us
    all_to_all x1, blocking collectives, on_device(): sums = lax.all_to_all(sums, ALL, 0, 0, tiled=True)  12.3 us
    ppermute x9, starting transfers between devices, gather(): same[way.source(k)] = lax.ppermute(value, 'chip', way.pairs(k))  11.3 us
    all_to_all x1, blocking collectives, on_device(): lax.all_to_all(keep + received, ('row', 'chip'), 0, 0, tiled=True)  10.6 us
    ppermute x6, starting transfers between devices, scatter(): lax.ppermute(sums[k], 'chip', way.pairs(k))  7.11 us
    ppermute x6, waiting for transfers between devices, scatter(): lax.ppermute(sums[k], 'chip', way.pairs(k))  5.15 us
  transfers between devices with their start and end apart: 30, of which 12 were waited for; matrix products, arithmetic and copies ran while one was open for 0% of the time, Pallas kernels for 4%

profile of v1, /device:TPU:0, one launch (start us, length us, event | category | flops | bytes accessed | tf_op | source)
XLA Modules:
  0.0 81.5 jit_solution(13605664857443227799)
XLA Ops:
  0.6 2.3 %shard_map.87 = (f32[4,96,256]{2,1,0:T(8,128)S(1)}, f32[4,96,256]{2,1,0:T(8,128)S(1)}) custom-call(s32[7]{0:T(128)} %bitcast.33, f32[96,256]{1,0:T(8,128)} %bitcast.25, f32[7,256,256]{2,1,0:T(8,128)} %bitcast.38), custom_call_target="tpu_custom_call" | custom-call | flops 264241152 | bytes 1933340 | tf_op jit(solution)/shard_map/pallas_call | solution.py:121
  3.6 3.5 %collective-permute-start.2 = (f32[96,256]{1,0:T(8,128)S(1)}, f32[96,256]{1,0:T(8,128)S(1)}, u32[]{:S(2)}, u32[]{:S(2)}) collective-permute-start(f32[96,256]{1,0:T(8,128)S(1)} %bitcast.27), channel_id=1, source_target_pairs={{0,6},{2,4},{4,2},{6,0},{1,7},{3,5},{5,3},{7,1},{8,14},{10,12},{12... | collective-permute-start | bytes 294920 | tf_op jit(solution)/shard_map/ppermute | solution.py:429
  7.7 2.8 %collective-permute-done.2.refs_6_.refs_5_ = f32[96,256]{1,0:T(8,128)S(1)} collective-permute-done((f32[96,256]{1,0:T(8,128)S(1)}, f32[96,256]{1,0:T(8,128)S(1)}, u32[]{:S(2)}, u32[]{:S(2)}) %collective-permute-start.2) | collective-permute-done | bytes 98336 | tf_op jit(solution)/shard_map/ppermute | solution.py:429
  10.5 2.0 %collective-permute-done.1.refs_5_.refs_4_ = f32[96,256]{1,0:T(8,128)S(1)} collective-permute-done((f32[96,256]{1,0:T(8,128)S(1)}, f32[96,256]{1,0:T(8,128)S(1)}, u32[]{:S(2)}, u32[]{:S(2)}) %collective-permute-start.1) | collective-permute-done | bytes 98336 | tf_op jit(solution)/shard_map/ppermute | solution.py:429
  13.1 1.8 %collective-permute-start.10 = (f32[96,256]{1,0:T(8,128)S(1)}, f32[96,256]{1,0:T(8,128)S(1)}, u32[]{:S(2)}, u32[]{:S(2)}) collective-permute-start(f32[96,256]{1,0:T(8,128)S(1)} %get-tuple-element.38), channel_id=1, source_target_pairs={{0,6},{2,4},{4,2},{6,0},{1,7},{3,5},{5,3},{7,1},{8,14},{10,12},{12... | collective-permute-start | bytes 294920 | tf_op jit(solution)/shard_map/ppermute | solution.py:438
  14.9 1.4 %collective-permute-start.9 = (f32[96,256]{1,0:T(8,128)S(1)}, f32[96,256]{1,0:T(8,128)S(1)}, u32[]{:S(2)}, u32[]{:S(2)}) collective-permute-start(f32[96,256]{1,0:T(8,128)S(1)} %get-tuple-element.39), channel_id=1, source_target_pairs={{0,4},{2,6},{4,0},{6,2},{1,5},{3,7},{5,1},{7,3},{8,12},{10,14},{12... | collective-permute-start | bytes 294920 | tf_op jit(solution)/shard_map/ppermute | solution.py:438
  16.7 2.2 %shard_map.86 = (f32[96,256]{1,0:T(8,128)S(1)}, bf16[2,7,256,256]{3,2,1,0:T(8,128)(2,1)S(1)}) custom-call(f32[96,256]{1,0:T(8,128)} %bitcast.26, f32[256,256]{1,0:T(8,128)} %bitcast.40, f32[7,256,256]{2,1,0:T(8,128)} %bitcast.39), custom_call_target="tpu_custom_call" | custom-call | flops 150994944 | bytes 2195456 | tf_op jit(solution)/shard_map/pallas_call | solution.py:121
  19.6 1.5 %collective-permute-done.9.refs_14_ = f32[96,256]{1,0:T(8,128)S(1)} collective-permute-done((f32[96,256]{1,0:T(8,128)S(1)}, f32[96,256]{1,0:T(8,128)S(1)}, u32[]{:S(2)}, u32[]{:S(2)}) %collective-permute-start.9) | collective-permute-done | bytes 98336 | tf_op jit(solution)/shard_map/ppermute | solution.py:438
  21.2 2.3 %shard_map.88 = (f32[96,256]{1,0:T(8,128)S(1)}, f32[4,96,256]{2,1,0:T(8,128)S(1)}, f32[4,96,256]{2,1,0:T(8,128)S(1)}) custom-call(s32[7]{0:T(128)S(1)} %bitcast.34, f32[96,256]{1,0:T(8,128)S(1)} %get-tuple-element.18.refs_1_, s32[1,96]{1,0:T(1,128)S(1)} %bitcast.37, f32[96,256]{1,0:T(8,128)S(1)} %bitcast.31, ...), custom_call_target="tpu_custom_call" | custom-call | flops 528482304 | bytes 3113344 | tf_op jit(solution)/shard_map/pallas_call | solution.py:121
  23.6 1.6 %collective-permute-start.13 = (f32[96,256]{1,0:T(8,128)S(1)}, f32[96,256]{1,0:T(8,128)S(1)}, u32[]{:S(2)}, u32[]{:S(2)}) collective-permute-start(f32[96,256]{1,0:T(8,128)S(1)} %get-tuple-element.22.refs_0_.refs_1_.refs_3_.refs_10_), channel_id=1, source_target_pairs={{0,6},{2,4},{4,2},{6,0},{1,7},{3,5},{5,3},{7,1},{8,14},{10,12},{12... | collective-permute-start | bytes 294920 | tf_op jit(solution)/shard_map/ppermute | solution.py:429
  25.1 1.5 %collective-permute-start.12 = (f32[96,256]{1,0:T(8,128)S(1)}, f32[96,256]{1,0:T(8,128)S(1)}, u32[]{:S(2)}, u32[]{:S(2)}) collective-permute-start(f32[96,256]{1,0:T(8,128)S(1)} %get-tuple-element.22.refs_0_.refs_1_.refs_3_.refs_10_), channel_id=1, source_target_pairs={{0,4},{2,6},{4,0},{6,2},{1,5},{3,7},{5,1},{7,3},{8,12},{10,14},{12... | collective-permute-start | bytes 294920 | tf_op jit(solution)/shard_map/ppermute | solution.py:429
  27.1 3.1 %collective-permute-done.13.refs_6_.refs_13_ = f32[96,256]{1,0:T(8,128)S(1)} collective-permute-done((f32[96,256]{1,0:T(8,128)S(1)}, f32[96,256]{1,0:T(8,128)S(1)}, u32[]{:S(2)}, u32[]{:S(2)}) %collective-permute-start.13) | collective-permute-done | bytes 98336 | tf_op jit(solution)/shard_map/ppermute | solution.py:429
  30.2 1.6 %collective-permute-done.12.refs_5_.refs_12_ = f32[96,256]{1,0:T(8,128)S(1)} collective-permute-done((f32[96,256]{1,0:T(8,128)S(1)}, f32[96,256]{1,0:T(8,128)S(1)}, u32[]{:S(2)}, u32[]{:S(2)}) %collective-permute-start.12) | collective-permute-done | bytes 98336 | tf_op jit(solution)/shard_map/ppermute | solution.py:429
  32.3 1.6 %collective-permute-start.21 = (f32[96,256]{1,0:T(8,128)S(1)}, f32[96,256]{1,0:T(8,128)S(1)}, u32[]{:S(2)}, u32[]{:S(2)}) collective-permute-start(f32[96,256]{1,0:T(8,128)S(1)} %get-tuple-element.34), channel_id=1, source_target_pairs={{0,6},{2,4},{4,2},{6,0},{1,7},{3,5},{5,3},{7,1},{8,14},{10,12},{12... | collective-permute-start | bytes 294920 | tf_op jit(solution)/shard_map/ppermute | solution.py:438
  33.9 1.5 %collective-permute-start.20 = (f32[96,256]{1,0:T(8,128)S(1)}, f32[96,256]{1,0:T(8,128)S(1)}, u32[]{:S(2)}, u32[]{:S(2)}) collective-permute-start(f32[96,256]{1,0:T(8,128)S(1)} %get-tuple-element.35), channel_id=1, source_target_pairs={{0,4},{2,6},{4,0},{6,2},{1,5},{3,7},{5,1},{7,3},{8,12},{10,14},{12... | collective-permute-start | bytes 294920 | tf_op jit(solution)/shard_map/ppermute | solution.py:438
  38.6 1.5 %collective-permute-done.20.refs_14_ = f32[96,256]{1,0:T(8,128)S(1)} collective-permute-done((f32[96,256]{1,0:T(8,128)S(1)}, f32[96,256]{1,0:T(8,128)S(1)}, u32[]{:S(2)}, u32[]{:S(2)}) %collective-permute-start.20) | collective-permute-done | bytes 98336 | tf_op jit(solution)/shard_map/ppermute | solution.py:438
  40.2 1.9 %shard_map.90 = (f32[96,256]{1,0:T(8,128)S(1)}, f32[32,3,96]{2,1,0:T(4,128)S(1)}) custom-call(s32[7]{0:T(128)S(1)} %bitcast.35, f32[96,256]{1,0:T(8,128)S(1)} %get-tuple-element.22.refs_0_.refs_1_.refs_3_.refs_10_, f32[96,256]{1,0:T(8,128)S(1)} %shard_map.89.refs_2_, f32[96,256]{1,0:T(8,128)S(1)} %get-tuple-element.22.refs_0_.refs_1_.refs_3_.refs_10_, ...), custom_call_target="tpu_custom_call" | custom-call | flops 264241152 | bytes 3211264 | tf_op jit(solution)/shard_map/pallas_call | solution.py:121
  42.1 1.6 %collective-permute-start.24 = (f32[96,256]{1,0:T(8,128)S(1)}, f32[96,256]{1,0:T(8,128)S(1)}, u32[]{:S(2)}, u32[]{:S(2)}) collective-permute-start(f32[96,256]{1,0:T(8,128)S(1)} %get-tuple-element.26.refs_18_), channel_id=1, source_target_pairs={{0,6},{2,4},{4,2},{6,0},{1,7},{3,5},{5,3},{7,1},{8,14},{10,12},{12... | collective-permute-start | bytes 294920 | tf_op jit(solution)/shard_map/ppermute | solution.py:429
  43.6 1.5 %collective-permute-start.23 = (f32[96,256]{1,0:T(8,128)S(1)}, f32[96,256]{1,0:T(8,128)S(1)}, u32[]{:S(2)}, u32[]{:S(2)}) collective-permute-start(f32[96,256]{1,0:T(8,128)S(1)} %get-tuple-element.26.refs_18_), channel_id=1, source_target_pairs={{0,4},{2,6},{4,0},{6,2},{1,5},{3,7},{5,1},{7,3},{8,12},{10,14},{12... | collective-permute-start | bytes 294920 | tf_op jit(solution)/shard_map/ppermute | solution.py:429
  45.6 2.7 %collective-permute-done.24.refs_21_ = f32[96,256]{1,0:T(8,128)S(1)} collective-permute-done((f32[96,256]{1,0:T(8,128)S(1)}, f32[96,256]{1,0:T(8,128)S(1)}, u32[]{:S(2)}, u32[]{:S(2)}) %collective-permute-start.24) | collective-permute-done | bytes 98336 | tf_op jit(solution)/shard_map/ppermute | solution.py:429
  48.3 1.5 %collective-permute-done.23.refs_20_ = f32[96,256]{1,0:T(8,128)S(1)} collective-permute-done((f32[96,256]{1,0:T(8,128)S(1)}, f32[96,256]{1,0:T(8,128)S(1)}, u32[]{:S(2)}, u32[]{:S(2)}) %collective-permute-start.23) | collective-permute-done | bytes 98336 | tf_op jit(solution)/shard_map/ppermute | solution.py:429
  50.3 12.3 %all_to_all.10.refs_1_ = f32[32,3,96]{2,1,0:T(4,128)S(1)} all-to-all(f32[32,3,96]{2,1,0:T(4,128)S(1)} %get-tuple-element.25), channel_id=1, replica_groups=mesh['row'=4,'chip'=4,'core'=2] {'row','chip','core'}, dimensions={0} | all-to-all | bytes 73728 | tf_op jit(solution)/shard_map/all_to_all | solution.py:482
  62.6 6.0 %shard_map.91 = (f32[96,256]{1,0:T(8,128)S(1)}, f32[96,256]{1,0:T(8,128)S(1)}, f32[1,96]{1,0:T(1,128)S(1)}, f32[16,16,128]{2,1,0:T(8,128)S(1)}, f32[16,16,128]{2,1,0:T(8,128)S(1)}) custom-call(s32[7]{0:T(128)S(1)} %bitcast.36, f32[32,3,96]{2,1,0:T(4,128)S(1)} %all_to_all.10.refs_1_, f32[96,256]{1,0:T(8,128)S(1)} %bitcast.32, ...), custom_call_target="tpu_custom_call" | custom-call | flops 1056964608 | bytes 6590464 | tf_op jit(solution)/shard_map/pallas_call | solution.py:121
  70.1 10.6 %all_to_all.11.refs_0_ = f32[16,16,128]{2,1,0:T(8,128)S(1)} all-to-all(f32[16,16,128]{2,1,0:T(8,128)S(1)} %add.65), channel_id=1, replica_groups=mesh['row'=4,'chip'=4,'core'=2] {'row','chip'}, dimensions={0} | all-to-all | bytes 262144 | tf_op jit(solution)/shard_map/all_to_all | solution.py:510
  (56 shorter events, 10.6 us)
Async XLA Ops:
  3.0 10.1 %collective-permute-start.7 = (f32[4,96,256]{2,1,0:T(8,128)S(1)}, f32[4,96,256]{2,1,0:T(8,128)S(1)}, u32[]{:S(2)}, u32[]{:S(2)}) collective-permute-start(f32[4,96,256]{2,1,0:T(8,128)S(1)} %get-tuple-element.21), channel_id=1, source_target_pairs={{0,1},{1,0},{2,3},{3,2},{4,5},{5,4},{6,7},{7,6},{8,9},{9,8},{10,11... | collective-permute-start | bytes 1179656 | tf_op jit(solution)/shard_map/ppermute | solution.py:436
  3.6 7.0 %collective-permute-start.2 = (f32[96,256]{1,0:T(8,128)S(1)}, f32[96,256]{1,0:T(8,128)S(1)}, u32[]{:S(2)}, u32[]{:S(2)}) collective-permute-start(f32[96,256]{1,0:T(8,128)S(1)} %bitcast.27), channel_id=1, source_target_pairs={{0,6},{2,4},{4,2},{6,0},{1,7},{3,5},{5,3},{7,1},{8,14},{10,12},{12... | collective-permute-start | bytes 294920 | tf_op jit(solution)/shard_map/ppermute | solution.py:429
  7.1 5.5 %collective-permute-start.1 = (f32[96,256]{1,0:T(8,128)S(1)}, f32[96,256]{1,0:T(8,128)S(1)}, u32[]{:S(2)}, u32[]{:S(2)}) collective-permute-start(f32[96,256]{1,0:T(8,128)S(1)} %bitcast.28), channel_id=1, source_target_pairs={{0,4},{2,6},{4,0},{6,2},{1,5},{3,7},{5,1},{7,3},{8,12},{10,14},{12... | collective-permute-start | bytes 294920 | tf_op jit(solution)/shard_map/ppermute | solution.py:429
  7.6 5.2 %collective-permute-start = (f32[96,256]{1,0:T(8,128)S(1)}, f32[96,256]{1,0:T(8,128)S(1)}, u32[]{:S(2)}, u32[]{:S(2)}) collective-permute-start(f32[96,256]{1,0:T(8,128)S(1)} %bitcast.29), channel_id=1, source_target_pairs={{0,2},{2,0},{4,6},{6,4},{1,3},{3,1},{5,7},{7,5},{8,10},{10,8},{12,... | collective-permute-start | bytes 294920 | tf_op jit(solution)/shard_map/ppermute | solution.py:429
  7.7 7.2 %collective-permute-start.3 = (f32[96,256]{1,0:T(8,128)S(1)}, f32[96,256]{1,0:T(8,128)S(1)}, u32[]{:S(2)}, u32[]{:S(2)}) collective-permute-start(f32[96,256]{1,0:T(8,128)S(1)} %bitcast.30), channel_id=1, source_target_pairs={{0,1},{1,0},{2,3},{3,2},{4,5},{5,4},{6,7},{7,6},{8,9},{9,8},{10,11... | collective-permute-start | bytes 294920 | tf_op jit(solution)/shard_map/ppermute | solution.py:433
  10.5 5.8 %collective-permute-start.6 = (f32[96,256]{1,0:T(8,128)S(1)}, f32[96,256]{1,0:T(8,128)S(1)}, u32[]{:S(2)}, u32[]{:S(2)}) collective-permute-start(f32[96,256]{1,0:T(8,128)S(1)} %collective-permute-done.2.refs_6_.refs_5_), channel_id=1, source_target_pairs={{0,1},{1,0},{2,3},{3,2},{4,5},{5,4},{6,7},{7,6},{8,9},{9,8},{10,11... | collective-permute-start | bytes 294920 | tf_op jit(solution)/shard_map/ppermute | solution.py:433
  12.6 6.3 %collective-permute-start.5 = (f32[96,256]{1,0:T(8,128)S(1)}, f32[96,256]{1,0:T(8,128)S(1)}, u32[]{:S(2)}, u32[]{:S(2)}) collective-permute-start(f32[96,256]{1,0:T(8,128)S(1)} %collective-permute-done.1.refs_5_.refs_4_), channel_id=1, source_target_pairs={{0,1},{1,0},{2,3},{3,2},{4,5},{5,4},{6,7},{7,6},{8,9},{9,8},{10,11... | collective-permute-start | bytes 294920 | tf_op jit(solution)/shard_map/ppermute | solution.py:433
  12.8 6.1 %collective-permute-start.4 = (f32[96,256]{1,0:T(8,128)S(1)}, f32[96,256]{1,0:T(8,128)S(1)}, u32[]{:S(2)}, u32[]{:S(2)}) collective-permute-start(f32[96,256]{1,0:T(8,128)S(1)} %collective-permute-done.refs_4_.refs_3_), channel_id=1, source_target_pairs={{0,1},{1,0},{2,3},{3,2},{4,5},{5,4},{6,7},{7,6},{8,9},{9,8},{10,11... | collective-permute-start | bytes 294920 | tf_op jit(solution)/shard_map/ppermute | solution.py:433
  13.1 6.5 %collective-permute-start.10 = (f32[96,256]{1,0:T(8,128)S(1)}, f32[96,256]{1,0:T(8,128)S(1)}, u32[]{:S(2)}, u32[]{:S(2)}) collective-permute-start(f32[96,256]{1,0:T(8,128)S(1)} %get-tuple-element.38), channel_id=1, source_target_pairs={{0,6},{2,4},{4,2},{6,0},{1,7},{3,5},{5,3},{7,1},{8,14},{10,12},{12... | collective-permute-start | bytes 294920 | tf_op jit(solution)/shard_map/ppermute | solution.py:438
  14.9 6.2 %collective-permute-start.9 = (f32[96,256]{1,0:T(8,128)S(1)}, f32[96,256]{1,0:T(8,128)S(1)}, u32[]{:S(2)}, u32[]{:S(2)}) collective-permute-start(f32[96,256]{1,0:T(8,128)S(1)} %get-tuple-element.39), channel_id=1, source_target_pairs={{0,4},{2,6},{4,0},{6,2},{1,5},{3,7},{5,1},{7,3},{8,12},{10,14},{12... | collective-permute-start | bytes 294920 | tf_op jit(solution)/shard_map/ppermute | solution.py:438
  23.5 8.8 %collective-permute-start.18 = (f32[4,96,256]{2,1,0:T(8,128)S(1)}, f32[4,96,256]{2,1,0:T(8,128)S(1)}, u32[]{:S(2)}, u32[]{:S(2)}) collective-permute-start(f32[4,96,256]{2,1,0:T(8,128)S(1)} %get-tuple-element.24), channel_id=1, source_target_pairs={{0,1},{1,0},{2,3},{3,2},{4,5},{5,4},{6,7},{7,6},{8,9},{9,8},{10,11... | collective-permute-start | bytes 1179656 | tf_op jit(solution)/shard_map/ppermute | solution.py:436
  23.6 6.6 %collective-permute-start.13 = (f32[96,256]{1,0:T(8,128)S(1)}, f32[96,256]{1,0:T(8,128)S(1)}, u32[]{:S(2)}, u32[]{:S(2)}) collective-permute-start(f32[96,256]{1,0:T(8,128)S(1)} %get-tuple-element.22.refs_0_.refs_1_.refs_3_.refs_10_), channel_id=1, source_target_pairs={{0,6},{2,4},{4,2},{6,0},{1,7},{3,5},{5,3},{7,1},{8,14},{10,12},{12... | collective-permute-start | bytes 294920 | tf_op jit(solution)/shard_map/ppermute | solution.py:429
  25.1 6.6 %collective-permute-start.12 = (f32[96,256]{1,0:T(8,128)S(1)}, f32[96,256]{1,0:T(8,128)S(1)}, u32[]{:S(2)}, u32[]{:S(2)}) collective-permute-start(f32[96,256]{1,0:T(8,128)S(1)} %get-tuple-element.22.refs_0_.refs_1_.refs_3_.refs_10_), channel_id=1, source_target_pairs={{0,4},{2,6},{4,0},{6,2},{1,5},{3,7},{5,1},{7,3},{8,12},{10,14},{12... | collective-permute-start | bytes 294920 | tf_op jit(solution)/shard_map/ppermute | solution.py:429
  27.1 6.8 %collective-permute-start.14 = (f32[96,256]{1,0:T(8,128)S(1)}, f32[96,256]{1,0:T(8,128)S(1)}, u32[]{:S(2)}, u32[]{:S(2)}) collective-permute-start(f32[96,256]{1,0:T(8,128)S(1)} %get-tuple-element.22.refs_0_.refs_1_.refs_3_.refs_10_), channel_id=1, source_target_pairs={{0,1},{1,0},{2,3},{3,2},{4,5},{5,4},{6,7},{7,6},{8,9},{9,8},{10,11... | collective-permute-start | bytes 294920 | tf_op jit(solution)/shard_map/ppermute | solution.py:433
  31.8 5.5 %collective-permute-start.16 = (f32[96,256]{1,0:T(8,128)S(1)}, f32[96,256]{1,0:T(8,128)S(1)}, u32[]{:S(2)}, u32[]{:S(2)}) collective-permute-start(f32[96,256]{1,0:T(8,128)S(1)} %collective-permute-done.12.refs_5_.refs_12_), channel_id=1, source_target_pairs={{0,1},{1,0},{2,3},{3,2},{4,5},{5,4},{6,7},{7,6},{8,9},{9,8},{10,11... | collective-permute-start | bytes 294920 | tf_op jit(solution)/shard_map/ppermute | solution.py:433
  31.8 5.5 %collective-permute-start.15 = (f32[96,256]{1,0:T(8,128)S(1)}, f32[96,256]{1,0:T(8,128)S(1)}, u32[]{:S(2)}, u32[]{:S(2)}) collective-permute-start(f32[96,256]{1,0:T(8,128)S(1)} %collective-permute-done.11.refs_4_.refs_11_), channel_id=1, source_target_pairs={{0,1},{1,0},{2,3},{3,2},{4,5},{5,4},{6,7},{7,6},{8,9},{9,8},{10,11... | collective-permute-start | bytes 294920 | tf_op jit(solution)/shard_map/ppermute | solution.py:433
  32.3 6.3 %collective-permute-start.21 = (f32[96,256]{1,0:T(8,128)S(1)}, f32[96,256]{1,0:T(8,128)S(1)}, u32[]{:S(2)}, u32[]{:S(2)}) collective-permute-start(f32[96,256]{1,0:T(8,128)S(1)} %get-tuple-element.34), channel_id=1, source_target_pairs={{0,6},{2,4},{4,2},{6,0},{1,7},{3,5},{5,3},{7,1},{8,14},{10,12},{12... | collective-permute-start | bytes 294920 | tf_op jit(solution)/shard_map/ppermute | solution.py:438
  33.9 6.2 %collective-permute-start.20 = (f32[96,256]{1,0:T(8,128)S(1)}, f32[96,256]{1,0:T(8,128)S(1)}, u32[]{:S(2)}, u32[]{:S(2)}) collective-permute-start(f32[96,256]{1,0:T(8,128)S(1)} %get-tuple-element.35), channel_id=1, source_target_pairs={{0,4},{2,6},{4,0},{6,2},{1,5},{3,7},{5,1},{7,3},{8,12},{10,14},{12... | collective-permute-start | bytes 294920 | tf_op jit(solution)/shard_map/ppermute | solution.py:438
  42.1 6.3 %collective-permute-start.24 = (f32[96,256]{1,0:T(8,128)S(1)}, f32[96,256]{1,0:T(8,128)S(1)}, u32[]{:S(2)}, u32[]{:S(2)}) collective-permute-start(f32[96,256]{1,0:T(8,128)S(1)} %get-tuple-element.26.refs_18_), channel_id=1, source_target_pairs={{0,6},{2,4},{4,2},{6,0},{1,7},{3,5},{5,3},{7,1},{8,14},{10,12},{12... | collective-permute-start | bytes 294920 | tf_op jit(solution)/shard_map/ppermute | solution.py:429
  43.6 6.2 %collective-permute-start.23 = (f32[96,256]{1,0:T(8,128)S(1)}, f32[96,256]{1,0:T(8,128)S(1)}, u32[]{:S(2)}, u32[]{:S(2)}) collective-permute-start(f32[96,256]{1,0:T(8,128)S(1)} %get-tuple-element.26.refs_18_), channel_id=1, source_target_pairs={{0,4},{2,6},{4,0},{6,2},{1,5},{3,7},{5,1},{7,3},{8,12},{10,14},{12... | collective-permute-start | bytes 294920 | tf_op jit(solution)/shard_map/ppermute | solution.py:429
  45.6 17.0 %collective-permute-start.25 = (f32[96,256]{1,0:T(8,128)S(1)}, f32[96,256]{1,0:T(8,128)S(1)}, u32[]{:S(2)}, u32[]{:S(2)}) collective-permute-start(f32[96,256]{1,0:T(8,128)S(1)} %get-tuple-element.26.refs_18_), channel_id=1, source_target_pairs={{0,1},{1,0},{2,3},{3,2},{4,5},{5,4},{6,7},{7,6},{8,9},{9,8},{10,11... | collective-permute-start | bytes 294920 | tf_op jit(solution)/shard_map/ppermute | solution.py:433
  48.3 14.3 %collective-permute-start.28 = (f32[96,256]{1,0:T(8,128)S(1)}, f32[96,256]{1,0:T(8,128)S(1)}, u32[]{:S(2)}, u32[]{:S(2)}) collective-permute-start(f32[96,256]{1,0:T(8,128)S(1)} %collective-permute-done.24.refs_21_), channel_id=1, source_target_pairs={{0,1},{1,0},{2,3},{3,2},{4,5},{5,4},{6,7},{7,6},{8,9},{9,8},{10,11... | collective-permute-start | bytes 294920 | tf_op jit(solution)/shard_map/ppermute | solution.py:433
  49.8 12.8 %collective-permute-start.27 = (f32[96,256]{1,0:T(8,128)S(1)}, f32[96,256]{1,0:T(8,128)S(1)}, u32[]{:S(2)}, u32[]{:S(2)}) collective-permute-start(f32[96,256]{1,0:T(8,128)S(1)} %collective-permute-done.23.refs_20_), channel_id=1, source_target_pairs={{0,1},{1,0},{2,3},{3,2},{4,5},{5,4},{6,7},{7,6},{8,9},{9,8},{10,11... | collective-permute-start | bytes 294920 | tf_op jit(solution)/shard_map/ppermute | solution.py:433
  49.9 12.8 %collective-permute-start.26 = (f32[96,256]{1,0:T(8,128)S(1)}, f32[96,256]{1,0:T(8,128)S(1)}, u32[]{:S(2)}, u32[]{:S(2)}) collective-permute-start(f32[96,256]{1,0:T(8,128)S(1)} %collective-permute-done.22.refs_19_), channel_id=1, source_target_pairs={{0,1},{1,0},{2,3},{3,2},{4,5},{5,4},{6,7},{7,6},{8,9},{9,8},{10,11... | collective-permute-start | bytes 294920 | tf_op jit(solution)/shard_map/ppermute | solution.py:433
  (10 other events, 83.8 us)

commit v2 on v1

--- a/solution.py
+++ b/solution.py
@@ -201,32 +201,29 @@
     ]
 
 
-def fresh_pairs(tiles):
-    n = tiles.shape[0]
-    half = (n + 1) // 2
+def first_kernel(way, cols, panel, tiles, keep, send, split_tiles, work):
+    cols = cols.wait()
+    n = split_tiles.shape[1]
 
     def pair(k):
-        if k in (0, half):
-            tiles.wait(half if k == 0 else n)
-        return split(tiles.ref[k])
-
-    return [functools.partial(pair, k) for k in range(n)]
-
-
-def first_kernel(way, cols, panel, tiles, keep, send, work):
-    cols = cols.wait()
-    contributions(way, cols, fresh_pairs(tiles), split(panel.all()), work, keep, send)
-
-
-def prepare_kernel(panel, diag, tiles, image, split_tiles):
-    image[...] = dot_full(panel.all(), diag.all(), NT)
-    tiles.wait()
+        if k in (0, (n + 1) // 2):
+            tiles.wait(n if k else (n + 1) // 2)
+        high, low = split(tiles.ref[k])
+        split_tiles[0, k], split_tiles[1, k] = high, low
+        return high, low
+
+    pairs = [functools.partial(pair, k) for k in range(n)]
+    contributions(way, cols, pairs, split(panel.all()), work, keep, send)
+
+
+def diag_kernel(panel, diag, image):
+    image[...] = dot_full(panel[...], diag[...], NT)
+
+
+def diag_split_kernel(panel, diag, tiles, image, split_tiles):
+    diag_kernel(panel, diag, image)
     for k in range(tiles.shape[0]):
-        split_tiles[0, k], split_tiles[1, k] = split(tiles.ref[k])
-
-
-def diag_kernel(panel, diag, image):
-    image[...] = dot_full(panel[...], diag.all(), NT)
+        split_tiles[0, k], split_tiles[1, k] = split(tiles[k])
 
 
 def residual_kernel(
@@ -281,9 +278,9 @@
     residuals,
     images,
     split_tiles,
+    newton_tiles,
     diag,
     newton_diag,
-    newton_tiles,
     x_out,
     d_out,
     norm_out,
@@ -294,7 +291,6 @@
     blocks,
     pieces,
 ):
-    n = newton_tiles.shape[0]
     norm_out[...], step, grow = steps(sums)
     count = d_out.shape[0]
     for k, image in enumerate(images):
@@ -313,23 +309,28 @@
     def product(rows, tile):
         return lax.dot_general(rows, tile, NT, preferred_element_type=F32)
 
-    high, low = split(diag.all() * 0.5)
-    own = held[0]
-    first = product(own[count : 3 * count], high)
-    second = product(own[count : 2 * count], low)
-    for k in range(n):
-        block = held[found[k]]
-        first += product(block[count : 3 * count], split_tiles[0, k])
-        second += product(block[count : 2 * count], split_tiles[1, k])
+    first = second = None
+    for seat, pair in zip(found, held_pairs(split_tiles)):
+        block, (high, low) = held[seat], pair()
+        one = product(block[count : 3 * count], high)
+        two = product(block[count : 2 * count], low)
+        first = one if first is None else first + one
+        second = two if second is None else second + two
+    own, (high, low) = held[0], split(diag[...] * 0.5)
+    first += product(own[count : 3 * count], high)
+    second += product(own[count : 2 * count], low)
     half_d = first[:count] + (first[count:] + second)
     curvature = 2.0 * row_sums(d1 * half_d)
-    high, low = split(newton_diag.all() * 0.5)
-    first = product(own, high)
-    second = product(own[: 2 * count], low)
-    for seat, pair in zip(found, fresh_pairs(newton_tiles)):
+    first = second = None
+    for seat, pair in zip(found, held_pairs(newton_tiles)):
         block, (high, low) = held[seat], pair()
-        first += product(block, high)
-        second += product(block[: 2 * count], low)
+        one = product(block, high)
+        two = product(block[: 2 * count], low)
+        first = one if first is None else first + one
+        second = two if second is None else second + two
+    high, low = split(newton_diag[...] * 0.5)
+    first += product(own, high)
+    second += product(own[: 2 * count], low)
     ux = first[:count] + (first[3 * count :] + second[:count])
     ud = first[count : 2 * count] + (first[2 * count : 3 * count] + second[count:])
     hr, hc = count // parts_rows, count // parts_cols
@@ -435,13 +436,16 @@
     def scatter(keep, send):
         received = lax.ppermute(send, "core", swap)
         sums = [keep[k] + received[k] for k in range(chips)]
-        return [sums[0]] + [lax.ppermute(sums[k], "chip", way.pairs(k)) for k in range(1, chips)]
+        added = [sums[0]]
+        for k in range(1, chips):
+            added.append(lax.ppermute(sums[k], "chip", way.pairs(k)))
+        return added
 
     start = warm_start[0]
     starts = gather(start)
-    keep, send = call(
+    keep, send, split_tiles = call(
         functools.partial(first_kernel, way),
-        [stack, stack],
+        [stack, stack, parts],
         [],
         [Far(cols, pltpu.SMEM), Far(start), Far(tiles)],
         scratch=[work],
@@ -449,13 +453,7 @@
     )
     added = scatter(keep, send)
     starts = forward(starts)
-    base, split_tiles = call(
-        prepare_kernel,
-        [panel, parts],
-        [],
-        [Far(start), Far(diag), Far(tiles)],
-        flops=4 * unit,
-    )
+    (base,) = call(diag_kernel, [panel], [], [start, diag], flops=2 * unit)
     residual, keep, send = call(
         functools.partial(residual_kernel, way),
         [panel, stack, stack],
@@ -467,8 +465,12 @@
     residuals = gather(residual)
     added = scatter(keep, send)
     residuals = forward(residuals)
-    (base,) = call(
-        diag_kernel, [panel], [], [residual, Far(diag)], flops=2 * unit
+    base, newton_tiles = call(
+        diag_split_kernel,
+        [panel, parts],
+        [],
+        [residual, diag, ntiles],
+        flops=4 * unit,
     )
     image, sums = call(
         functools.partial(image_kernel, way),
@@ -494,9 +496,9 @@
             residuals,
             images,
             split_tiles,
-            Far(diag),
-            Far(ndiag),
-            Far(ntiles),
+            newton_tiles,
+            diag,
+            ndiag,
         ],
         scratch=[
             jax.ShapeDtypeStruct((2 * chips + 1, 4 * count, size), BF16),

time: 81.8 us -> 80.6 us (0.985)
  Pallas kernels: 16.8 us -> 13.1 us
  waiting for transfers between devices: 20.4 us -> 22.9 us
    pallas_call x7, Pallas kernels: 16.8 us -> 13.1 us  [call(): pl.pallas_call(kernel, out_shape=outs, in_specs=specs, out_specs=[vmem] *...]
    ppermute x6, waiting for transfers between devices: 5.15 us -> 7.66 us  [scatter(): added.append(lax.ppermute(sums[k], 'chip', way.pairs(k)))]
  transfers between devices with their start and end apart: 30 -> 30, of which waited for: 12 -> 12; matrix products, arithmetic and copies ran while one was open for 0% -> 0% of each run, Pallas kernels for 4% -> 1%
where the time goes in v2:
time: 80.6 us; the launch traced here: 80.4 us
  waiting for transfers between devices  22.9 us (28%)
  blocking collectives  22.9 us (28%)
  starting transfers between devices  20.5 us (25%)
  Pallas kernels  13.1 us (16%)
  between operations  0.82 us (1%)
    ppermute x9, waiting for transfers between devices, gather(): same[way.source(k)] = lax.ppermute(value, 'chip', way.pairs(k))  14 us
    pallas_call x7, Pallas kernels, call(): pl.pallas_call(kernel, out_shape=outs, in_specs=specs, out_specs=[vmem] *...  13.1 us
    all_to_all x1, blocking collectives, on_device(): sums = lax.all_to_all(sums, ALL, 0, 0, tiled=True)  12.3 us
    ppermute x9, starting transfers between devices, gather(): same[way.source(k)] = lax.ppermute(value, 'chip', way.pairs(k))  11.3 us
    all_to_all x1, blocking collectives, on_device(): lax.all_to_all(keep + received, ('row', 'chip'), 0, 0, tiled=True)  10.6 us
    ppermute x6, waiting for transfers between devices, scatter(): added.append(lax.ppermute(sums[k], 'chip', way.pairs(k)))  7.66 us
    ppermute x6, starting transfers between devices, scatter(): added.append(lax.ppermute(sums[k], 'chip', way.pairs(k)))  7.11 us
  transfers between devices with their start and end apart: 30, of which 12 were waited for; matrix products, arithmetic and copies ran while one was open for 0% of the time, Pallas kernels for 1%

profile of v2, /device:TPU:0, one launch (start us, length us, event | category | flops | bytes accessed | tf_op | source)
XLA Modules:
  0.0 80.4 jit_solution(2812123298720193436)
XLA Ops:
  0.7 2.3 %shard_map.87 = (f32[4,96,256]{2,1,0:T(8,128)S(1)}, f32[4,96,256]{2,1,0:T(8,128)S(1)}, bf16[2,7,256,256]{3,2,1,0:T(8,128)(2,1)S(1)}) custom-call(s32[7]{0:T(128)} %bitcast.38, f32[96,256]{1,0:T(8,128)} %bitcast.29, f32[7,256,256]{2,1,0:T(8,128)} %bitcast.43), custom_call_target="tpu_custom_call" | custom-call | flops 264241152 | bytes 1933340 | tf_op jit(solution)/shard_map/pallas_call | solution.py:121
  3.6 3.5 %collective-permute-start.2 = (f32[96,256]{1,0:T(8,128)S(1)}, f32[96,256]{1,0:T(8,128)S(1)}, u32[]{:S(2)}, u32[]{:S(2)}) collective-permute-start(f32[96,256]{1,0:T(8,128)S(1)} %bitcast.30), channel_id=1, source_target_pairs={{0,6},{2,4},{4,2},{6,0},{1,7},{3,5},{5,3},{7,1},{8,14},{10,12},{12... | collective-permute-start | bytes 294920 | tf_op jit(solution)/shard_map/ppermute | solution.py:430
  7.7 2.8 %collective-permute-done.2.refs_6_.refs_5_ = f32[96,256]{1,0:T(8,128)S(1)} collective-permute-done((f32[96,256]{1,0:T(8,128)S(1)}, f32[96,256]{1,0:T(8,128)S(1)}, u32[]{:S(2)}, u32[]{:S(2)}) %collective-permute-start.2) | collective-permute-done | bytes 98336 | tf_op jit(solution)/shard_map/ppermute | solution.py:430
  10.5 2.0 %collective-permute-done.1.refs_5_.refs_4_ = f32[96,256]{1,0:T(8,128)S(1)} collective-permute-done((f32[96,256]{1,0:T(8,128)S(1)}, f32[96,256]{1,0:T(8,128)S(1)}, u32[]{:S(2)}, u32[]{:S(2)}) %collective-permute-start.1) | collective-permute-done | bytes 98336 | tf_op jit(solution)/shard_map/ppermute | solution.py:430
  13.2 1.8 %collective-permute-start.10 = (f32[96,256]{1,0:T(8,128)S(1)}, f32[96,256]{1,0:T(8,128)S(1)}, u32[]{:S(2)}, u32[]{:S(2)}) collective-permute-start(f32[96,256]{1,0:T(8,128)S(1)} %get-tuple-element.40), channel_id=1, source_target_pairs={{0,6},{2,4},{4,2},{6,0},{1,7},{3,5},{5,3},{7,1},{8,14},{10,12},{12... | collective-permute-start | bytes 294920 | tf_op jit(solution)/shard_map/ppermute | solution.py:441
  17.1 2.5 %collective-permute-done.10.refs_15_ = f32[96,256]{1,0:T(8,128)S(1)} collective-permute-done((f32[96,256]{1,0:T(8,128)S(1)}, f32[96,256]{1,0:T(8,128)S(1)}, u32[]{:S(2)}, u32[]{:S(2)}) %collective-permute-start.10) | collective-permute-done | bytes 98336 | tf_op jit(solution)/shard_map/ppermute | solution.py:441
  19.7 1.5 %collective-permute-done.9.refs_14_ = f32[96,256]{1,0:T(8,128)S(1)} collective-permute-done((f32[96,256]{1,0:T(8,128)S(1)}, f32[96,256]{1,0:T(8,128)S(1)}, u32[]{:S(2)}, u32[]{:S(2)}) %collective-permute-start.9) | collective-permute-done | bytes 98336 | tf_op jit(solution)/shard_map/ppermute | solution.py:441
  21.2 2.3 %shard_map.88 = (f32[96,256]{1,0:T(8,128)S(1)}, f32[4,96,256]{2,1,0:T(8,128)S(1)}, f32[4,96,256]{2,1,0:T(8,128)S(1)}) custom-call(s32[7]{0:T(128)S(1)} %bitcast.39, f32[96,256]{1,0:T(8,128)S(1)} %shard_map.86.refs_1_, s32[1,96]{1,0:T(1,128)S(1)} %bitcast.42, f32[96,256]{1,0:T(8,128)S(1)} %bitcast.35, f32[96,256]{1,0:T(8,128)S(1)} %collective-permute-done.refs_4_.refs_3_, ...), custom_call_target="tpu_custom_call" | custom-call | flops 528482304 | bytes 3113344 | tf_op jit(solution)/shard_map/pallas_call | solution.py:121
  23.6 1.6 %collective-permute-start.13 = (f32[96,256]{1,0:T(8,128)S(1)}, f32[96,256]{1,0:T(8,128)S(1)}, u32[]{:S(2)}, u32[]{:S(2)}) collective-permute-start(f32[96,256]{1,0:T(8,128)S(1)} %get-tuple-element.22.refs_0_.refs_1_.refs_3_.refs_10_), channel_id=1, source_target_pairs={{0,6},{2,4},{4,2},{6,0},{1,7},{3,5},{5,3},{7,1},{8,14},{10,12},{12... | collective-permute-start | bytes 294920 | tf_op jit(solution)/shard_map/ppermute | solution.py:430
  25.1 1.5 %collective-permute-start.12 = (f32[96,256]{1,0:T(8,128)S(1)}, f32[96,256]{1,0:T(8,128)S(1)}, u32[]{:S(2)}, u32[]{:S(2)}) collective-permute-start(f32[96,256]{1,0:T(8,128)S(1)} %get-tuple-element.22.refs_0_.refs_1_.refs_3_.refs_10_), channel_id=1, source_target_pairs={{0,4},{2,6},{4,0},{6,2},{1,5},{3,7},{5,1},{7,3},{8,12},{10,14},{12... | collective-permute-start | bytes 294920 | tf_op jit(solution)/shard_map/ppermute | solution.py:430
  27.1 3.1 %collective-permute-done.13.refs_6_.refs_13_ = f32[96,256]{1,0:T(8,128)S(1)} collective-permute-done((f32[96,256]{1,0:T(8,128)S(1)}, f32[96,256]{1,0:T(8,128)S(1)}, u32[]{:S(2)}, u32[]{:S(2)}) %collective-permute-start.13) | collective-permute-done | bytes 98336 | tf_op jit(solution)/shard_map/ppermute | solution.py:430
  30.2 1.6 %collective-permute-done.12.refs_5_.refs_12_ = f32[96,256]{1,0:T(8,128)S(1)} collective-permute-done((f32[96,256]{1,0:T(8,128)S(1)}, f32[96,256]{1,0:T(8,128)S(1)}, u32[]{:S(2)}, u32[]{:S(2)}) %collective-permute-start.12) | collective-permute-done | bytes 98336 | tf_op jit(solution)/shard_map/ppermute | solution.py:430
  32.4 1.6 %collective-permute-start.21 = (f32[96,256]{1,0:T(8,128)S(1)}, f32[96,256]{1,0:T(8,128)S(1)}, u32[]{:S(2)}, u32[]{:S(2)}) collective-permute-start(f32[96,256]{1,0:T(8,128)S(1)} %get-tuple-element.36), channel_id=1, source_target_pairs={{0,6},{2,4},{4,2},{6,0},{1,7},{3,5},{5,3},{7,1},{8,14},{10,12},{12... | collective-permute-start | bytes 294920 | tf_op jit(solution)/shard_map/ppermute | solution.py:441
  33.9 1.5 %collective-permute-start.20 = (f32[96,256]{1,0:T(8,128)S(1)}, f32[96,256]{1,0:T(8,128)S(1)}, u32[]{:S(2)}, u32[]{:S(2)}) collective-permute-start(f32[96,256]{1,0:T(8,128)S(1)} %get-tuple-element.37), channel_id=1, source_target_pairs={{0,4},{2,6},{4,0},{6,2},{1,5},{3,7},{5,1},{7,3},{8,12},{10,14},{12... | collective-permute-start | bytes 294920 | tf_op jit(solution)/shard_map/ppermute | solution.py:441
  36.6 2.0 %collective-permute-done.21.refs_15_ = f32[96,256]{1,0:T(8,128)S(1)} collective-permute-done((f32[96,256]{1,0:T(8,128)S(1)}, f32[96,256]{1,0:T(8,128)S(1)}, u32[]{:S(2)}, u32[]{:S(2)}) %collective-permute-start.21) | collective-permute-done | bytes 98336 | tf_op jit(solution)/shard_map/ppermute | solution.py:441
  38.7 1.5 %collective-permute-done.20.refs_14_ = f32[96,256]{1,0:T(8,128)S(1)} collective-permute-done((f32[96,256]{1,0:T(8,128)S(1)}, f32[96,256]{1,0:T(8,128)S(1)}, u32[]{:S(2)}, u32[]{:S(2)}) %collective-permute-start.20) | collective-permute-done | bytes 98336 | tf_op jit(solution)/shard_map/ppermute | solution.py:441
  40.2 1.9 %shard_map.90 = (f32[96,256]{1,0:T(8,128)S(1)}, f32[32,3,96]{2,1,0:T(4,128)S(1)}) custom-call(s32[7]{0:T(128)S(1)} %bitcast.40, f32[96,256]{1,0:T(8,128)S(1)} %get-tuple-element.22.refs_0_.refs_1_.refs_3_.refs_10_, f32[96,256]{1,0:T(8,128)S(1)} %get-tuple-element.23.refs_2_, f32[96,256]{1,0:T(8,128)S(1)} %get-tuple-element.22.refs_0_.refs_1_.refs_3_.refs_10_, ...), custom_call_target="tpu_custom_call" | custom-call | flops 264241152 | bytes 3211264 | tf_op jit(solution)/shard_map/pallas_call | solution.py:121
  42.1 1.6 %collective-permute-start.24 = (f32[96,256]{1,0:T(8,128)S(1)}, f32[96,256]{1,0:T(8,128)S(1)}, u32[]{:S(2)}, u32[]{:S(2)}) collective-permute-start(f32[96,256]{1,0:T(8,128)S(1)} %get-tuple-element.27.refs_18_), channel_id=1, source_target_pairs={{0,6},{2,4},{4,2},{6,0},{1,7},{3,5},{5,3},{7,1},{8,14},{10,12},{12... | collective-permute-start | bytes 294920 | tf_op jit(solution)/shard_map/ppermute | solution.py:430
  43.6 1.5 %collective-permute-start.23 = (f32[96,256]{1,0:T(8,128)S(1)}, f32[96,256]{1,0:T(8,128)S(1)}, u32[]{:S(2)}, u32[]{:S(2)}) collective-permute-start(f32[96,256]{1,0:T(8,128)S(1)} %get-tuple-element.27.refs_18_), channel_id=1, source_target_pairs={{0,4},{2,6},{4,0},{6,2},{1,5},{3,7},{5,1},{7,3},{8,12},{10,14},{12... | collective-permute-start | bytes 294920 | tf_op jit(solution)/shard_map/ppermute | solution.py:430
  45.6 2.7 %collective-permute-done.24.refs_21_ = f32[96,256]{1,0:T(8,128)S(1)} collective-permute-done((f32[96,256]{1,0:T(8,128)S(1)}, f32[96,256]{1,0:T(8,128)S(1)}, u32[]{:S(2)}, u32[]{:S(2)}) %collective-permute-start.24) | collective-permute-done | bytes 98336 | tf_op jit(solution)/shard_map/ppermute | solution.py:430
  48.4 1.5 %collective-permute-done.23.refs_20_ = f32[96,256]{1,0:T(8,128)S(1)} collective-permute-done((f32[96,256]{1,0:T(8,128)S(1)}, f32[96,256]{1,0:T(8,128)S(1)}, u32[]{:S(2)}, u32[]{:S(2)}) %collective-permute-start.23) | collective-permute-done | bytes 98336 | tf_op jit(solution)/shard_map/ppermute | solution.py:430
  50.4 12.3 %all_to_all.10.refs_1_ = f32[32,3,96]{2,1,0:T(4,128)S(1)} all-to-all(f32[32,3,96]{2,1,0:T(4,128)S(1)} %get-tuple-element.26), channel_id=1, replica_groups=mesh['row'=4,'chip'=4,'core'=2] {'row','chip','core'}, dimensions={0} | all-to-all | bytes 73728 | tf_op jit(solution)/shard_map/all_to_all | solution.py:484
  62.7 4.8 %shard_map.91 = (f32[96,256]{1,0:T(8,128)S(1)}, f32[96,256]{1,0:T(8,128)S(1)}, f32[1,96]{1,0:T(1,128)S(1)}, f32[16,16,128]{2,1,0:T(8,128)S(1)}, f32[16,16,128]{2,1,0:T(8,128)S(1)}) custom-call(s32[7]{0:T(128)S(1)} %bitcast.41, f32[32,3,96]{2,1,0:T(4,128)S(1)} %all_to_all.10.refs_1_, f32[96,256]{1,0:T(8,128)S(1)} %bitcast.36, ...), custom_call_target="tpu_custom_call" | custom-call | flops 1056964608 | bytes 6590464 | tf_op jit(solution)/shard_map/pallas_call | solution.py:121
  68.9 10.6 %all_to_all.11.refs_0_ = f32[16,16,128]{2,1,0:T(8,128)S(1)} all-to-all(f32[16,16,128]{2,1,0:T(8,128)S(1)} %add.65), channel_id=1, replica_groups=mesh['row'=4,'chip'=4,'core'=2] {'row','chip'}, dimensions={0} | all-to-all | bytes 262144 | tf_op jit(solution)/shard_map/all_to_all | solution.py:512
  (60 shorter events, 9.7 us)
Async XLA Ops:
  3.0 10.1 %collective-permute-start.7 = (f32[4,96,256]{2,1,0:T(8,128)S(1)}, f32[4,96,256]{2,1,0:T(8,128)S(1)}, u32[]{:S(2)}, u32[]{:S(2)}) collective-permute-start(f32[4,96,256]{2,1,0:T(8,128)S(1)} %get-tuple-element.21), channel_id=1, source_target_pairs={{0,1},{1,0},{2,3},{3,2},{4,5},{5,4},{6,7},{7,6},{8,9},{9,8},{10,11... | collective-permute-start | bytes 1179656 | tf_op jit(solution)/shard_map/ppermute | solution.py:437
  3.6 7.0 %collective-permute-start.2 = (f32[96,256]{1,0:T(8,128)S(1)}, f32[96,256]{1,0:T(8,128)S(1)}, u32[]{:S(2)}, u32[]{:S(2)}) collective-permute-start(f32[96,256]{1,0:T(8,128)S(1)} %bitcast.30), channel_id=1, source_target_pairs={{0,6},{2,4},{4,2},{6,0},{1,7},{3,5},{5,3},{7,1},{8,14},{10,12},{12... | collective-permute-start | bytes 294920 | tf_op jit(solution)/shard_map/ppermute | solution.py:430
  7.1 5.5 %collective-permute-start.1 = (f32[96,256]{1,0:T(8,128)S(1)}, f32[96,256]{1,0:T(8,128)S(1)}, u32[]{:S(2)}, u32[]{:S(2)}) collective-permute-start(f32[96,256]{1,0:T(8,128)S(1)} %bitcast.31), channel_id=1, source_target_pairs={{0,4},{2,6},{4,0},{6,2},{1,5},{3,7},{5,1},{7,3},{8,12},{10,14},{12... | collective-permute-start | bytes 294920 | tf_op jit(solution)/shard_map/ppermute | solution.py:430
  7.6 5.2 %collective-permute-start = (f32[96,256]{1,0:T(8,128)S(1)}, f32[96,256]{1,0:T(8,128)S(1)}, u32[]{:S(2)}, u32[]{:S(2)}) collective-permute-start(f32[96,256]{1,0:T(8,128)S(1)} %bitcast.32), channel_id=1, source_target_pairs={{0,2},{2,0},{4,6},{6,4},{1,3},{3,1},{5,7},{7,5},{8,10},{10,8},{12,... | collective-permute-start | bytes 294920 | tf_op jit(solution)/shard_map/ppermute | solution.py:430
  7.7 7.2 %collective-permute-start.3 = (f32[96,256]{1,0:T(8,128)S(1)}, f32[96,256]{1,0:T(8,128)S(1)}, u32[]{:S(2)}, u32[]{:S(2)}) collective-permute-start(f32[96,256]{1,0:T(8,128)S(1)} %bitcast.33), channel_id=1, source_target_pairs={{0,1},{1,0},{2,3},{3,2},{4,5},{5,4},{6,7},{7,6},{8,9},{9,8},{10,11... | collective-permute-start | bytes 294920 | tf_op jit(solution)/shard_map/ppermute | solution.py:434
  10.5 5.8 %collective-permute-start.6 = (f32[96,256]{1,0:T(8,128)S(1)}, f32[96,256]{1,0:T(8,128)S(1)}, u32[]{:S(2)}, u32[]{:S(2)}) collective-permute-start(f32[96,256]{1,0:T(8,128)S(1)} %collective-permute-done.2.refs_6_.refs_5_), channel_id=1, source_target_pairs={{0,1},{1,0},{2,3},{3,2},{4,5},{5,4},{6,7},{7,6},{8,9},{9,8},{10,11... | collective-permute-start | bytes 294920 | tf_op jit(solution)/shard_map/ppermute | solution.py:434
  13.2 6.5 %collective-permute-start.10 = (f32[96,256]{1,0:T(8,128)S(1)}, f32[96,256]{1,0:T(8,128)S(1)}, u32[]{:S(2)}, u32[]{:S(2)}) collective-permute-start(f32[96,256]{1,0:T(8,128)S(1)} %get-tuple-element.40), channel_id=1, source_target_pairs={{0,6},{2,4},{4,2},{6,0},{1,7},{3,5},{5,3},{7,1},{8,14},{10,12},{12... | collective-permute-start | bytes 294920 | tf_op jit(solution)/shard_map/ppermute | solution.py:441
  15.0 6.2 %collective-permute-start.9 = (f32[96,256]{1,0:T(8,128)S(1)}, f32[96,256]{1,0:T(8,128)S(1)}, u32[]{:S(2)}, u32[]{:S(2)}) collective-permute-start(f32[96,256]{1,0:T(8,128)S(1)} %get-tuple-element.41), channel_id=1, source_target_pairs={{0,4},{2,6},{4,0},{6,2},{1,5},{3,7},{5,1},{7,3},{8,12},{10,14},{12... | collective-permute-start | bytes 294920 | tf_op jit(solution)/shard_map/ppermute | solution.py:441
  16.4 4.8 %collective-permute-start.8 = (f32[96,256]{1,0:T(8,128)S(1)}, f32[96,256]{1,0:T(8,128)S(1)}, u32[]{:S(2)}, u32[]{:S(2)}) collective-permute-start(f32[96,256]{1,0:T(8,128)S(1)} %get-tuple-element.42), channel_id=1, source_target_pairs={{0,2},{2,0},{4,6},{6,4},{1,3},{3,1},{5,7},{7,5},{8,10},{10,8},{12,... | collective-permute-start | bytes 294920 | tf_op jit(solution)/shard_map/ppermute | solution.py:441
  23.5 8.8 %collective-permute-start.18 = (f32[4,96,256]{2,1,0:T(8,128)S(1)}, f32[4,96,256]{2,1,0:T(8,128)S(1)}, u32[]{:S(2)}, u32[]{:S(2)}) collective-permute-start(f32[4,96,256]{2,1,0:T(8,128)S(1)} %get-tuple-element.25), channel_id=1, source_target_pairs={{0,1},{1,0},{2,3},{3,2},{4,5},{5,4},{6,7},{7,6},{8,9},{9,8},{10,11... | collective-permute-start | bytes 1179656 | tf_op jit(solution)/shard_map/ppermute | solution.py:437
  23.6 6.6 %collective-permute-start.13 = (f32[96,256]{1,0:T(8,128)S(1)}, f32[96,256]{1,0:T(8,128)S(1)}, u32[]{:S(2)}, u32[]{:S(2)}) collective-permute-start(f32[96,256]{1,0:T(8,128)S(1)} %get-tuple-element.22.refs_0_.refs_1_.refs_3_.refs_10_), channel_id=1, source_target_pairs={{0,6},{2,4},{4,2},{6,0},{1,7},{3,5},{5,3},{7,1},{8,14},{10,12},{12... | collective-permute-start | bytes 294920 | tf_op jit(solution)/shard_map/ppermute | solution.py:430
  25.1 6.6 %collective-permute-start.12 = (f32[96,256]{1,0:T(8,128)S(1)}, f32[96,256]{1,0:T(8,128)S(1)}, u32[]{:S(2)}, u32[]{:S(2)}) collective-permute-start(f32[96,256]{1,0:T(8,128)S(1)} %get-tuple-element.22.refs_0_.refs_1_.refs_3_.refs_10_), channel_id=1, source_target_pairs={{0,4},{2,6},{4,0},{6,2},{1,5},{3,7},{5,1},{7,3},{8,12},{10,14},{12... | collective-permute-start | bytes 294920 | tf_op jit(solution)/shard_map/ppermute | solution.py:430
  26.6 5.2 %collective-permute-start.11 = (f32[96,256]{1,0:T(8,128)S(1)}, f32[96,256]{1,0:T(8,128)S(1)}, u32[]{:S(2)}, u32[]{:S(2)}) collective-permute-start(f32[96,256]{1,0:T(8,128)S(1)} %get-tuple-element.22.refs_0_.refs_1_.refs_3_.refs_10_), channel_id=1, source_target_pairs={{0,2},{2,0},{4,6},{6,4},{1,3},{3,1},{5,7},{7,5},{8,10},{10,8},{12,... | collective-permute-start | bytes 294920 | tf_op jit(solution)/shard_map/ppermute | solution.py:430
  27.1 6.8 %collective-permute-start.14 = (f32[96,256]{1,0:T(8,128)S(1)}, f32[96,256]{1,0:T(8,128)S(1)}, u32[]{:S(2)}, u32[]{:S(2)}) collective-permute-start(f32[96,256]{1,0:T(8,128)S(1)} %get-tuple-element.22.refs_0_.refs_1_.refs_3_.refs_10_), channel_id=1, source_target_pairs={{0,1},{1,0},{2,3},{3,2},{4,5},{5,4},{6,7},{7,6},{8,9},{9,8},{10,11... | collective-permute-start | bytes 294920 | tf_op jit(solution)/shard_map/ppermute | solution.py:434
  30.2 5.2 %collective-permute-start.17 = (f32[96,256]{1,0:T(8,128)S(1)}, f32[96,256]{1,0:T(8,128)S(1)}, u32[]{:S(2)}, u32[]{:S(2)}) collective-permute-start(f32[96,256]{1,0:T(8,128)S(1)} %collective-permute-done.13.refs_6_.refs_13_), channel_id=1, source_target_pairs={{0,1},{1,0},{2,3},{3,2},{4,5},{5,4},{6,7},{7,6},{8,9},{9,8},{10,11... | collective-permute-start | bytes 294920 | tf_op jit(solution)/shard_map/ppermute | solution.py:434
  31.8 4.8 %collective-permute-start.16 = (f32[96,256]{1,0:T(8,128)S(1)}, f32[96,256]{1,0:T(8,128)S(1)}, u32[]{:S(2)}, u32[]{:S(2)}) collective-permute-start(f32[96,256]{1,0:T(8,128)S(1)} %collective-permute-done.12.refs_5_.refs_12_), channel_id=1, source_target_pairs={{0,1},{1,0},{2,3},{3,2},{4,5},{5,4},{6,7},{7,6},{8,9},{9,8},{10,11... | collective-permute-start | bytes 294920 | tf_op jit(solution)/shard_map/ppermute | solution.py:434
  32.4 6.3 %collective-permute-start.21 = (f32[96,256]{1,0:T(8,128)S(1)}, f32[96,256]{1,0:T(8,128)S(1)}, u32[]{:S(2)}, u32[]{:S(2)}) collective-permute-start(f32[96,256]{1,0:T(8,128)S(1)} %get-tuple-element.36), channel_id=1, source_target_pairs={{0,6},{2,4},{4,2},{6,0},{1,7},{3,5},{5,3},{7,1},{8,14},{10,12},{12... | collective-permute-start | bytes 294920 | tf_op jit(solution)/shard_map/ppermute | solution.py:441
  33.9 6.2 %collective-permute-start.20 = (f32[96,256]{1,0:T(8,128)S(1)}, f32[96,256]{1,0:T(8,128)S(1)}, u32[]{:S(2)}, u32[]{:S(2)}) collective-permute-start(f32[96,256]{1,0:T(8,128)S(1)} %get-tuple-element.37), channel_id=1, source_target_pairs={{0,4},{2,6},{4,0},{6,2},{1,5},{3,7},{5,1},{7,3},{8,12},{10,14},{12... | collective-permute-start | bytes 294920 | tf_op jit(solution)/shard_map/ppermute | solution.py:441
  42.1 6.3 %collective-permute-start.24 = (f32[96,256]{1,0:T(8,128)S(1)}, f32[96,256]{1,0:T(8,128)S(1)}, u32[]{:S(2)}, u32[]{:S(2)}) collective-permute-start(f32[96,256]{1,0:T(8,128)S(1)} %get-tuple-element.27.refs_18_), channel_id=1, source_target_pairs={{0,6},{2,4},{4,2},{6,0},{1,7},{3,5},{5,3},{7,1},{8,14},{10,12},{12... | collective-permute-start | bytes 294920 | tf_op jit(solution)/shard_map/ppermute | solution.py:430
  43.6 6.2 %collective-permute-start.23 = (f32[96,256]{1,0:T(8,128)S(1)}, f32[96,256]{1,0:T(8,128)S(1)}, u32[]{:S(2)}, u32[]{:S(2)}) collective-permute-start(f32[96,256]{1,0:T(8,128)S(1)} %get-tuple-element.27.refs_18_), channel_id=1, source_target_pairs={{0,4},{2,6},{4,0},{6,2},{1,5},{3,7},{5,1},{7,3},{8,12},{10,14},{12... | collective-permute-start | bytes 294920 | tf_op jit(solution)/shard_map/ppermute | solution.py:430
  45.6 17.0 %collective-permute-start.25 = (f32[96,256]{1,0:T(8,128)S(1)}, f32[96,256]{1,0:T(8,128)S(1)}, u32[]{:S(2)}, u32[]{:S(2)}) collective-permute-start(f32[96,256]{1,0:T(8,128)S(1)} %get-tuple-element.27.refs_18_), channel_id=1, source_target_pairs={{0,1},{1,0},{2,3},{3,2},{4,5},{5,4},{6,7},{7,6},{8,9},{9,8},{10,11... | collective-permute-start | bytes 294920 | tf_op jit(solution)/shard_map/ppermute | solution.py:434
  48.4 14.3 %collective-permute-start.28 = (f32[96,256]{1,0:T(8,128)S(1)}, f32[96,256]{1,0:T(8,128)S(1)}, u32[]{:S(2)}, u32[]{:S(2)}) collective-permute-start(f32[96,256]{1,0:T(8,128)S(1)} %collective-permute-done.24.refs_21_), channel_id=1, source_target_pairs={{0,1},{1,0},{2,3},{3,2},{4,5},{5,4},{6,7},{7,6},{8,9},{9,8},{10,11... | collective-permute-start | bytes 294920 | tf_op jit(solution)/shard_map/ppermute | solution.py:434
  49.9 12.8 %collective-permute-start.27 = (f32[96,256]{1,0:T(8,128)S(1)}, f32[96,256]{1,0:T(8,128)S(1)}, u32[]{:S(2)}, u32[]{:S(2)}) collective-permute-start(f32[96,256]{1,0:T(8,128)S(1)} %collective-permute-done.23.refs_20_), channel_id=1, source_target_pairs={{0,1},{1,0},{2,3},{3,2},{4,5},{5,4},{6,7},{7,6},{8,9},{9,8},{10,11... | collective-permute-start | bytes 294920 | tf_op jit(solution)/shard_map/ppermute | solution.py:434
  49.9 12.8 %collective-permute-start.26 = (f32[96,256]{1,0:T(8,128)S(1)}, f32[96,256]{1,0:T(8,128)S(1)}, u32[]{:S(2)}, u32[]{:S(2)}) collective-permute-start(f32[96,256]{1,0:T(8,128)S(1)} %collective-permute-done.22.refs_19_), channel_id=1, source_target_pairs={{0,1},{1,0},{2,3},{3,2},{4,5},{5,4},{6,7},{7,6},{8,9},{9,8},{10,11... | collective-permute-start | bytes 294920 | tf_op jit(solution)/shard_map/ppermute | solution.py:434
  (12 other events, 125.5 us)

commit v3 on v2

--- a/solution.py
+++ b/solution.py
@@ -217,13 +217,7 @@
 
 
 def diag_kernel(panel, diag, image):
-    image[...] = dot_full(panel[...], diag[...], NT)
-
-
-def diag_split_kernel(panel, diag, tiles, image, split_tiles):
-    diag_kernel(panel, diag, image)
-    for k in range(tiles.shape[0]):
-        split_tiles[0, k], split_tiles[1, k] = split(tiles[k])
+    image[...] = dot_full(panel[...], diag.all(), NT)
 
 
 def residual_kernel(
@@ -245,9 +239,13 @@
     contributions(way, cols, pairs, split(value), work, keep, send)
 
 
-def image_kernel(way, cols, panel, base, gathered, split_tiles, added, image, sums, held):
+def image_kernel(
+    way, cols, panel, base, gathered, split_tiles, added, image, half, sums, held
+):
     hold(gathered, held)
-    total = base[...] + off_diagonal(way, cols, held_pairs(split_tiles), held)
+    off = off_diagonal(way, cols, held_pairs(split_tiles), held)
+    half[...] = off + 0.5 * base[...]
+    total = off + base[...]
     for block in added:
         total = total + block[...]
     image[...] = total
@@ -268,71 +266,86 @@
     return norm, column_of(step), 1.0 + column_of(norm / rr)
 
 
+def newton_kernel(way, cols, gathered, diag, tiles, out, *more):
+    *split_tiles, held = more
+    rows = out.shape[0]
+    for k, block in enumerate(gathered):
+        value = block[...]
+        high, rest = split(value)
+        middle = value - high.astype(F32)
+        held[k, 0:rows], held[k, rows : 2 * rows] = high, rest
+        held[k, 2 * rows : 3 * rows] = (middle - rest.astype(F32)).astype(BF16)
+    held[len(gathered)] = jnp.zeros(held.shape[1:], BF16)
+    first = second = None
+    work = [(seat, tiles[k]) for k, seat in enumerate(seats(way, cols))]
+    for k, (seat, tile) in enumerate(work + [(0, None)]):
+        three = held[seat]
+        high, low = split(diag.all() * 0.5 if tile is None else tile)
+        if tile is not None and split_tiles:
+            split_tiles[0][0, k], split_tiles[0][1, k] = high, low
+        one = lax.dot_general(three, high, NT, preferred_element_type=F32)
+        two = lax.dot_general(three[: 2 * rows], low, NT, preferred_element_type=F32)
+        first = one if first is None else first + one
+        second = two if second is None else second + two
+    small = first[2 * rows :] + second[rows:]
+    out[...] = first[:rows] + (first[rows : 2 * rows] + second[:rows] + small)
+
+
+def half_product(both, pair):
+    rows = both.shape[0] // 2
+    one = lax.dot_general(both, pair[0], NT, preferred_element_type=F32)
+    two = lax.dot_general(both[:rows], pair[1], NT, preferred_element_type=F32)
+    return one[:rows] + (one[rows:] + two)
+
+
+def whole_pairs(tiles):
+    return [
+        functools.partial(lambda k: split(tiles[k]), k) for k in range(tiles.shape[0])
+    ]
+
+
+def halves_kernel(
+    way, cols, images, tiles, newton_tiles, diag, newton_diag, half, newton, held
+):
+    hold(images, held)
+    first = off_diagonal(way, cols, whole_pairs(tiles), held)
+    second = off_diagonal(way, cols, held_pairs(newton_tiles), held)
+    half[...] = first + half_product(held[0], split(diag.all() * 0.5))
+    newton[...] = second + half_product(held[0], split(newton_diag.all() * 0.5))
+
+
 def middle_kernel(
-    way,
     parts_rows,
     parts_cols,
-    cols,
     sums,
-    starts,
-    residuals,
-    images,
-    split_tiles,
-    newton_tiles,
-    diag,
-    newton_diag,
+    start,
+    residual,
+    image,
+    half_residual,
+    half_image,
+    newton_start,
+    newton_residual,
+    newton_image,
     x_out,
     d_out,
     norm_out,
     keep,
     send,
-    held,
     order,
     blocks,
     pieces,
 ):
     norm_out[...], step, grow = steps(sums)
     count = d_out.shape[0]
-    for k, image in enumerate(images):
-        r = residuals[k][...]
-        x = starts[k][...] + step * r
-        d = grow * r - step * image[...]
-        if k == 0:
-            x_out[...] = x
-            d_out[...] = d
-        held[k, 0:count], held[k, 3 * count : 4 * count] = split(x)
-        held[k, count : 2 * count], held[k, 2 * count : 3 * count] = split(d)
-    held[len(images)] = jnp.zeros(held.shape[1:], BF16)
-    x1, d1 = x_out[...], d_out[...]
-    found = seats(way, cols)
-
-    def product(rows, tile):
-        return lax.dot_general(rows, tile, NT, preferred_element_type=F32)
-
-    first = second = None
-    for seat, pair in zip(found, held_pairs(split_tiles)):
-        block, (high, low) = held[seat], pair()
-        one = product(block[count : 3 * count], high)
-        two = product(block[count : 2 * count], low)
-        first = one if first is None else first + one
-        second = two if second is None else second + two
-    own, (high, low) = held[0], split(diag[...] * 0.5)
-    first += product(own[count : 3 * count], high)
-    second += product(own[count : 2 * count], low)
-    half_d = first[:count] + (first[count:] + second)
+    r, q = residual[...], image[...]
+    x1 = start[...] + step * r
+    d1 = grow * r - step * q
+    x_out[...] = x1
+    d_out[...] = d1
+    half_d = grow * half_residual[...] - step * half_image[...]
     curvature = 2.0 * row_sums(d1 * half_d)
-    first = second = None
-    for seat, pair in zip(found, held_pairs(newton_tiles)):
-        block, (high, low) = held[seat], pair()
-        one = product(block, high)
-        two = product(block[: 2 * count], low)
-        first = one if first is None else first + one
-        second = two if second is None else second + two
-    high, low = split(newton_diag[...] * 0.5)
-    first += product(own, high)
-    second += product(own[: 2 * count], low)
-    ux = first[:count] + (first[3 * count :] + second[:count])
-    ud = first[count : 2 * count] + (first[2 * count : 3 * count] + second[count:])
+    ux = newton_start[...] + step * newton_residual[...]
+    ud = grow * newton_residual[...] - step * newton_image[...]
     hr, hc = count // parts_rows, count // parts_cols
     for r_index in range(parts_rows):
         for kind, pair in enumerate(((x1, ux), (d1, ud))):
@@ -453,7 +466,7 @@
     )
     added = scatter(keep, send)
     starts = forward(starts)
-    (base,) = call(diag_kernel, [panel], [], [start, diag], flops=2 * unit)
+    (base,) = call(diag_kernel, [panel], [], [start, Far(diag)], flops=2 * unit)
     residual, keep, send = call(
         functools.partial(residual_kernel, way),
         [panel, stack, stack],
@@ -465,16 +478,25 @@
     residuals = gather(residual)
     added = scatter(keep, send)
     residuals = forward(residuals)
-    base, newton_tiles = call(
-        diag_split_kernel,
-        [panel, parts],
-        [],
-        [residual, diag, ntiles],
-        flops=4 * unit,
-    )
-    image, sums = call(
+    (base,) = call(diag_kernel, [panel], [], [residual, Far(diag)], flops=2 * unit)
+
+    def newton_half(gathered, phase):
+        return call(
+            functools.partial(newton_kernel, way),
+            [panel, parts][: phase + 1],
+            [cols],
+            [gathered, Far(ndiag), ntiles],
+            scratch=[
+                jax.ShapeDtypeStruct((2 * chips + 1, 3 * count, size), BF16)
+            ],
+            flops=2 * n * unit,
+        )
+
+    (newton_start,) = newton_half(starts, 0)
+    newton_residual, newton_tiles = newton_half(residuals, 1)
+    image, half_residual, sums = call(
         functools.partial(image_kernel, way),
-        [panel, (groups * columns, 3, count)],
+        [panel, panel, (groups * columns, 3, count)],
         [cols],
         [residual, base, residuals, split_tiles, added],
         scratch=[held],
@@ -486,27 +508,35 @@
     hr, hc = count // groups, count // columns
     depth = -(-(hc + 1) // 8) * 8
     share = (groups * chips, depth, LANES)
+    half_image, newton_image = call(
+        functools.partial(halves_kernel, way),
+        [panel, panel],
+        [cols],
+        [images, tiles, newton_tiles, Far(diag), Far(ndiag)],
+        scratch=[held],
+        flops=2 * n * unit,
+    )
     x1, d1, norm, keep, send = call(
-        functools.partial(middle_kernel, way, groups, columns),
+        functools.partial(middle_kernel, groups, columns),
         [panel, panel, (1, count), share, share],
-        [cols],
+        [],
         [
             sums,
-            starts,
-            residuals,
-            images,
-            split_tiles,
-            newton_tiles,
-            diag,
-            ndiag,
+            start,
+            residual,
+            image,
+            half_residual,
+            half_image,
+            newton_start,
+            newton_residual,
+            newton_image,
         ],
         scratch=[
-            jax.ShapeDtypeStruct((2 * chips + 1, 4 * count, size), BF16),
             (2, groups * HALF, size),
             (2 * count, groups * HALF),
             (groups, count + depth, LANES),
         ],
-        flops=4 * n * unit,
+        flops=n * unit,
     )
     received = lax.ppermute(send, "core", swap)
     received = lax.all_to_all(keep + received, ("row", "chip"), 0, 0, tiled=True)

time: 80.6 us -> 83.7 us (1.038)
  blocking collectives: 22.9 us -> 13.8 us
  Pallas kernels: 13.1 us -> 20.2 us
  starting transfers between devices: 20.5 us -> 25.7 us
  waiting for transfers between devices: 22.9 us -> 21.9 us
    all_to_all x1 -> x0, blocking collectives: 12.3 us -> none  [on_device(): sums = lax.all_to_all(sums, ALL, 0, 0, tiled=True)]
    pallas_call x7 -> x10, Pallas kernels: 13.1 us -> 20.2 us  [call(): pl.pallas_call(kernel, out_shape=outs, in_specs=specs, out_specs=[vmem] *...]
    all_to_all x0 -> x1, starting transfers between devices: none -> 5.21 us  [on_device(): sums = lax.all_to_all(sums, ALL, 0, 0, tiled=True)]
    all_to_all x1, blocking collectives: 10.6 us -> 13.8 us  [on_device(): lax.all_to_all(keep + received, ('row', 'chip'), 0, 0, tiled=True)]
    ppermute x6, waiting for transfers between devices: 7.66 us -> 5.99 us  [scatter(): added.append(lax.ppermute(sums[k], 'chip', way.pairs(k)))]
  transfers between devices with their start and end apart: 30 -> 31, of which waited for: 12 -> 13; matrix products, arithmetic and copies ran while one was open for 0% -> 0% of each run, Pallas kernels for 1% -> 13%
where the time goes in v3:
time: 83.7 us; the launch traced here: 83.2 us
  starting transfers between devices  25.7 us (31%)
  waiting for transfers between devices  21.9 us (26%)
  Pallas kernels  20.2 us (24%)
  blocking collectives  13.8 us (16%)
  between operations  0.9 us (1%)
    pallas_call x10, Pallas kernels, call(): pl.pallas_call(kernel, out_shape=outs, in_specs=specs, out_specs=[vmem] *...  20.2 us
    ppermute x9, waiting for transfers between devices, gather(): same[way.source(k)] = lax.ppermute(value, 'chip', way.pairs(k))  13.9 us
    all_to_all x1, blocking collectives, on_device(): lax.all_to_all(keep + received, ('row', 'chip'), 0, 0, tiled=True)  13.8 us
    ppermute x9, starting transfers between devices, gather(): same[way.source(k)] = lax.ppermute(value, 'chip', way.pairs(k))  11.3 us
    ppermute x6, starting transfers between devices, scatter(): added.append(lax.ppermute(sums[k], 'chip', way.pairs(k)))  7.11 us
    ppermute x6, waiting for transfers between devices, scatter(): added.append(lax.ppermute(sums[k], 'chip', way.pairs(k)))  5.99 us
    all_to_all x1, starting transfers between devices, on_device(): sums = lax.all_to_all(sums, ALL, 0, 0, tiled=True)  5.21 us
  transfers between devices with their start and end apart: 31, of which 13 were waited for; matrix products, arithmetic and copies ran while one was open for 0% of the time, Pallas kernels for 13%

profile of v3, /device:TPU:0, one launch (start us, length us, event | category | flops | bytes accessed | tf_op | source)
XLA Modules:
  0.0 83.2 jit_solution(18180732647910235063)
XLA Ops:
  0.7 2.3 %shard_map.87 = (f32[4,96,256]{2,1,0:T(8,128)S(1)}, f32[4,96,256]{2,1,0:T(8,128)S(1)}, bf16[2,7,256,256]{3,2,1,0:T(8,128)(2,1)S(1)}) custom-call(s32[7]{0:T(128)} %bitcast.38, f32[96,256]{1,0:T(8,128)} %bitcast.29, f32[7,256,256]{2,1,0:T(8,128)} %bitcast.27), custom_call_target="tpu_custom_call" | custom-call | flops 264241152 | bytes 1933340 | tf_op jit(solution)/shard_map/pallas_call | solution.py:121
  3.6 3.5 %collective-permute-start.2 = (f32[96,256]{1,0:T(8,128)S(1)}, f32[96,256]{1,0:T(8,128)S(1)}, u32[]{:S(2)}, u32[]{:S(2)}) collective-permute-start(f32[96,256]{1,0:T(8,128)S(1)} %bitcast.30), channel_id=1, source_target_pairs={{0,6},{2,4},{4,2},{6,0},{1,7},{3,5},{5,3},{7,1},{8,14},{10,12},{12... | collective-permute-start | bytes 294920 | tf_op jit(solution)/shard_map/ppermute | solution.py:443
  7.7 2.8 %collective-permute-done.2.refs_6_.refs_4_ = f32[96,256]{1,0:T(8,128)S(1)} collective-permute-done((f32[96,256]{1,0:T(8,128)S(1)}, f32[96,256]{1,0:T(8,128)S(1)}, u32[]{:S(2)}, u32[]{:S(2)}) %collective-permute-start.2) | collective-permute-done | bytes 98336 | tf_op jit(solution)/shard_map/ppermute | solution.py:443
  10.5 2.0 %collective-permute-done.1.refs_5_.refs_3_ = f32[96,256]{1,0:T(8,128)S(1)} collective-permute-done((f32[96,256]{1,0:T(8,128)S(1)}, f32[96,256]{1,0:T(8,128)S(1)}, u32[]{:S(2)}, u32[]{:S(2)}) %collective-permute-start.1) | collective-permute-done | bytes 98336 | tf_op jit(solution)/shard_map/ppermute | solution.py:443
  13.1 1.8 %collective-permute-start.10 = (f32[96,256]{1,0:T(8,128)S(1)}, f32[96,256]{1,0:T(8,128)S(1)}, u32[]{:S(2)}, u32[]{:S(2)}) collective-permute-start(f32[96,256]{1,0:T(8,128)S(1)} %get-tuple-element.46), channel_id=1, source_target_pairs={{0,6},{2,4},{4,2},{6,0},{1,7},{3,5},{5,3},{7,1},{8,14},{10,12},{12... | collective-permute-start | bytes 294920 | tf_op jit(solution)/shard_map/ppermute | solution.py:454
  18.1 1.6 %collective-permute-done.10.refs_15_ = f32[96,256]{1,0:T(8,128)S(1)} collective-permute-done((f32[96,256]{1,0:T(8,128)S(1)}, f32[96,256]{1,0:T(8,128)S(1)}, u32[]{:S(2)}, u32[]{:S(2)}) %collective-permute-start.10) | collective-permute-done | bytes 98336 | tf_op jit(solution)/shard_map/ppermute | solution.py:454
  19.6 1.5 %collective-permute-done.9.refs_14_ = f32[96,256]{1,0:T(8,128)S(1)} collective-permute-done((f32[96,256]{1,0:T(8,128)S(1)}, f32[96,256]{1,0:T(8,128)S(1)}, u32[]{:S(2)}, u32[]{:S(2)}) %collective-permute-start.9) | collective-permute-done | bytes 98336 | tf_op jit(solution)/shard_map/ppermute | solution.py:454
  21.2 2.3 %shard_map.88 = (f32[96,256]{1,0:T(8,128)S(1)}, f32[4,96,256]{2,1,0:T(8,128)S(1)}, f32[4,96,256]{2,1,0:T(8,128)S(1)}) custom-call(s32[7]{0:T(128)S(1)} %bitcast.39, f32[96,256]{1,0:T(8,128)S(1)} %shard_map.86.refs_1_, s32[1,96]{1,0:T(1,128)S(1)} %bitcast.44, f32[96,256]{1,0:T(8,128)S(1)} %bitcast.35, f32[96,256]{1,0:T(8,128)S(1)} %collective-permute-done.refs_4_.refs_2_, ...), custom_call_target="tpu_custom_call" | custom-call | flops 528482304 | bytes 3113344 | tf_op jit(solution)/shard_map/pallas_call | solution.py:121
  23.6 1.6 %collective-permute-start.13 = (f32[96,256]{1,0:T(8,128)S(1)}, f32[96,256]{1,0:T(8,128)S(1)}, u32[]{:S(2)}, u32[]{:S(2)}) collective-permute-start(f32[96,256]{1,0:T(8,128)S(1)} %get-tuple-element.25.refs_0_.refs_1_.refs_3_.refs_2_), channel_id=1, source_target_pairs={{0,6},{2,4},{4,2},{6,0},{1,7},{3,5},{5,3},{7,1},{8,14},{10,12},{12... | collective-permute-start | bytes 294920 | tf_op jit(solution)/shard_map/ppermute | solution.py:443
  27.1 3.1 %collective-permute-done.13.refs_6_.refs_4_ = f32[96,256]{1,0:T(8,128)S(1)} collective-permute-done((f32[96,256]{1,0:T(8,128)S(1)}, f32[96,256]{1,0:T(8,128)S(1)}, u32[]{:S(2)}, u32[]{:S(2)}) %collective-permute-start.13) | collective-permute-done | bytes 98336 | tf_op jit(solution)/shard_map/ppermute | solution.py:443
  30.2 1.6 %collective-permute-done.12.refs_5_.refs_3_ = f32[96,256]{1,0:T(8,128)S(1)} collective-permute-done((f32[96,256]{1,0:T(8,128)S(1)}, f32[96,256]{1,0:T(8,128)S(1)}, u32[]{:S(2)}, u32[]{:S(2)}) %collective-permute-start.12) | collective-permute-done | bytes 98336 | tf_op jit(solution)/shard_map/ppermute | solution.py:443
  32.3 1.6 %collective-permute-start.21 = (f32[96,256]{1,0:T(8,128)S(1)}, f32[96,256]{1,0:T(8,128)S(1)}, u32[]{:S(2)}, u32[]{:S(2)}) collective-permute-start(f32[96,256]{1,0:T(8,128)S(1)} %get-tuple-element.42), channel_id=1, source_target_pairs={{0,6},{2,4},{4,2},{6,0},{1,7},{3,5},{5,3},{7,1},{8,14},{10,12},{12... | collective-permute-start | bytes 294920 | tf_op jit(solution)/shard_map/ppermute | solution.py:454
  33.9 1.5 %collective-permute-start.20 = (f32[96,256]{1,0:T(8,128)S(1)}, f32[96,256]{1,0:T(8,128)S(1)}, u32[]{:S(2)}, u32[]{:S(2)}) collective-permute-start(f32[96,256]{1,0:T(8,128)S(1)} %get-tuple-element.43), channel_id=1, source_target_pairs={{0,4},{2,6},{4,0},{6,2},{1,5},{3,7},{5,1},{7,3},{8,12},{10,14},{12... | collective-permute-start | bytes 294920 | tf_op jit(solution)/shard_map/ppermute | solution.py:454
  38.6 1.5 %collective-permute-done.20.refs_14_ = f32[96,256]{1,0:T(8,128)S(1)} collective-permute-done((f32[96,256]{1,0:T(8,128)S(1)}, f32[96,256]{1,0:T(8,128)S(1)}, u32[]{:S(2)}, u32[]{:S(2)}) %collective-permute-start.20) | collective-permute-done | bytes 98336 | tf_op jit(solution)/shard_map/ppermute | solution.py:454
  40.2 1.9 %shard_map.90 = (f32[96,256]{1,0:T(8,128)S(1)}, f32[96,256]{1,0:T(8,128)S(1)}, f32[32,3,96]{2,1,0:T(4,128)S(1)}) custom-call(s32[7]{0:T(128)S(1)} %bitcast.40, f32[96,256]{1,0:T(8,128)S(1)} %get-tuple-element.25.refs_0_.refs_1_.refs_3_.refs_2_, f32[96,256]{1,0:T(8,128)S(1)} %shard_map.89.refs_2_, ...), custom_call_target="tpu_custom_call" | custom-call | flops 264241152 | bytes 3211264 | tf_op jit(solution)/shard_map/pallas_call | solution.py:121
  42.1 1.6 %collective-permute-start.24 = (f32[96,256]{1,0:T(8,128)S(1)}, f32[96,256]{1,0:T(8,128)S(1)}, u32[]{:S(2)}, u32[]{:S(2)}) collective-permute-start(f32[96,256]{1,0:T(8,128)S(1)} %get-tuple-element.29.refs_1_.refs_3_), channel_id=1, source_target_pairs={{0,6},{2,4},{4,2},{6,0},{1,7},{3,5},{5,3},{7,1},{8,14},{10,12},{12... | collective-permute-start | bytes 294920 | tf_op jit(solution)/shard_map/ppermute | solution.py:443
  45.6 2.7 %collective-permute-done.24.refs_4_ = f32[96,256]{1,0:T(8,128)S(1)} collective-permute-done((f32[96,256]{1,0:T(8,128)S(1)}, f32[96,256]{1,0:T(8,128)S(1)}, u32[]{:S(2)}, u32[]{:S(2)}) %collective-permute-start.24) | collective-permute-done | bytes 98336 | tf_op jit(solution)/shard_map/ppermute | solution.py:443
  48.3 1.5 %collective-permute-done.23.refs_3_ = f32[96,256]{1,0:T(8,128)S(1)} collective-permute-done((f32[96,256]{1,0:T(8,128)S(1)}, f32[96,256]{1,0:T(8,128)S(1)}, u32[]{:S(2)}, u32[]{:S(2)}) %collective-permute-start.23) | collective-permute-done | bytes 98336 | tf_op jit(solution)/shard_map/ppermute | solution.py:443
  50.4 2.5 %shard_map.93.refs_6_ = f32[96,256]{1,0:T(8,128)S(1)} custom-call(s32[7]{0:T(128)S(1)} %bitcast.41, f32[96,256]{1,0:T(8,128)S(1)} %bitcast.36, f32[96,256]{1,0:T(8,128)S(1)} %collective-permute-done.refs_4_.refs_2_, f32[96,256]{1,0:T(8,128)S(1)} %collective-permute-done.1.refs_5_.refs_3_, f32[96,256]{1,0:T(8,128)S(1)} %collective-permute-done.2.refs_6_.refs_4_, ...), custom_call_target="tpu_custom_call" | custom-call | flops 528482304 | bytes 2883584 | tf_op jit(solution)/shard_map/pallas_call | solution.py:121
  52.8 5.2 %all-to-all-start = ((f32[32,3,96]{2,1,0:T(4,128)}), f32[32,3,96]{2,1,0:T(4,128)}, u32[]{:S(2)}, u32[]{:S(2)}) async-start(f32[32,3,96]{2,1,0:T(4,128)} %copy-done.3), calls=%async_computation | async-start | bytes 131072 | tf_op jit(solution)/shard_map/all_to_all | solution.py:506
  58.1 2.5 %shard_map.91 = (f32[96,256]{1,0:T(8,128)S(1)}, bf16[2,7,256,256]{3,2,1,0:T(8,128)(2,1)S(1)}) custom-call(s32[7]{0:T(128)S(1)} %bitcast.42, f32[96,256]{1,0:T(8,128)S(1)} %get-tuple-element.25.refs_0_.refs_1_.refs_3_.refs_2_, f32[96,256]{1,0:T(8,128)S(1)} %collective-permute-done.11.refs_4_.refs_2_, f32[96,256]{1,0:T(8,128)S(1)} %collective-permute-done.12.refs_5_.refs_3_, ...), custom_call_target="tpu_custom_call" | custom-call | flops 528482304 | bytes 2883584 | tf_op jit(solution)/shard_map/pallas_call | solution.py:121
  61.3 3.5 %shard_map.92 = (f32[96,256]{1,0:T(8,128)S(1)}, f32[96,256]{1,0:T(8,128)S(1)}) custom-call(s32[7]{0:T(128)S(1)} %bitcast.43, f32[96,256]{1,0:T(8,128)S(1)} %get-tuple-element.29.refs_1_.refs_3_, f32[96,256]{1,0:T(8,128)S(1)} %collective-permute-done.22.refs_2_, f32[96,256]{1,0:T(8,128)S(1)} %collective-permute-done.23.refs_3_, ...), custom_call_target="tpu_custom_call" | custom-call | flops 528482304 | bytes 4980736 | tf_op jit(solution)/shard_map/pallas_call | solution.py:121
  65.5 1.7 %shard_map.94 = (f32[96,256]{1,0:T(8,128)S(1)}, f32[96,256]{1,0:T(8,128)S(1)}, f32[1,96]{1,0:T(1,128)S(1)}, f32[16,16,128]{2,1,0:T(8,128)S(1)}, f32[16,16,128]{2,1,0:T(8,128)S(1)}) custom-call(f32[32,3,96]{2,1,0:T(4,128)} %all-to-all-done.refs_0_, f32[96,256]{1,0:T(8,128)S(1)} %bitcast.37, f32[96,256]{1,0:T(8,128)S(1)} %get-tuple-element.25.refs_0_.refs_1_.refs_3_.refs_2_, ...), custom_call_target="tpu_custom_call" | custom-call | flops 264241152 | bytes 823296 | tf_op jit(solution)/shard_map/pallas_call | solution.py:121
  68.6 13.8 %all_to_all.10.refs_0_ = f32[16,16,128]{2,1,0:T(8,128)S(1)} all-to-all(f32[16,16,128]{2,1,0:T(8,128)S(1)} %add.65), channel_id=1, replica_groups=mesh['row'=4,'chip'=4,'core'=2] {'row','chip'}, dimensions={0} | all-to-all | bytes 262144 | tf_op jit(solution)/shard_map/all_to_all | solution.py:542
  (72 shorter events, 16.9 us)
Async XLA Ops:
  3.0 10.1 %collective-permute-start.7 = (f32[4,96,256]{2,1,0:T(8,128)S(1)}, f32[4,96,256]{2,1,0:T(8,128)S(1)}, u32[]{:S(2)}, u32[]{:S(2)}) collective-permute-start(f32[4,96,256]{2,1,0:T(8,128)S(1)} %get-tuple-element.24), channel_id=1, source_target_pairs={{0,1},{1,0},{2,3},{3,2},{4,5},{5,4},{6,7},{7,6},{8,9},{9,8},{10,11... | collective-permute-start | bytes 1179656 | tf_op jit(solution)/shard_map/ppermute | solution.py:450
  3.6 7.0 %collective-permute-start.2 = (f32[96,256]{1,0:T(8,128)S(1)}, f32[96,256]{1,0:T(8,128)S(1)}, u32[]{:S(2)}, u32[]{:S(2)}) collective-permute-start(f32[96,256]{1,0:T(8,128)S(1)} %bitcast.30), channel_id=1, source_target_pairs={{0,6},{2,4},{4,2},{6,0},{1,7},{3,5},{5,3},{7,1},{8,14},{10,12},{12... | collective-permute-start | bytes 294920 | tf_op jit(solution)/shard_map/ppermute | solution.py:443
  7.1 5.5 %collective-permute-start.1 = (f32[96,256]{1,0:T(8,128)S(1)}, f32[96,256]{1,0:T(8,128)S(1)}, u32[]{:S(2)}, u32[]{:S(2)}) collective-permute-start(f32[96,256]{1,0:T(8,128)S(1)} %bitcast.31), channel_id=1, source_target_pairs={{0,4},{2,6},{4,0},{6,2},{1,5},{3,7},{5,1},{7,3},{8,12},{10,14},{12... | collective-permute-start | bytes 294920 | tf_op jit(solution)/shard_map/ppermute | solution.py:443
  7.7 7.2 %collective-permute-start.3 = (f32[96,256]{1,0:T(8,128)S(1)}, f32[96,256]{1,0:T(8,128)S(1)}, u32[]{:S(2)}, u32[]{:S(2)}) collective-permute-start(f32[96,256]{1,0:T(8,128)S(1)} %bitcast.33), channel_id=1, source_target_pairs={{0,1},{1,0},{2,3},{3,2},{4,5},{5,4},{6,7},{7,6},{8,9},{9,8},{10,11... | collective-permute-start | bytes 294920 | tf_op jit(solution)/shard_map/ppermute | solution.py:447
  10.5 5.8 %collective-permute-start.6 = (f32[96,256]{1,0:T(8,128)S(1)}, f32[96,256]{1,0:T(8,128)S(1)}, u32[]{:S(2)}, u32[]{:S(2)}) collective-permute-start(f32[96,256]{1,0:T(8,128)S(1)} %collective-permute-done.2.refs_6_.refs_4_), channel_id=1, source_target_pairs={{0,1},{1,0},{2,3},{3,2},{4,5},{5,4},{6,7},{7,6},{8,9},{9,8},{10,11... | collective-permute-start | bytes 294920 | tf_op jit(solution)/shard_map/ppermute | solution.py:447
  12.6 5.5 %collective-permute-start.5 = (f32[96,256]{1,0:T(8,128)S(1)}, f32[96,256]{1,0:T(8,128)S(1)}, u32[]{:S(2)}, u32[]{:S(2)}) collective-permute-start(f32[96,256]{1,0:T(8,128)S(1)} %collective-permute-done.1.refs_5_.refs_3_), channel_id=1, source_target_pairs={{0,1},{1,0},{2,3},{3,2},{4,5},{5,4},{6,7},{7,6},{8,9},{9,8},{10,11... | collective-permute-start | bytes 294920 | tf_op jit(solution)/shard_map/ppermute | solution.py:447
  12.8 5.2 %collective-permute-start.4 = (f32[96,256]{1,0:T(8,128)S(1)}, f32[96,256]{1,0:T(8,128)S(1)}, u32[]{:S(2)}, u32[]{:S(2)}) collective-permute-start(f32[96,256]{1,0:T(8,128)S(1)} %collective-permute-done.refs_4_.refs_2_), channel_id=1, source_target_pairs={{0,1},{1,0},{2,3},{3,2},{4,5},{5,4},{6,7},{7,6},{8,9},{9,8},{10,11... | collective-permute-start | bytes 294920 | tf_op jit(solution)/shard_map/ppermute | solution.py:447
  13.1 6.5 %collective-permute-start.10 = (f32[96,256]{1,0:T(8,128)S(1)}, f32[96,256]{1,0:T(8,128)S(1)}, u32[]{:S(2)}, u32[]{:S(2)}) collective-permute-start(f32[96,256]{1,0:T(8,128)S(1)} %get-tuple-element.46), channel_id=1, source_target_pairs={{0,6},{2,4},{4,2},{6,0},{1,7},{3,5},{5,3},{7,1},{8,14},{10,12},{12... | collective-permute-start | bytes 294920 | tf_op jit(solution)/shard_map/ppermute | solution.py:454
  15.0 6.2 %collective-permute-start.9 = (f32[96,256]{1,0:T(8,128)S(1)}, f32[96,256]{1,0:T(8,128)S(1)}, u32[]{:S(2)}, u32[]{:S(2)}) collective-permute-start(f32[96,256]{1,0:T(8,128)S(1)} %get-tuple-element.47), channel_id=1, source_target_pairs={{0,4},{2,6},{4,0},{6,2},{1,5},{3,7},{5,1},{7,3},{8,12},{10,14},{12... | collective-permute-start | bytes 294920 | tf_op jit(solution)/shard_map/ppermute | solution.py:454
  23.5 8.8 %collective-permute-start.18 = (f32[4,96,256]{2,1,0:T(8,128)S(1)}, f32[4,96,256]{2,1,0:T(8,128)S(1)}, u32[]{:S(2)}, u32[]{:S(2)}) collective-permute-start(f32[4,96,256]{2,1,0:T(8,128)S(1)} %get-tuple-element.27), channel_id=1, source_target_pairs={{0,1},{1,0},{2,3},{3,2},{4,5},{5,4},{6,7},{7,6},{8,9},{9,8},{10,11... | collective-permute-start | bytes 1179656 | tf_op jit(solution)/shard_map/ppermute | solution.py:450
  23.6 6.6 %collective-permute-start.13 = (f32[96,256]{1,0:T(8,128)S(1)}, f32[96,256]{1,0:T(8,128)S(1)}, u32[]{:S(2)}, u32[]{:S(2)}) collective-permute-start(f32[96,256]{1,0:T(8,128)S(1)} %get-tuple-element.25.refs_0_.refs_1_.refs_3_.refs_2_), channel_id=1, source_target_pairs={{0,6},{2,4},{4,2},{6,0},{1,7},{3,5},{5,3},{7,1},{8,14},{10,12},{12... | collective-permute-start | bytes 294920 | tf_op jit(solution)/shard_map/ppermute | solution.py:443
  25.1 6.6 %collective-permute-start.12 = (f32[96,256]{1,0:T(8,128)S(1)}, f32[96,256]{1,0:T(8,128)S(1)}, u32[]{:S(2)}, u32[]{:S(2)}) collective-permute-start(f32[96,256]{1,0:T(8,128)S(1)} %get-tuple-element.25.refs_0_.refs_1_.refs_3_.refs_2_), channel_id=1, source_target_pairs={{0,4},{2,6},{4,0},{6,2},{1,5},{3,7},{5,1},{7,3},{8,12},{10,14},{12... | collective-permute-start | bytes 294920 | tf_op jit(solution)/shard_map/ppermute | solution.py:443
  27.1 6.8 %collective-permute-start.14 = (f32[96,256]{1,0:T(8,128)S(1)}, f32[96,256]{1,0:T(8,128)S(1)}, u32[]{:S(2)}, u32[]{:S(2)}) collective-permute-start(f32[96,256]{1,0:T(8,128)S(1)} %get-tuple-element.25.refs_0_.refs_1_.refs_3_.refs_2_), channel_id=1, source_target_pairs={{0,1},{1,0},{2,3},{3,2},{4,5},{5,4},{6,7},{7,6},{8,9},{9,8},{10,11... | collective-permute-start | bytes 294920 | tf_op jit(solution)/shard_map/ppermute | solution.py:447
  31.8 5.5 %collective-permute-start.16 = (f32[96,256]{1,0:T(8,128)S(1)}, f32[96,256]{1,0:T(8,128)S(1)}, u32[]{:S(2)}, u32[]{:S(2)}) collective-permute-start(f32[96,256]{1,0:T(8,128)S(1)} %collective-permute-done.12.refs_5_.refs_3_), channel_id=1, source_target_pairs={{0,1},{1,0},{2,3},{3,2},{4,5},{5,4},{6,7},{7,6},{8,9},{9,8},{10,11... | collective-permute-start | bytes 294920 | tf_op jit(solution)/shard_map/ppermute | solution.py:447
  31.8 5.5 %collective-permute-start.15 = (f32[96,256]{1,0:T(8,128)S(1)}, f32[96,256]{1,0:T(8,128)S(1)}, u32[]{:S(2)}, u32[]{:S(2)}) collective-permute-start(f32[96,256]{1,0:T(8,128)S(1)} %collective-permute-done.11.refs_4_.refs_2_), channel_id=1, source_target_pairs={{0,1},{1,0},{2,3},{3,2},{4,5},{5,4},{6,7},{7,6},{8,9},{9,8},{10,11... | collective-permute-start | bytes 294920 | tf_op jit(solution)/shard_map/ppermute | solution.py:447
  32.3 6.3 %collective-permute-start.21 = (f32[96,256]{1,0:T(8,128)S(1)}, f32[96,256]{1,0:T(8,128)S(1)}, u32[]{:S(2)}, u32[]{:S(2)}) collective-permute-start(f32[96,256]{1,0:T(8,128)S(1)} %get-tuple-element.42), channel_id=1, source_target_pairs={{0,6},{2,4},{4,2},{6,0},{1,7},{3,5},{5,3},{7,1},{8,14},{10,12},{12... | collective-permute-start | bytes 294920 | tf_op jit(solution)/shard_map/ppermute | solution.py:454
  33.9 6.2 %collective-permute-start.20 = (f32[96,256]{1,0:T(8,128)S(1)}, f32[96,256]{1,0:T(8,128)S(1)}, u32[]{:S(2)}, u32[]{:S(2)}) collective-permute-start(f32[96,256]{1,0:T(8,128)S(1)} %get-tuple-element.43), channel_id=1, source_target_pairs={{0,4},{2,6},{4,0},{6,2},{1,5},{3,7},{5,1},{7,3},{8,12},{10,14},{12... | collective-permute-start | bytes 294920 | tf_op jit(solution)/shard_map/ppermute | solution.py:454
  42.1 6.3 %collective-permute-start.24 = (f32[96,256]{1,0:T(8,128)S(1)}, f32[96,256]{1,0:T(8,128)S(1)}, u32[]{:S(2)}, u32[]{:S(2)}) collective-permute-start(f32[96,256]{1,0:T(8,128)S(1)} %get-tuple-element.29.refs_1_.refs_3_), channel_id=1, source_target_pairs={{0,6},{2,4},{4,2},{6,0},{1,7},{3,5},{5,3},{7,1},{8,14},{10,12},{12... | collective-permute-start | bytes 294920 | tf_op jit(solution)/shard_map/ppermute | solution.py:443
  43.6 6.2 %collective-permute-start.23 = (f32[96,256]{1,0:T(8,128)S(1)}, f32[96,256]{1,0:T(8,128)S(1)}, u32[]{:S(2)}, u32[]{:S(2)}) collective-permute-start(f32[96,256]{1,0:T(8,128)S(1)} %get-tuple-element.29.refs_1_.refs_3_), channel_id=1, source_target_pairs={{0,4},{2,6},{4,0},{6,2},{1,5},{3,7},{5,1},{7,3},{8,12},{10,14},{12... | collective-permute-start | bytes 294920 | tf_op jit(solution)/shard_map/ppermute | solution.py:443
  45.6 15.7 %collective-permute-start.25 = (f32[96,256]{1,0:T(8,128)S(1)}, f32[96,256]{1,0:T(8,128)S(1)}, u32[]{:S(2)}, u32[]{:S(2)}) collective-permute-start(f32[96,256]{1,0:T(8,128)S(1)} %get-tuple-element.29.refs_1_.refs_3_), channel_id=1, source_target_pairs={{0,1},{1,0},{2,3},{3,2},{4,5},{5,4},{6,7},{7,6},{8,9},{9,8},{10,11... | collective-permute-start | bytes 294920 | tf_op jit(solution)/shard_map/ppermute | solution.py:447
  48.3 12.9 %collective-permute-start.28 = (f32[96,256]{1,0:T(8,128)S(1)}, f32[96,256]{1,0:T(8,128)S(1)}, u32[]{:S(2)}, u32[]{:S(2)}) collective-permute-start(f32[96,256]{1,0:T(8,128)S(1)} %collective-permute-done.24.refs_4_), channel_id=1, source_target_pairs={{0,1},{1,0},{2,3},{3,2},{4,5},{5,4},{6,7},{7,6},{8,9},{9,8},{10,11... | collective-permute-start | bytes 294920 | tf_op jit(solution)/shard_map/ppermute | solution.py:447
  49.8 11.4 %collective-permute-start.27 = (f32[96,256]{1,0:T(8,128)S(1)}, f32[96,256]{1,0:T(8,128)S(1)}, u32[]{:S(2)}, u32[]{:S(2)}) collective-permute-start(f32[96,256]{1,0:T(8,128)S(1)} %collective-permute-done.23.refs_3_), channel_id=1, source_target_pairs={{0,1},{1,0},{2,3},{3,2},{4,5},{5,4},{6,7},{7,6},{8,9},{9,8},{10,11... | collective-permute-start | bytes 294920 | tf_op jit(solution)/shard_map/ppermute | solution.py:447
  49.9 11.4 %collective-permute-start.26 = (f32[96,256]{1,0:T(8,128)S(1)}, f32[96,256]{1,0:T(8,128)}, u32[]{:S(2)}, u32[]{:S(2)}) collective-permute-start(f32[96,256]{1,0:T(8,128)S(1)} %collective-permute-done.22.refs_2_), channel_id=1, source_target_pairs={{0,1},{1,0},{2,3},{3,2},{4,5},{5,4},{6,7},{7,6},{8,9},{9,8},{10,11... | collective-permute-start | bytes 294920 | tf_op jit(solution)/shard_map/ppermute | solution.py:447
  52.8 12.6 %all-to-all-start = ((f32[32,3,96]{2,1,0:T(4,128)}), f32[32,3,96]{2,1,0:T(4,128)}, u32[]{:S(2)}, u32[]{:S(2)}) async-start(f32[32,3,96]{2,1,0:T(4,128)} %copy-done.3), calls=%async_computation | async-start | bytes 131072 | tf_op jit(solution)/shard_map/all_to_all | solution.py:506
  (17 other events, 124.2 us)

commit v4 on v3

--- a/solution.py
+++ b/solution.py
@@ -217,15 +217,18 @@
 
 
 def diag_kernel(panel, diag, image):
-    image[...] = dot_full(panel[...], diag.all(), NT)
+    image[...] = dot_full(panel[...], diag[...], NT)
+
+
+def off_kernel(way, cols, gathered, split_tiles, out, held):
+    hold(gathered, held)
+    out[...] = off_diagonal(way, cols, held_pairs(split_tiles), held)
 
 
 def residual_kernel(
-    way, cols, base, target, gathered, split_tiles, added, residual, keep, send, work, held
+    way, cols, base, off, target, split_tiles, added, residual, keep, send, work
 ):
-    pairs = held_pairs(split_tiles)
-    hold(gathered, held)
-    total = base[...] + off_diagonal(way, cols, pairs, held)
+    total = base[...] + off[...]
     for block in added:
         total = total + block[...]
     rows, size = residual.shape
@@ -236,16 +239,12 @@
     unit = at == lax.broadcasted_iota(jnp.int32, (rows, size), 1).astype(F32)
     value = unit.astype(F32) - total
     residual[...] = value
-    contributions(way, cols, pairs, split(value), work, keep, send)
-
-
-def image_kernel(
-    way, cols, panel, base, gathered, split_tiles, added, image, half, sums, held
-):
-    hold(gathered, held)
-    off = off_diagonal(way, cols, held_pairs(split_tiles), held)
-    half[...] = off + 0.5 * base[...]
-    total = off + base[...]
+    contributions(way, cols, held_pairs(split_tiles), split(value), work, keep, send)
+
+
+def image_kernel(panel, base, off, added, image, half, sums):
+    half[...] = off[...] + 0.5 * base[...]
+    total = off[...] + base[...]
     for block in added:
         total = total + block[...]
     image[...] = total
@@ -466,19 +465,30 @@
     )
     added = scatter(keep, send)
     starts = forward(starts)
-    (base,) = call(diag_kernel, [panel], [], [start, Far(diag)], flops=2 * unit)
+    (base,) = call(diag_kernel, [panel], [], [start, diag], flops=2 * unit)
+
+    def off_half(gathered):
+        return call(
+            functools.partial(off_kernel, way),
+            [panel],
+            [cols],
+            [gathered, split_tiles],
+            scratch=[held],
+            flops=n * unit,
+        )[0]
+
     residual, keep, send = call(
         functools.partial(residual_kernel, way),
         [panel, stack, stack],
         [cols],
-        [base, target, starts, split_tiles, added],
-        scratch=[work, held],
-        flops=2 * n * unit,
+        [base, off_half(starts), target, split_tiles, added],
+        scratch=[work],
+        flops=n * unit,
     )
     residuals = gather(residual)
     added = scatter(keep, send)
     residuals = forward(residuals)
-    (base,) = call(diag_kernel, [panel], [], [residual, Far(diag)], flops=2 * unit)
+    (base,) = call(diag_kernel, [panel], [], [residual, diag], flops=2 * unit)
 
     def newton_half(gathered, phase):
         return call(
@@ -495,12 +505,11 @@
     (newton_start,) = newton_half(starts, 0)
     newton_residual, newton_tiles = newton_half(residuals, 1)
     image, half_residual, sums = call(
-        functools.partial(image_kernel, way),
+        image_kernel,
         [panel, panel, (groups * columns, 3, count)],
-        [cols],
-        [residual, base, residuals, split_tiles, added],
-        scratch=[held],
-        flops=n * unit,
+        [],
+        [residual, base, off_half(residuals), added],
+        flops=unit // 10,
     )
     images = gather(image)
     sums = lax.all_to_all(sums, ALL, 0, 0, tiled=True)

time: 83.7 us -> 80.7 us (0.964)
  Pallas kernels: 20.2 us -> 18.1 us
    pallas_call x10 -> x12, Pallas kernels: 20.2 us -> 18.1 us  [call(): pl.pallas_call(kernel, out_shape=outs, in_specs=specs, out_specs=[vmem] *...]
  transfers between devices with their start and end apart: 31 -> 31, of which waited for: 13 -> 13; matrix products, arithmetic and copies ran while one was open for 0% -> 0% of each run, Pallas kernels for 13% -> 15%
where the time goes in v4:
time: 80.7 us; the launch traced here: 80.3 us
  starting transfers between devices  25.5 us (32%)
  waiting for transfers between devices  21.2 us (26%)
  Pallas kernels  18.1 us (22%)
  blocking collectives  13.9 us (17%)
  between operations  0.89 us (1%)
    pallas_call x12, Pallas kernels, call(): pl.pallas_call(kernel, out_shape=outs, in_specs=specs, out_specs=[vmem] *...  18.1 us
    ppermute x9, waiting for transfers between devices, gather(): same[way.source(k)] = lax.ppermute(value, 'chip', way.pairs(k))  14 us
    all_to_all x1, blocking collectives, on_device(): lax.all_to_all(keep + received, ('row', 'chip'), 0, 0, tiled=True)  13.9 us
    ppermute x9, starting transfers between devices, gather(): same[way.source(k)] = lax.ppermute(value, 'chip', way.pairs(k))  11.2 us
    ppermute x6, starting transfers between devices, scatter(): added.append(lax.ppermute(sums[k], 'chip', way.pairs(k)))  7.11 us
    ppermute x6, waiting for transfers between devices, scatter(): added.append(lax.ppermute(sums[k], 'chip', way.pairs(k)))  5.33 us
    all_to_all x1, starting transfers between devices, on_device(): sums = lax.all_to_all(sums, ALL, 0, 0, tiled=True)  5.08 us
  transfers between devices with their start and end apart: 31, of which 13 were waited for; matrix products, arithmetic and copies ran while one was open for 0% of the time, Pallas kernels for 15%

profile of v4, /device:TPU:0, one launch (start us, length us, event | category | flops | bytes accessed | tf_op | source)
XLA Modules:
  0.0 80.3 jit_solution(3056318085216295131)
XLA Ops:
  0.7 2.3 %shard_map.87 = (f32[4,96,256]{2,1,0:T(8,128)S(1)}, f32[4,96,256]{2,1,0:T(8,128)S(1)}, bf16[2,7,256,256]{3,2,1,0:T(8,128)(2,1)S(1)}) custom-call(s32[7]{0:T(128)} %bitcast.41, f32[96,256]{1,0:T(8,128)} %bitcast.32, f32[7,256,256]{2,1,0:T(8,128)} %bitcast.27), custom_call_target="tpu_custom_call" | custom-call | flops 264241152 | bytes 1933340 | tf_op jit(solution)/shard_map/pallas_call | solution.py:121
  3.6 3.5 %collective-permute-start.2 = (f32[96,256]{1,0:T(8,128)S(1)}, f32[96,256]{1,0:T(8,128)S(1)}, u32[]{:S(2)}, u32[]{:S(2)}) collective-permute-start(f32[96,256]{1,0:T(8,128)S(1)} %bitcast.33), channel_id=1, source_target_pairs={{0,6},{2,4},{4,2},{6,0},{1,7},{3,5},{5,3},{7,1},{8,14},{10,12},{12... | collective-permute-start | bytes 294920 | tf_op jit(solution)/shard_map/ppermute | solution.py:442
  7.7 2.8 %collective-permute-done.2.refs_4_ = f32[96,256]{1,0:T(8,128)S(1)} collective-permute-done((f32[96,256]{1,0:T(8,128)S(1)}, f32[96,256]{1,0:T(8,128)S(1)}, u32[]{:S(2)}, u32[]{:S(2)}) %collective-permute-start.2) | collective-permute-done | bytes 98336 | tf_op jit(solution)/shard_map/ppermute | solution.py:442
  10.5 2.0 %collective-permute-done.1.refs_3_ = f32[96,256]{1,0:T(8,128)S(1)} collective-permute-done((f32[96,256]{1,0:T(8,128)S(1)}, f32[96,256]{1,0:T(8,128)S(1)}, u32[]{:S(2)}, u32[]{:S(2)}) %collective-permute-start.1) | collective-permute-done | bytes 98336 | tf_op jit(solution)/shard_map/ppermute | solution.py:442
  13.2 1.8 %collective-permute-start.10 = (f32[96,256]{1,0:T(8,128)S(1)}, f32[96,256]{1,0:T(8,128)S(1)}, u32[]{:S(2)}, u32[]{:S(2)}) collective-permute-start(f32[96,256]{1,0:T(8,128)S(1)} %get-tuple-element.46), channel_id=1, source_target_pairs={{0,6},{2,4},{4,2},{6,0},{1,7},{3,5},{5,3},{7,1},{8,14},{10,12},{12... | collective-permute-start | bytes 294920 | tf_op jit(solution)/shard_map/ppermute | solution.py:453
  15.0 1.4 %collective-permute-start.9 = (f32[96,256]{1,0:T(8,128)S(1)}, f32[96,256]{1,0:T(8,128)S(1)}, u32[]{:S(2)}, u32[]{:S(2)}) collective-permute-start(f32[96,256]{1,0:T(8,128)S(1)} %get-tuple-element.47), channel_id=1, source_target_pairs={{0,4},{2,6},{4,0},{6,2},{1,5},{3,7},{5,1},{7,3},{8,12},{10,14},{12... | collective-permute-start | bytes 294920 | tf_op jit(solution)/shard_map/ppermute | solution.py:453
  19.7 1.5 %collective-permute-done.9.refs_7_ = f32[96,256]{1,0:T(8,128)S(1)} collective-permute-done((f32[96,256]{1,0:T(8,128)S(1)}, f32[96,256]{1,0:T(8,128)S(1)}, u32[]{:S(2)}, u32[]{:S(2)}) %collective-permute-start.9) | collective-permute-done | bytes 98336 | tf_op jit(solution)/shard_map/ppermute | solution.py:453
  22.4 1.6 %collective-permute-start.13 = (f32[96,256]{1,0:T(8,128)S(1)}, f32[96,256]{1,0:T(8,128)S(1)}, u32[]{:S(2)}, u32[]{:S(2)}) collective-permute-start(f32[96,256]{1,0:T(8,128)S(1)} %get-tuple-element.25.refs_0_.refs_1_.refs_2_), channel_id=1, source_target_pairs={{0,6},{2,4},{4,2},{6,0},{1,7},{3,5},{5,3},{7,1},{8,14},{10,12},{12... | collective-permute-start | bytes 294920 | tf_op jit(solution)/shard_map/ppermute | solution.py:442
  24.0 1.5 %collective-permute-start.12 = (f32[96,256]{1,0:T(8,128)S(1)}, f32[96,256]{1,0:T(8,128)S(1)}, u32[]{:S(2)}, u32[]{:S(2)}) collective-permute-start(f32[96,256]{1,0:T(8,128)S(1)} %get-tuple-element.25.refs_0_.refs_1_.refs_2_), channel_id=1, source_target_pairs={{0,4},{2,6},{4,0},{6,2},{1,5},{3,7},{5,1},{7,3},{8,12},{10,14},{12... | collective-permute-start | bytes 294920 | tf_op jit(solution)/shard_map/ppermute | solution.py:442
  26.0 3.1 %collective-permute-done.13.refs_4_ = f32[96,256]{1,0:T(8,128)S(1)} collective-permute-done((f32[96,256]{1,0:T(8,128)S(1)}, f32[96,256]{1,0:T(8,128)S(1)}, u32[]{:S(2)}, u32[]{:S(2)}) %collective-permute-start.13) | collective-permute-done | bytes 98336 | tf_op jit(solution)/shard_map/ppermute | solution.py:442
  29.1 1.6 %collective-permute-done.12.refs_3_ = f32[96,256]{1,0:T(8,128)S(1)} collective-permute-done((f32[96,256]{1,0:T(8,128)S(1)}, f32[96,256]{1,0:T(8,128)S(1)}, u32[]{:S(2)}, u32[]{:S(2)}) %collective-permute-start.12) | collective-permute-done | bytes 98336 | tf_op jit(solution)/shard_map/ppermute | solution.py:442
  31.2 1.6 %collective-permute-start.21 = (f32[96,256]{1,0:T(8,128)S(1)}, f32[96,256]{1,0:T(8,128)S(1)}, u32[]{:S(2)}, u32[]{:S(2)}) collective-permute-start(f32[96,256]{1,0:T(8,128)S(1)} %get-tuple-element.42), channel_id=1, source_target_pairs={{0,6},{2,4},{4,2},{6,0},{1,7},{3,5},{5,3},{7,1},{8,14},{10,12},{12... | collective-permute-start | bytes 294920 | tf_op jit(solution)/shard_map/ppermute | solution.py:453
  32.8 1.5 %collective-permute-start.20 = (f32[96,256]{1,0:T(8,128)S(1)}, f32[96,256]{1,0:T(8,128)S(1)}, u32[]{:S(2)}, u32[]{:S(2)}) collective-permute-start(f32[96,256]{1,0:T(8,128)S(1)} %get-tuple-element.43), channel_id=1, source_target_pairs={{0,4},{2,6},{4,0},{6,2},{1,5},{3,7},{5,1},{7,3},{8,12},{10,14},{12... | collective-permute-start | bytes 294920 | tf_op jit(solution)/shard_map/ppermute | solution.py:453
  35.2 1.3 %shard_map.91.refs_2_ = f32[96,256]{1,0:T(8,128)S(1)} custom-call(s32[7]{0:T(128)S(1)} %bitcast.44, f32[96,256]{1,0:T(8,128)S(1)} %get-tuple-element.25.refs_0_.refs_1_.refs_2_, f32[96,256]{1,0:T(8,128)S(1)} %collective-permute-done.11.refs_2_, f32[96,256]{1,0:T(8,128)S(1)} %collective-permute-done.12.refs_3_, ...), custom_call_target="tpu_custom_call" | custom-call | flops 264241152 | bytes 2621440 | tf_op jit(solution)/shard_map/pallas_call | solution.py:121
  37.5 1.5 %collective-permute-done.20.refs_5_ = f32[96,256]{1,0:T(8,128)S(1)} collective-permute-done((f32[96,256]{1,0:T(8,128)S(1)}, f32[96,256]{1,0:T(8,128)S(1)}, u32[]{:S(2)}, u32[]{:S(2)}) %collective-permute-start.20) | collective-permute-done | bytes 98336 | tf_op jit(solution)/shard_map/ppermute | solution.py:453
  40.0 1.5 %collective-permute-start.24 = (f32[96,256]{1,0:T(8,128)S(1)}, f32[96,256]{1,0:T(8,128)S(1)}, u32[]{:S(2)}, u32[]{:S(2)}) collective-permute-start(f32[96,256]{1,0:T(8,128)S(1)} %get-tuple-element.29.refs_1_.refs_3_), channel_id=1, source_target_pairs={{0,6},{2,4},{4,2},{6,0},{1,7},{3,5},{5,3},{7,1},{8,14},{10,12},{12... | collective-permute-start | bytes 294920 | tf_op jit(solution)/shard_map/ppermute | solution.py:442
  41.5 1.5 %collective-permute-start.23 = (f32[96,256]{1,0:T(8,128)S(1)}, f32[96,256]{1,0:T(8,128)S(1)}, u32[]{:S(2)}, u32[]{:S(2)}) collective-permute-start(f32[96,256]{1,0:T(8,128)S(1)} %get-tuple-element.29.refs_1_.refs_3_), channel_id=1, source_target_pairs={{0,4},{2,6},{4,0},{6,2},{1,5},{3,7},{5,1},{7,3},{8,12},{10,14},{12... | collective-permute-start | bytes 294920 | tf_op jit(solution)/shard_map/ppermute | solution.py:442
  43.5 2.7 %collective-permute-done.24.refs_4_ = f32[96,256]{1,0:T(8,128)S(1)} collective-permute-done((f32[96,256]{1,0:T(8,128)S(1)}, f32[96,256]{1,0:T(8,128)S(1)}, u32[]{:S(2)}, u32[]{:S(2)}) %collective-permute-start.24) | collective-permute-done | bytes 98336 | tf_op jit(solution)/shard_map/ppermute | solution.py:442
  46.2 1.5 %collective-permute-done.23.refs_3_ = f32[96,256]{1,0:T(8,128)S(1)} collective-permute-done((f32[96,256]{1,0:T(8,128)S(1)}, f32[96,256]{1,0:T(8,128)S(1)}, u32[]{:S(2)}, u32[]{:S(2)}) %collective-permute-start.23) | collective-permute-done | bytes 98336 | tf_op jit(solution)/shard_map/ppermute | solution.py:442
  48.3 2.5 %shard_map.95.refs_6_ = f32[96,256]{1,0:T(8,128)S(1)} custom-call(s32[7]{0:T(128)S(1)} %bitcast.45, f32[96,256]{1,0:T(8,128)S(1)} %bitcast.39, f32[96,256]{1,0:T(8,128)S(1)} %collective-permute-done.refs_2_, f32[96,256]{1,0:T(8,128)S(1)} %collective-permute-done.1.refs_3_, f32[96,256]{1,0:T(8,128)S(1)} %collective-permute-done.2.refs_4_, ...), custom_call_target="tpu_custom_call" | custom-call | flops 528482304 | bytes 2883584 | tf_op jit(solution)/shard_map/pallas_call | solution.py:121
  50.8 5.1 %all-to-all-start = ((f32[32,3,96]{2,1,0:T(4,128)}), f32[32,3,96]{2,1,0:T(4,128)S(1)}, u32[]{:S(2)}, u32[]{:S(2)}) async-start(f32[32,3,96]{2,1,0:T(4,128)} %get-tuple-element.28), calls=%async_computation | async-start | bytes 131072 | tf_op jit(solution)/shard_map/all_to_all | solution.py:515
  55.9 2.5 %shard_map.93 = (f32[96,256]{1,0:T(8,128)S(1)}, bf16[2,7,256,256]{3,2,1,0:T(8,128)(2,1)S(1)}) custom-call(s32[7]{0:T(128)S(1)} %bitcast.46, f32[96,256]{1,0:T(8,128)S(1)} %get-tuple-element.25.refs_0_.refs_1_.refs_2_, f32[96,256]{1,0:T(8,128)S(1)} %collective-permute-done.11.refs_2_, f32[96,256]{1,0:T(8,128)S(1)} %collective-permute-done.12.refs_3_, ...), custom_call_target="tpu_custom_call" | custom-call | flops 528482304 | bytes 2883584 | tf_op jit(solution)/shard_map/pallas_call | solution.py:121
  59.1 3.5 %shard_map.94 = (f32[96,256]{1,0:T(8,128)S(1)}, f32[96,256]{1,0:T(8,128)S(1)}) custom-call(s32[7]{0:T(128)S(1)} %bitcast.47, f32[96,256]{1,0:T(8,128)S(1)} %get-tuple-element.29.refs_1_.refs_3_, f32[96,256]{1,0:T(8,128)S(1)} %collective-permute-done.22.refs_2_, f32[96,256]{1,0:T(8,128)S(1)} %collective-permute-done.23.refs_3_, ...), custom_call_target="tpu_custom_call" | custom-call | flops 528482304 | bytes 4980736 | tf_op jit(solution)/shard_map/pallas_call | solution.py:121
  65.6 13.9 %all_to_all.10.refs_0_ = f32[16,16,128]{2,1,0:T(8,128)S(1)} all-to-all(f32[16,16,128]{2,1,0:T(8,128)S(1)} %add.65), channel_id=1, replica_groups=mesh['row'=4,'chip'=4,'core'=2] {'row','chip'}, dimensions={0} | all-to-all | bytes 262144 | tf_op jit(solution)/shard_map/all_to_all | solution.py:551
  (74 shorter events, 15.9 us)
Async XLA Ops:
  3.0 10.1 %collective-permute-start.7 = (f32[4,96,256]{2,1,0:T(8,128)S(1)}, f32[4,96,256]{2,1,0:T(8,128)S(1)}, u32[]{:S(2)}, u32[]{:S(2)}) collective-permute-start(f32[4,96,256]{2,1,0:T(8,128)S(1)} %get-tuple-element.24), channel_id=1, source_target_pairs={{0,1},{1,0},{2,3},{3,2},{4,5},{5,4},{6,7},{7,6},{8,9},{9,8},{10,11... | collective-permute-start | bytes 1179656 | tf_op jit(solution)/shard_map/ppermute | solution.py:449
  3.6 7.0 %collective-permute-start.2 = (f32[96,256]{1,0:T(8,128)S(1)}, f32[96,256]{1,0:T(8,128)S(1)}, u32[]{:S(2)}, u32[]{:S(2)}) collective-permute-start(f32[96,256]{1,0:T(8,128)S(1)} %bitcast.33), channel_id=1, source_target_pairs={{0,6},{2,4},{4,2},{6,0},{1,7},{3,5},{5,3},{7,1},{8,14},{10,12},{12... | collective-permute-start | bytes 294920 | tf_op jit(solution)/shard_map/ppermute | solution.py:442
  7.1 5.5 %collective-permute-start.1 = (f32[96,256]{1,0:T(8,128)S(1)}, f32[96,256]{1,0:T(8,128)S(1)}, u32[]{:S(2)}, u32[]{:S(2)}) collective-permute-start(f32[96,256]{1,0:T(8,128)S(1)} %bitcast.34), channel_id=1, source_target_pairs={{0,4},{2,6},{4,0},{6,2},{1,5},{3,7},{5,1},{7,3},{8,12},{10,14},{12... | collective-permute-start | bytes 294920 | tf_op jit(solution)/shard_map/ppermute | solution.py:442
  7.6 5.2 %collective-permute-start = (f32[96,256]{1,0:T(8,128)S(1)}, f32[96,256]{1,0:T(8,128)S(1)}, u32[]{:S(2)}, u32[]{:S(2)}) collective-permute-start(f32[96,256]{1,0:T(8,128)S(1)} %bitcast.35), channel_id=1, source_target_pairs={{0,2},{2,0},{4,6},{6,4},{1,3},{3,1},{5,7},{7,5},{8,10},{10,8},{12,... | collective-permute-start | bytes 294920 | tf_op jit(solution)/shard_map/ppermute | solution.py:442
  7.7 7.2 %collective-permute-start.3 = (f32[96,256]{1,0:T(8,128)S(1)}, f32[96,256]{1,0:T(8,128)S(1)}, u32[]{:S(2)}, u32[]{:S(2)}) collective-permute-start(f32[96,256]{1,0:T(8,128)S(1)} %bitcast.36), channel_id=1, source_target_pairs={{0,1},{1,0},{2,3},{3,2},{4,5},{5,4},{6,7},{7,6},{8,9},{9,8},{10,11... | collective-permute-start | bytes 294920 | tf_op jit(solution)/shard_map/ppermute | solution.py:446
  10.5 5.8 %collective-permute-start.6 = (f32[96,256]{1,0:T(8,128)S(1)}, f32[96,256]{1,0:T(8,128)S(1)}, u32[]{:S(2)}, u32[]{:S(2)}) collective-permute-start(f32[96,256]{1,0:T(8,128)S(1)} %collective-permute-done.2.refs_4_), channel_id=1, source_target_pairs={{0,1},{1,0},{2,3},{3,2},{4,5},{5,4},{6,7},{7,6},{8,9},{9,8},{10,11... | collective-permute-start | bytes 294920 | tf_op jit(solution)/shard_map/ppermute | solution.py:446
  13.2 6.5 %collective-permute-start.10 = (f32[96,256]{1,0:T(8,128)S(1)}, f32[96,256]{1,0:T(8,128)S(1)}, u32[]{:S(2)}, u32[]{:S(2)}) collective-permute-start(f32[96,256]{1,0:T(8,128)S(1)} %get-tuple-element.46), channel_id=1, source_target_pairs={{0,6},{2,4},{4,2},{6,0},{1,7},{3,5},{5,3},{7,1},{8,14},{10,12},{12... | collective-permute-start | bytes 294920 | tf_op jit(solution)/shard_map/ppermute | solution.py:453
  15.0 6.2 %collective-permute-start.9 = (f32[96,256]{1,0:T(8,128)S(1)}, f32[96,256]{1,0:T(8,128)S(1)}, u32[]{:S(2)}, u32[]{:S(2)}) collective-permute-start(f32[96,256]{1,0:T(8,128)S(1)} %get-tuple-element.47), channel_id=1, source_target_pairs={{0,4},{2,6},{4,0},{6,2},{1,5},{3,7},{5,1},{7,3},{8,12},{10,14},{12... | collective-permute-start | bytes 294920 | tf_op jit(solution)/shard_map/ppermute | solution.py:453
  16.4 4.8 %collective-permute-start.8 = (f32[96,256]{1,0:T(8,128)S(1)}, f32[96,256]{1,0:T(8,128)S(1)}, u32[]{:S(2)}, u32[]{:S(2)}) collective-permute-start(f32[96,256]{1,0:T(8,128)S(1)} %get-tuple-element.48), channel_id=1, source_target_pairs={{0,2},{2,0},{4,6},{6,4},{1,3},{3,1},{5,7},{7,5},{8,10},{10,8},{12,... | collective-permute-start | bytes 294920 | tf_op jit(solution)/shard_map/ppermute | solution.py:453
  22.4 8.8 %collective-permute-start.18 = (f32[4,96,256]{2,1,0:T(8,128)S(1)}, f32[4,96,256]{2,1,0:T(8,128)S(1)}, u32[]{:S(2)}, u32[]{:S(2)}) collective-permute-start(f32[4,96,256]{2,1,0:T(8,128)S(1)} %get-tuple-element.27), channel_id=1, source_target_pairs={{0,1},{1,0},{2,3},{3,2},{4,5},{5,4},{6,7},{7,6},{8,9},{9,8},{10,11... | collective-permute-start | bytes 1179656 | tf_op jit(solution)/shard_map/ppermute | solution.py:449
  22.4 6.6 %collective-permute-start.13 = (f32[96,256]{1,0:T(8,128)S(1)}, f32[96,256]{1,0:T(8,128)S(1)}, u32[]{:S(2)}, u32[]{:S(2)}) collective-permute-start(f32[96,256]{1,0:T(8,128)S(1)} %get-tuple-element.25.refs_0_.refs_1_.refs_2_), channel_id=1, source_target_pairs={{0,6},{2,4},{4,2},{6,0},{1,7},{3,5},{5,3},{7,1},{8,14},{10,12},{12... | collective-permute-start | bytes 294920 | tf_op jit(solution)/shard_map/ppermute | solution.py:442
  24.0 6.6 %collective-permute-start.12 = (f32[96,256]{1,0:T(8,128)S(1)}, f32[96,256]{1,0:T(8,128)S(1)}, u32[]{:S(2)}, u32[]{:S(2)}) collective-permute-start(f32[96,256]{1,0:T(8,128)S(1)} %get-tuple-element.25.refs_0_.refs_1_.refs_2_), channel_id=1, source_target_pairs={{0,4},{2,6},{4,0},{6,2},{1,5},{3,7},{5,1},{7,3},{8,12},{10,14},{12... | collective-permute-start | bytes 294920 | tf_op jit(solution)/shard_map/ppermute | solution.py:442
  25.5 5.2 %collective-permute-start.11 = (f32[96,256]{1,0:T(8,128)S(1)}, f32[96,256]{1,0:T(8,128)S(1)}, u32[]{:S(2)}, u32[]{:S(2)}) collective-permute-start(f32[96,256]{1,0:T(8,128)S(1)} %get-tuple-element.25.refs_0_.refs_1_.refs_2_), channel_id=1, source_target_pairs={{0,2},{2,0},{4,6},{6,4},{1,3},{3,1},{5,7},{7,5},{8,10},{10,8},{12,... | collective-permute-start | bytes 294920 | tf_op jit(solution)/shard_map/ppermute | solution.py:442
  26.0 6.8 %collective-permute-start.14 = (f32[96,256]{1,0:T(8,128)S(1)}, f32[96,256]{1,0:T(8,128)S(1)}, u32[]{:S(2)}, u32[]{:S(2)}) collective-permute-start(f32[96,256]{1,0:T(8,128)S(1)} %get-tuple-element.25.refs_0_.refs_1_.refs_2_), channel_id=1, source_target_pairs={{0,1},{1,0},{2,3},{3,2},{4,5},{5,4},{6,7},{7,6},{8,9},{9,8},{10,11... | collective-permute-start | bytes 294920 | tf_op jit(solution)/shard_map/ppermute | solution.py:446
  29.1 5.2 %collective-permute-start.17 = (f32[96,256]{1,0:T(8,128)S(1)}, f32[96,256]{1,0:T(8,128)S(1)}, u32[]{:S(2)}, u32[]{:S(2)}) collective-permute-start(f32[96,256]{1,0:T(8,128)S(1)} %collective-permute-done.13.refs_4_), channel_id=1, source_target_pairs={{0,1},{1,0},{2,3},{3,2},{4,5},{5,4},{6,7},{7,6},{8,9},{9,8},{10,11... | collective-permute-start | bytes 294920 | tf_op jit(solution)/shard_map/ppermute | solution.py:446
  31.2 6.3 %collective-permute-start.21 = (f32[96,256]{1,0:T(8,128)S(1)}, f32[96,256]{1,0:T(8,128)S(1)}, u32[]{:S(2)}, u32[]{:S(2)}) collective-permute-start(f32[96,256]{1,0:T(8,128)S(1)} %get-tuple-element.42), channel_id=1, source_target_pairs={{0,6},{2,4},{4,2},{6,0},{1,7},{3,5},{5,3},{7,1},{8,14},{10,12},{12... | collective-permute-start | bytes 294920 | tf_op jit(solution)/shard_map/ppermute | solution.py:453
  32.8 6.2 %collective-permute-start.20 = (f32[96,256]{1,0:T(8,128)S(1)}, f32[96,256]{1,0:T(8,128)S(1)}, u32[]{:S(2)}, u32[]{:S(2)}) collective-permute-start(f32[96,256]{1,0:T(8,128)S(1)} %get-tuple-element.43), channel_id=1, source_target_pairs={{0,4},{2,6},{4,0},{6,2},{1,5},{3,7},{5,1},{7,3},{8,12},{10,14},{12... | collective-permute-start | bytes 294920 | tf_op jit(solution)/shard_map/ppermute | solution.py:453
  40.0 6.2 %collective-permute-start.24 = (f32[96,256]{1,0:T(8,128)S(1)}, f32[96,256]{1,0:T(8,128)S(1)}, u32[]{:S(2)}, u32[]{:S(2)}) collective-permute-start(f32[96,256]{1,0:T(8,128)S(1)} %get-tuple-element.29.refs_1_.refs_3_), channel_id=1, source_target_pairs={{0,6},{2,4},{4,2},{6,0},{1,7},{3,5},{5,3},{7,1},{8,14},{10,12},{12... | collective-permute-start | bytes 294920 | tf_op jit(solution)/shard_map/ppermute | solution.py:442
  41.5 6.2 %collective-permute-start.23 = (f32[96,256]{1,0:T(8,128)S(1)}, f32[96,256]{1,0:T(8,128)S(1)}, u32[]{:S(2)}, u32[]{:S(2)}) collective-permute-start(f32[96,256]{1,0:T(8,128)S(1)} %get-tuple-element.29.refs_1_.refs_3_), channel_id=1, source_target_pairs={{0,4},{2,6},{4,0},{6,2},{1,5},{3,7},{5,1},{7,3},{8,12},{10,14},{12... | collective-permute-start | bytes 294920 | tf_op jit(solution)/shard_map/ppermute | solution.py:442
  43.5 15.5 %collective-permute-start.25 = (f32[96,256]{1,0:T(8,128)S(1)}, f32[96,256]{1,0:T(8,128)S(1)}, u32[]{:S(2)}, u32[]{:S(2)}) collective-permute-start(f32[96,256]{1,0:T(8,128)S(1)} %get-tuple-element.29.refs_1_.refs_3_), channel_id=1, source_target_pairs={{0,1},{1,0},{2,3},{3,2},{4,5},{5,4},{6,7},{7,6},{8,9},{9,8},{10,11... | collective-permute-start | bytes 294920 | tf_op jit(solution)/shard_map/ppermute | solution.py:446
  46.2 12.8 %collective-permute-start.28 = (f32[96,256]{1,0:T(8,128)S(1)}, f32[96,256]{1,0:T(8,128)S(1)}, u32[]{:S(2)}, u32[]{:S(2)}) collective-permute-start(f32[96,256]{1,0:T(8,128)S(1)} %collective-permute-done.24.refs_4_), channel_id=1, source_target_pairs={{0,1},{1,0},{2,3},{3,2},{4,5},{5,4},{6,7},{7,6},{8,9},{9,8},{10,11... | collective-permute-start | bytes 294920 | tf_op jit(solution)/shard_map/ppermute | solution.py:446
  47.8 11.3 %collective-permute-start.27 = (f32[96,256]{1,0:T(8,128)S(1)}, f32[96,256]{1,0:T(8,128)}, u32[]{:S(2)}, u32[]{:S(2)}) collective-permute-start(f32[96,256]{1,0:T(8,128)S(1)} %collective-permute-done.23.refs_3_), channel_id=1, source_target_pairs={{0,1},{1,0},{2,3},{3,2},{4,5},{5,4},{6,7},{7,6},{8,9},{9,8},{10,11... | collective-permute-start | bytes 294920 | tf_op jit(solution)/shard_map/ppermute | solution.py:446
  47.8 11.3 %collective-permute-start.26 = (f32[96,256]{1,0:T(8,128)S(1)}, f32[96,256]{1,0:T(8,128)}, u32[]{:S(2)}, u32[]{:S(2)}) collective-permute-start(f32[96,256]{1,0:T(8,128)S(1)} %collective-permute-done.22.refs_2_), channel_id=1, source_target_pairs={{0,1},{1,0},{2,3},{3,2},{4,5},{5,4},{6,7},{7,6},{8,9},{9,8},{10,11... | collective-permute-start | bytes 294920 | tf_op jit(solution)/shard_map/ppermute | solution.py:446
  50.8 12.5 %all-to-all-start = ((f32[32,3,96]{2,1,0:T(4,128)}), f32[32,3,96]{2,1,0:T(4,128)S(1)}, u32[]{:S(2)}, u32[]{:S(2)}) async-start(f32[32,3,96]{2,1,0:T(4,128)} %get-tuple-element.28), calls=%async_computation | async-start | bytes 131072 | tf_op jit(solution)/shard_map/all_to_all | solution.py:515
  (17 other events, 109.3 us)

commit v5 on v4

--- a/solution.py
+++ b/solution.py
@@ -262,7 +262,7 @@
     rr, rq, qq = totals[0:1], totals[1:2], totals[2:3]
     step = rr / rq
     norm = rr - 2.0 * step * rq + step * step * qq
-    return norm, column_of(step), 1.0 + column_of(norm / rr)
+    return column_of(step), column_of(norm / rr)
 
 
 def newton_kernel(way, cols, gathered, diag, tiles, out, *more):
@@ -327,22 +327,24 @@
     newton_image,
     x_out,
     d_out,
-    norm_out,
     keep,
     send,
     order,
     blocks,
     pieces,
 ):
-    norm_out[...], step, grow = steps(sums)
+    step, ratio = steps(sums)
     count = d_out.shape[0]
     r, q = residual[...], image[...]
     x1 = start[...] + step * r
-    d1 = grow * r - step * q
+    r1 = r - step * q
+    d1 = r1 + ratio * r
+    grow = 1.0 + ratio
     x_out[...] = x1
     d_out[...] = d1
     half_d = grow * half_residual[...] - step * half_image[...]
     curvature = 2.0 * row_sums(d1 * half_d)
+    norm = row_sums(r1 * r1)
     ux = newton_start[...] + step * newton_residual[...]
     ud = grow * newton_residual[...] - step * newton_image[...]
     hr, hc = count // parts_rows, count // parts_cols
@@ -362,8 +364,12 @@
     ) + dot_full(jnp.concatenate([ux, ud], axis=0), order[0], NT)
     depth = keep.shape[1]
     left = lax.broadcasted_iota(jnp.int32, (count, LANES), 1) < HALF
-    wide = jnp.concatenate([curvature, jnp.zeros((1, LANES - count), F32)], axis=1)
-    spot = lax.broadcasted_iota(jnp.int32, (depth, LANES), 0) == hc
+    pad = jnp.zeros((1, LANES - count), F32)
+    wide = jnp.concatenate([curvature, pad], axis=1)
+    norm = jnp.concatenate([norm, pad], axis=1)
+    line = lax.broadcasted_iota(jnp.int32, (depth, LANES), 0)
+    wide = jnp.where(line == hc, wide, norm)
+    spot = (line == hc) | (line == hc + 1)
     first_core = lax.axis_index("core") == 0
     for r_index in range(parts_rows):
         lanes = slice(r_index // 2 * LANES, (r_index // 2 + 1) * LANES)
@@ -383,13 +389,13 @@
             send[at] = jnp.where(first_core, two, one)
 
 
-def last_kernel(parts_rows, parts_cols, received, norm, x1, d1, x_out, hessian):
+def last_kernel(parts_rows, parts_cols, received, x1, d1, x_out, hessian):
     total = received[0]
     for device in range(1, received.shape[0]):
         total = total + received[device]
     count = x1.shape[0]
     hr, hc = count // parts_rows, count // parts_cols
-    step = norm[...] / total[hc : hc + 1, 0:count]
+    step = total[hc + 1 : hc + 2, 0:count] / total[hc : hc + 1, 0:count]
     step_col = column_of(step)
     x_out[...] = x1[...] + step_col * d1[...]
     row_at = lax.axis_index("row") * hr
@@ -515,7 +521,7 @@
     sums = lax.all_to_all(sums, ALL, 0, 0, tiled=True)
     images = forward(images)
     hr, hc = count // groups, count // columns
-    depth = -(-(hc + 1) // 8) * 8
+    depth = -(-(hc + 2) // 8) * 8
     share = (groups * chips, depth, LANES)
     half_image, newton_image = call(
         functools.partial(halves_kernel, way),
@@ -525,9 +531,9 @@
         scratch=[held],
         flops=2 * n * unit,
     )
-    x1, d1, norm, keep, send = call(
+    x1, d1, keep, send = call(
         functools.partial(middle_kernel, groups, columns),
-        [panel, panel, (1, count), share, share],
+        [panel, panel, share, share],
         [],
         [
             sums,
@@ -553,7 +559,7 @@
         functools.partial(last_kernel, groups, columns),
         [panel, (hc, hr)],
         [],
-        [received, norm, x1, d1],
+        [received, x1, d1],
         flops=unit // 100,
     )
     return solved[None], hessian.T

time: 80.7 us -> 80.8 us (level)
  no operation moved by 1% of the time
where the time goes in v5:
time: 80.8 us; the launch traced here: 80.5 us
  starting transfers between devices  25.5 us (32%)
  waiting for transfers between devices  21.2 us (26%)
  Pallas kernels  18.2 us (23%)
  blocking collectives  13.9 us (17%)
  between operations  0.89 us (1%)
    pallas_call x12, Pallas kernels, call(): pl.pallas_call(kernel, out_shape=outs, in_specs=specs, out_specs=[vmem] *...  18.2 us
    ppermute x9, waiting for transfers between devices, gather(): same[way.source(k)] = lax.ppermute(value, 'chip', way.pairs(k))  14 us
    all_to_all x1, blocking collectives, on_device(): lax.all_to_all(keep + received, ('row', 'chip'), 0, 0, tiled=True)  13.9 us
    ppermute x9, starting transfers between devices, gather(): same[way.source(k)] = lax.ppermute(value, 'chip', way.pairs(k))  11.2 us
    ppermute x6, starting transfers between devices, scatter(): added.append(lax.ppermute(sums[k], 'chip', way.pairs(k)))  7.11 us
    ppermute x6, waiting for transfers between devices, scatter(): added.append(lax.ppermute(sums[k], 'chip', way.pairs(k)))  5.33 us
    all_to_all x1, starting transfers between devices, on_device(): sums = lax.all_to_all(sums, ALL, 0, 0, tiled=True)  5.08 us
  transfers between devices with their start and end apart: 31, of which 13 were waited for; matrix products, arithmetic and copies ran while one was open for 0% of the time, Pallas kernels for 15%

profile of v5, /device:TPU:0, one launch (start us, length us, event | category | flops | bytes accessed | tf_op | source)
XLA Modules:
  0.0 80.5 jit_solution(10434946852555053209)
XLA Ops:
  0.7 2.3 %shard_map.87 = (f32[4,96,256]{2,1,0:T(8,128)S(1)}, f32[4,96,256]{2,1,0:T(8,128)S(1)}, bf16[2,7,256,256]{3,2,1,0:T(8,128)(2,1)S(1)}) custom-call(s32[7]{0:T(128)} %bitcast.41, f32[96,256]{1,0:T(8,128)} %bitcast.32, f32[7,256,256]{2,1,0:T(8,128)} %bitcast.27), custom_call_target="tpu_custom_call" | custom-call | flops 264241152 | bytes 1933340 | tf_op jit(solution)/shard_map/pallas_call | solution.py:121
  3.6 3.5 %collective-permute-start.2 = (f32[96,256]{1,0:T(8,128)S(1)}, f32[96,256]{1,0:T(8,128)S(1)}, u32[]{:S(2)}, u32[]{:S(2)}) collective-permute-start(f32[96,256]{1,0:T(8,128)S(1)} %bitcast.33), channel_id=1, source_target_pairs={{0,6},{2,4},{4,2},{6,0},{1,7},{3,5},{5,3},{7,1},{8,14},{10,12},{12... | collective-permute-start | bytes 294920 | tf_op jit(solution)/shard_map/ppermute | solution.py:448
  7.7 2.8 %collective-permute-done.2.refs_4_ = f32[96,256]{1,0:T(8,128)S(1)} collective-permute-done((f32[96,256]{1,0:T(8,128)S(1)}, f32[96,256]{1,0:T(8,128)S(1)}, u32[]{:S(2)}, u32[]{:S(2)}) %collective-permute-start.2) | collective-permute-done | bytes 98336 | tf_op jit(solution)/shard_map/ppermute | solution.py:448
  10.5 2.0 %collective-permute-done.1.refs_3_ = f32[96,256]{1,0:T(8,128)S(1)} collective-permute-done((f32[96,256]{1,0:T(8,128)S(1)}, f32[96,256]{1,0:T(8,128)S(1)}, u32[]{:S(2)}, u32[]{:S(2)}) %collective-permute-start.1) | collective-permute-done | bytes 98336 | tf_op jit(solution)/shard_map/ppermute | solution.py:448
  13.2 1.8 %collective-permute-start.10 = (f32[96,256]{1,0:T(8,128)S(1)}, f32[96,256]{1,0:T(8,128)S(1)}, u32[]{:S(2)}, u32[]{:S(2)}) collective-permute-start(f32[96,256]{1,0:T(8,128)S(1)} %get-tuple-element.44), channel_id=1, source_target_pairs={{0,6},{2,4},{4,2},{6,0},{1,7},{3,5},{5,3},{7,1},{8,14},{10,12},{12... | collective-permute-start | bytes 294920 | tf_op jit(solution)/shard_map/ppermute | solution.py:459
  15.0 1.4 %collective-permute-start.9 = (f32[96,256]{1,0:T(8,128)S(1)}, f32[96,256]{1,0:T(8,128)S(1)}, u32[]{:S(2)}, u32[]{:S(2)}) collective-permute-start(f32[96,256]{1,0:T(8,128)S(1)} %get-tuple-element.45), channel_id=1, source_target_pairs={{0,4},{2,6},{4,0},{6,2},{1,5},{3,7},{5,1},{7,3},{8,12},{10,14},{12... | collective-permute-start | bytes 294920 | tf_op jit(solution)/shard_map/ppermute | solution.py:459
  19.7 1.5 %collective-permute-done.9.refs_7_ = f32[96,256]{1,0:T(8,128)S(1)} collective-permute-done((f32[96,256]{1,0:T(8,128)S(1)}, f32[96,256]{1,0:T(8,128)S(1)}, u32[]{:S(2)}, u32[]{:S(2)}) %collective-permute-start.9) | collective-permute-done | bytes 98336 | tf_op jit(solution)/shard_map/ppermute | solution.py:459
  22.4 1.6 %collective-permute-start.13 = (f32[96,256]{1,0:T(8,128)S(1)}, f32[96,256]{1,0:T(8,128)S(1)}, u32[]{:S(2)}, u32[]{:S(2)}) collective-permute-start(f32[96,256]{1,0:T(8,128)S(1)} %get-tuple-element.24.refs_0_.refs_1_.refs_2_), channel_id=1, source_target_pairs={{0,6},{2,4},{4,2},{6,0},{1,7},{3,5},{5,3},{7,1},{8,14},{10,12},{12... | collective-permute-start | bytes 294920 | tf_op jit(solution)/shard_map/ppermute | solution.py:448
  24.0 1.5 %collective-permute-start.12 = (f32[96,256]{1,0:T(8,128)S(1)}, f32[96,256]{1,0:T(8,128)S(1)}, u32[]{:S(2)}, u32[]{:S(2)}) collective-permute-start(f32[96,256]{1,0:T(8,128)S(1)} %get-tuple-element.24.refs_0_.refs_1_.refs_2_), channel_id=1, source_target_pairs={{0,4},{2,6},{4,0},{6,2},{1,5},{3,7},{5,1},{7,3},{8,12},{10,14},{12... | collective-permute-start | bytes 294920 | tf_op jit(solution)/shard_map/ppermute | solution.py:448
  26.0 3.1 %collective-permute-done.13.refs_4_ = f32[96,256]{1,0:T(8,128)S(1)} collective-permute-done((f32[96,256]{1,0:T(8,128)S(1)}, f32[96,256]{1,0:T(8,128)S(1)}, u32[]{:S(2)}, u32[]{:S(2)}) %collective-permute-start.13) | collective-permute-done | bytes 98336 | tf_op jit(solution)/shard_map/ppermute | solution.py:448
  29.1 1.6 %collective-permute-done.12.refs_3_ = f32[96,256]{1,0:T(8,128)S(1)} collective-permute-done((f32[96,256]{1,0:T(8,128)S(1)}, f32[96,256]{1,0:T(8,128)S(1)}, u32[]{:S(2)}, u32[]{:S(2)}) %collective-permute-start.12) | collective-permute-done | bytes 98336 | tf_op jit(solution)/shard_map/ppermute | solution.py:448
  31.2 1.6 %collective-permute-start.21 = (f32[96,256]{1,0:T(8,128)S(1)}, f32[96,256]{1,0:T(8,128)S(1)}, u32[]{:S(2)}, u32[]{:S(2)}) collective-permute-start(f32[96,256]{1,0:T(8,128)S(1)} %get-tuple-element.40), channel_id=1, source_target_pairs={{0,6},{2,4},{4,2},{6,0},{1,7},{3,5},{5,3},{7,1},{8,14},{10,12},{12... | collective-permute-start | bytes 294920 | tf_op jit(solution)/shard_map/ppermute | solution.py:459
  32.8 1.5 %collective-permute-start.20 = (f32[96,256]{1,0:T(8,128)S(1)}, f32[96,256]{1,0:T(8,128)S(1)}, u32[]{:S(2)}, u32[]{:S(2)}) collective-permute-start(f32[96,256]{1,0:T(8,128)S(1)} %get-tuple-element.41), channel_id=1, source_target_pairs={{0,4},{2,6},{4,0},{6,2},{1,5},{3,7},{5,1},{7,3},{8,12},{10,14},{12... | collective-permute-start | bytes 294920 | tf_op jit(solution)/shard_map/ppermute | solution.py:459
  35.2 1.3 %shard_map.91.refs_2_ = f32[96,256]{1,0:T(8,128)S(1)} custom-call(s32[7]{0:T(128)S(1)} %bitcast.44, f32[96,256]{1,0:T(8,128)S(1)} %get-tuple-element.24.refs_0_.refs_1_.refs_2_, f32[96,256]{1,0:T(8,128)S(1)} %collective-permute-done.11.refs_2_, f32[96,256]{1,0:T(8,128)S(1)} %collective-permute-done.12.refs_3_, ...), custom_call_target="tpu_custom_call" | custom-call | flops 264241152 | bytes 2621440 | tf_op jit(solution)/shard_map/pallas_call | solution.py:121
  37.5 1.5 %collective-permute-done.20.refs_5_ = f32[96,256]{1,0:T(8,128)S(1)} collective-permute-done((f32[96,256]{1,0:T(8,128)S(1)}, f32[96,256]{1,0:T(8,128)S(1)}, u32[]{:S(2)}, u32[]{:S(2)}) %collective-permute-start.20) | collective-permute-done | bytes 98336 | tf_op jit(solution)/shard_map/ppermute | solution.py:459
  40.0 1.5 %collective-permute-start.24 = (f32[96,256]{1,0:T(8,128)S(1)}, f32[96,256]{1,0:T(8,128)S(1)}, u32[]{:S(2)}, u32[]{:S(2)}) collective-permute-start(f32[96,256]{1,0:T(8,128)S(1)} %get-tuple-element.28.refs_1_.refs_3_), channel_id=1, source_target_pairs={{0,6},{2,4},{4,2},{6,0},{1,7},{3,5},{5,3},{7,1},{8,14},{10,12},{12... | collective-permute-start | bytes 294920 | tf_op jit(solution)/shard_map/ppermute | solution.py:448
  41.5 1.5 %collective-permute-start.23 = (f32[96,256]{1,0:T(8,128)S(1)}, f32[96,256]{1,0:T(8,128)S(1)}, u32[]{:S(2)}, u32[]{:S(2)}) collective-permute-start(f32[96,256]{1,0:T(8,128)S(1)} %get-tuple-element.28.refs_1_.refs_3_), channel_id=1, source_target_pairs={{0,4},{2,6},{4,0},{6,2},{1,5},{3,7},{5,1},{7,3},{8,12},{10,14},{12... | collective-permute-start | bytes 294920 | tf_op jit(solution)/shard_map/ppermute | solution.py:448
  43.5 2.7 %collective-permute-done.24.refs_4_ = f32[96,256]{1,0:T(8,128)S(1)} collective-permute-done((f32[96,256]{1,0:T(8,128)S(1)}, f32[96,256]{1,0:T(8,128)S(1)}, u32[]{:S(2)}, u32[]{:S(2)}) %collective-permute-start.24) | collective-permute-done | bytes 98336 | tf_op jit(solution)/shard_map/ppermute | solution.py:448
  46.2 1.5 %collective-permute-done.23.refs_3_ = f32[96,256]{1,0:T(8,128)S(1)} collective-permute-done((f32[96,256]{1,0:T(8,128)S(1)}, f32[96,256]{1,0:T(8,128)S(1)}, u32[]{:S(2)}, u32[]{:S(2)}) %collective-permute-start.23) | collective-permute-done | bytes 98336 | tf_op jit(solution)/shard_map/ppermute | solution.py:448
  48.3 2.5 %shard_map.95.refs_6_ = f32[96,256]{1,0:T(8,128)S(1)} custom-call(s32[7]{0:T(128)S(1)} %bitcast.45, f32[96,256]{1,0:T(8,128)S(1)} %bitcast.39, f32[96,256]{1,0:T(8,128)S(1)} %collective-permute-done.refs_2_, f32[96,256]{1,0:T(8,128)S(1)} %collective-permute-done.1.refs_3_, f32[96,256]{1,0:T(8,128)S(1)} %collective-permute-done.2.refs_4_, ...), custom_call_target="tpu_custom_call" | custom-call | flops 528482304 | bytes 2883584 | tf_op jit(solution)/shard_map/pallas_call | solution.py:121
  50.8 5.1 %all-to-all-start = ((f32[32,3,96]{2,1,0:T(4,128)}), f32[32,3,96]{2,1,0:T(4,128)S(1)}, u32[]{:S(2)}, u32[]{:S(2)}) async-start(f32[32,3,96]{2,1,0:T(4,128)} %get-tuple-element.27), calls=%async_computation | async-start | bytes 131072 | tf_op jit(solution)/shard_map/all_to_all | solution.py:521
  55.9 2.5 %shard_map.93 = (f32[96,256]{1,0:T(8,128)S(1)}, bf16[2,7,256,256]{3,2,1,0:T(8,128)(2,1)S(1)}) custom-call(s32[7]{0:T(128)S(1)} %bitcast.46, f32[96,256]{1,0:T(8,128)S(1)} %get-tuple-element.24.refs_0_.refs_1_.refs_2_, f32[96,256]{1,0:T(8,128)S(1)} %collective-permute-done.11.refs_2_, f32[96,256]{1,0:T(8,128)S(1)} %collective-permute-done.12.refs_3_, ...), custom_call_target="tpu_custom_call" | custom-call | flops 528482304 | bytes 2883584 | tf_op jit(solution)/shard_map/pallas_call | solution.py:121
  59.1 3.5 %shard_map.94 = (f32[96,256]{1,0:T(8,128)S(1)}, f32[96,256]{1,0:T(8,128)S(1)}) custom-call(s32[7]{0:T(128)S(1)} %bitcast.47, f32[96,256]{1,0:T(8,128)S(1)} %get-tuple-element.28.refs_1_.refs_3_, f32[96,256]{1,0:T(8,128)S(1)} %collective-permute-done.22.refs_2_, f32[96,256]{1,0:T(8,128)S(1)} %collective-permute-done.23.refs_3_, ...), custom_call_target="tpu_custom_call" | custom-call | flops 528482304 | bytes 4980736 | tf_op jit(solution)/shard_map/pallas_call | solution.py:121
  65.7 13.9 %all_to_all.10.refs_0_ = f32[16,16,128]{2,1,0:T(8,128)S(1)} all-to-all(f32[16,16,128]{2,1,0:T(8,128)S(1)} %add.65), channel_id=1, replica_groups=mesh['row'=4,'chip'=4,'core'=2] {'row','chip'}, dimensions={0} | all-to-all | bytes 262144 | tf_op jit(solution)/shard_map/all_to_all | solution.py:557
  (74 shorter events, 16.0 us)
Async XLA Ops:
  3.0 10.1 %collective-permute-start.7 = (f32[4,96,256]{2,1,0:T(8,128)S(1)}, f32[4,96,256]{2,1,0:T(8,128)S(1)}, u32[]{:S(2)}, u32[]{:S(2)}) collective-permute-start(f32[4,96,256]{2,1,0:T(8,128)S(1)} %get-tuple-element.23), channel_id=1, source_target_pairs={{0,1},{1,0},{2,3},{3,2},{4,5},{5,4},{6,7},{7,6},{8,9},{9,8},{10,11... | collective-permute-start | bytes 1179656 | tf_op jit(solution)/shard_map/ppermute | solution.py:455
  3.6 7.0 %collective-permute-start.2 = (f32[96,256]{1,0:T(8,128)S(1)}, f32[96,256]{1,0:T(8,128)S(1)}, u32[]{:S(2)}, u32[]{:S(2)}) collective-permute-start(f32[96,256]{1,0:T(8,128)S(1)} %bitcast.33), channel_id=1, source_target_pairs={{0,6},{2,4},{4,2},{6,0},{1,7},{3,5},{5,3},{7,1},{8,14},{10,12},{12... | collective-permute-start | bytes 294920 | tf_op jit(solution)/shard_map/ppermute | solution.py:448
  7.1 5.5 %collective-permute-start.1 = (f32[96,256]{1,0:T(8,128)S(1)}, f32[96,256]{1,0:T(8,128)S(1)}, u32[]{:S(2)}, u32[]{:S(2)}) collective-permute-start(f32[96,256]{1,0:T(8,128)S(1)} %bitcast.34), channel_id=1, source_target_pairs={{0,4},{2,6},{4,0},{6,2},{1,5},{3,7},{5,1},{7,3},{8,12},{10,14},{12... | collective-permute-start | bytes 294920 | tf_op jit(solution)/shard_map/ppermute | solution.py:448
  7.6 5.2 %collective-permute-start = (f32[96,256]{1,0:T(8,128)S(1)}, f32[96,256]{1,0:T(8,128)S(1)}, u32[]{:S(2)}, u32[]{:S(2)}) collective-permute-start(f32[96,256]{1,0:T(8,128)S(1)} %bitcast.35), channel_id=1, source_target_pairs={{0,2},{2,0},{4,6},{6,4},{1,3},{3,1},{5,7},{7,5},{8,10},{10,8},{12,... | collective-permute-start | bytes 294920 | tf_op jit(solution)/shard_map/ppermute | solution.py:448
  7.7 7.2 %collective-permute-start.3 = (f32[96,256]{1,0:T(8,128)S(1)}, f32[96,256]{1,0:T(8,128)S(1)}, u32[]{:S(2)}, u32[]{:S(2)}) collective-permute-start(f32[96,256]{1,0:T(8,128)S(1)} %bitcast.36), channel_id=1, source_target_pairs={{0,1},{1,0},{2,3},{3,2},{4,5},{5,4},{6,7},{7,6},{8,9},{9,8},{10,11... | collective-permute-start | bytes 294920 | tf_op jit(solution)/shard_map/ppermute | solution.py:452
  10.5 5.8 %collective-permute-start.6 = (f32[96,256]{1,0:T(8,128)S(1)}, f32[96,256]{1,0:T(8,128)S(1)}, u32[]{:S(2)}, u32[]{:S(2)}) collective-permute-start(f32[96,256]{1,0:T(8,128)S(1)} %collective-permute-done.2.refs_4_), channel_id=1, source_target_pairs={{0,1},{1,0},{2,3},{3,2},{4,5},{5,4},{6,7},{7,6},{8,9},{9,8},{10,11... | collective-permute-start | bytes 294920 | tf_op jit(solution)/shard_map/ppermute | solution.py:452
  13.2 6.5 %collective-permute-start.10 = (f32[96,256]{1,0:T(8,128)S(1)}, f32[96,256]{1,0:T(8,128)S(1)}, u32[]{:S(2)}, u32[]{:S(2)}) collective-permute-start(f32[96,256]{1,0:T(8,128)S(1)} %get-tuple-element.44), channel_id=1, source_target_pairs={{0,6},{2,4},{4,2},{6,0},{1,7},{3,5},{5,3},{7,1},{8,14},{10,12},{12... | collective-permute-start | bytes 294920 | tf_op jit(solution)/shard_map/ppermute | solution.py:459
  15.0 6.2 %collective-permute-start.9 = (f32[96,256]{1,0:T(8,128)S(1)}, f32[96,256]{1,0:T(8,128)S(1)}, u32[]{:S(2)}, u32[]{:S(2)}) collective-permute-start(f32[96,256]{1,0:T(8,128)S(1)} %get-tuple-element.45), channel_id=1, source_target_pairs={{0,4},{2,6},{4,0},{6,2},{1,5},{3,7},{5,1},{7,3},{8,12},{10,14},{12... | collective-permute-start | bytes 294920 | tf_op jit(solution)/shard_map/ppermute | solution.py:459
  16.4 4.8 %collective-permute-start.8 = (f32[96,256]{1,0:T(8,128)S(1)}, f32[96,256]{1,0:T(8,128)S(1)}, u32[]{:S(2)}, u32[]{:S(2)}) collective-permute-start(f32[96,256]{1,0:T(8,128)S(1)} %get-tuple-element.46), channel_id=1, source_target_pairs={{0,2},{2,0},{4,6},{6,4},{1,3},{3,1},{5,7},{7,5},{8,10},{10,8},{12,... | collective-permute-start | bytes 294920 | tf_op jit(solution)/shard_map/ppermute | solution.py:459
  22.4 8.8 %collective-permute-start.18 = (f32[4,96,256]{2,1,0:T(8,128)S(1)}, f32[4,96,256]{2,1,0:T(8,128)S(1)}, u32[]{:S(2)}, u32[]{:S(2)}) collective-permute-start(f32[4,96,256]{2,1,0:T(8,128)S(1)} %get-tuple-element.26), channel_id=1, source_target_pairs={{0,1},{1,0},{2,3},{3,2},{4,5},{5,4},{6,7},{7,6},{8,9},{9,8},{10,11... | collective-permute-start | bytes 1179656 | tf_op jit(solution)/shard_map/ppermute | solution.py:455
  22.4 6.6 %collective-permute-start.13 = (f32[96,256]{1,0:T(8,128)S(1)}, f32[96,256]{1,0:T(8,128)S(1)}, u32[]{:S(2)}, u32[]{:S(2)}) collective-permute-start(f32[96,256]{1,0:T(8,128)S(1)} %get-tuple-element.24.refs_0_.refs_1_.refs_2_), channel_id=1, source_target_pairs={{0,6},{2,4},{4,2},{6,0},{1,7},{3,5},{5,3},{7,1},{8,14},{10,12},{12... | collective-permute-start | bytes 294920 | tf_op jit(solution)/shard_map/ppermute | solution.py:448
  24.0 6.6 %collective-permute-start.12 = (f32[96,256]{1,0:T(8,128)S(1)}, f32[96,256]{1,0:T(8,128)S(1)}, u32[]{:S(2)}, u32[]{:S(2)}) collective-permute-start(f32[96,256]{1,0:T(8,128)S(1)} %get-tuple-element.24.refs_0_.refs_1_.refs_2_), channel_id=1, source_target_pairs={{0,4},{2,6},{4,0},{6,2},{1,5},{3,7},{5,1},{7,3},{8,12},{10,14},{12... | collective-permute-start | bytes 294920 | tf_op jit(solution)/shard_map/ppermute | solution.py:448
  25.5 5.2 %collective-permute-start.11 = (f32[96,256]{1,0:T(8,128)S(1)}, f32[96,256]{1,0:T(8,128)S(1)}, u32[]{:S(2)}, u32[]{:S(2)}) collective-permute-start(f32[96,256]{1,0:T(8,128)S(1)} %get-tuple-element.24.refs_0_.refs_1_.refs_2_), channel_id=1, source_target_pairs={{0,2},{2,0},{4,6},{6,4},{1,3},{3,1},{5,7},{7,5},{8,10},{10,8},{12,... | collective-permute-start | bytes 294920 | tf_op jit(solution)/shard_map/ppermute | solution.py:448
  26.0 6.8 %collective-permute-start.14 = (f32[96,256]{1,0:T(8,128)S(1)}, f32[96,256]{1,0:T(8,128)S(1)}, u32[]{:S(2)}, u32[]{:S(2)}) collective-permute-start(f32[96,256]{1,0:T(8,128)S(1)} %get-tuple-element.24.refs_0_.refs_1_.refs_2_), channel_id=1, source_target_pairs={{0,1},{1,0},{2,3},{3,2},{4,5},{5,4},{6,7},{7,6},{8,9},{9,8},{10,11... | collective-permute-start | bytes 294920 | tf_op jit(solution)/shard_map/ppermute | solution.py:452
  29.1 5.2 %collective-permute-start.17 = (f32[96,256]{1,0:T(8,128)S(1)}, f32[96,256]{1,0:T(8,128)S(1)}, u32[]{:S(2)}, u32[]{:S(2)}) collective-permute-start(f32[96,256]{1,0:T(8,128)S(1)} %collective-permute-done.13.refs_4_), channel_id=1, source_target_pairs={{0,1},{1,0},{2,3},{3,2},{4,5},{5,4},{6,7},{7,6},{8,9},{9,8},{10,11... | collective-permute-start | bytes 294920 | tf_op jit(solution)/shard_map/ppermute | solution.py:452
  31.2 6.3 %collective-permute-start.21 = (f32[96,256]{1,0:T(8,128)S(1)}, f32[96,256]{1,0:T(8,128)S(1)}, u32[]{:S(2)}, u32[]{:S(2)}) collective-permute-start(f32[96,256]{1,0:T(8,128)S(1)} %get-tuple-element.40), channel_id=1, source_target_pairs={{0,6},{2,4},{4,2},{6,0},{1,7},{3,5},{5,3},{7,1},{8,14},{10,12},{12... | collective-permute-start | bytes 294920 | tf_op jit(solution)/shard_map/ppermute | solution.py:459
  32.8 6.2 %collective-permute-start.20 = (f32[96,256]{1,0:T(8,128)S(1)}, f32[96,256]{1,0:T(8,128)S(1)}, u32[]{:S(2)}, u32[]{:S(2)}) collective-permute-start(f32[96,256]{1,0:T(8,128)S(1)} %get-tuple-element.41), channel_id=1, source_target_pairs={{0,4},{2,6},{4,0},{6,2},{1,5},{3,7},{5,1},{7,3},{8,12},{10,14},{12... | collective-permute-start | bytes 294920 | tf_op jit(solution)/shard_map/ppermute | solution.py:459
  40.0 6.2 %collective-permute-start.24 = (f32[96,256]{1,0:T(8,128)S(1)}, f32[96,256]{1,0:T(8,128)S(1)}, u32[]{:S(2)}, u32[]{:S(2)}) collective-permute-start(f32[96,256]{1,0:T(8,128)S(1)} %get-tuple-element.28.refs_1_.refs_3_), channel_id=1, source_target_pairs={{0,6},{2,4},{4,2},{6,0},{1,7},{3,5},{5,3},{7,1},{8,14},{10,12},{12... | collective-permute-start | bytes 294920 | tf_op jit(solution)/shard_map/ppermute | solution.py:448
  41.5 6.2 %collective-permute-start.23 = (f32[96,256]{1,0:T(8,128)S(1)}, f32[96,256]{1,0:T(8,128)S(1)}, u32[]{:S(2)}, u32[]{:S(2)}) collective-permute-start(f32[96,256]{1,0:T(8,128)S(1)} %get-tuple-element.28.refs_1_.refs_3_), channel_id=1, source_target_pairs={{0,4},{2,6},{4,0},{6,2},{1,5},{3,7},{5,1},{7,3},{8,12},{10,14},{12... | collective-permute-start | bytes 294920 | tf_op jit(solution)/shard_map/ppermute | solution.py:448
  43.5 15.5 %collective-permute-start.25 = (f32[96,256]{1,0:T(8,128)S(1)}, f32[96,256]{1,0:T(8,128)S(1)}, u32[]{:S(2)}, u32[]{:S(2)}) collective-permute-start(f32[96,256]{1,0:T(8,128)S(1)} %get-tuple-element.28.refs_1_.refs_3_), channel_id=1, source_target_pairs={{0,1},{1,0},{2,3},{3,2},{4,5},{5,4},{6,7},{7,6},{8,9},{9,8},{10,11... | collective-permute-start | bytes 294920 | tf_op jit(solution)/shard_map/ppermute | solution.py:452
  46.2 12.8 %collective-permute-start.28 = (f32[96,256]{1,0:T(8,128)S(1)}, f32[96,256]{1,0:T(8,128)S(1)}, u32[]{:S(2)}, u32[]{:S(2)}) collective-permute-start(f32[96,256]{1,0:T(8,128)S(1)} %collective-permute-done.24.refs_4_), channel_id=1, source_target_pairs={{0,1},{1,0},{2,3},{3,2},{4,5},{5,4},{6,7},{7,6},{8,9},{9,8},{10,11... | collective-permute-start | bytes 294920 | tf_op jit(solution)/shard_map/ppermute | solution.py:452
  47.8 11.3 %collective-permute-start.27 = (f32[96,256]{1,0:T(8,128)S(1)}, f32[96,256]{1,0:T(8,128)}, u32[]{:S(2)}, u32[]{:S(2)}) collective-permute-start(f32[96,256]{1,0:T(8,128)S(1)} %collective-permute-done.23.refs_3_), channel_id=1, source_target_pairs={{0,1},{1,0},{2,3},{3,2},{4,5},{5,4},{6,7},{7,6},{8,9},{9,8},{10,11... | collective-permute-start | bytes 294920 | tf_op jit(solution)/shard_map/ppermute | solution.py:452
  47.8 11.3 %collective-permute-start.26 = (f32[96,256]{1,0:T(8,128)S(1)}, f32[96,256]{1,0:T(8,128)}, u32[]{:S(2)}, u32[]{:S(2)}) collective-permute-start(f32[96,256]{1,0:T(8,128)S(1)} %collective-permute-done.22.refs_2_), channel_id=1, source_target_pairs={{0,1},{1,0},{2,3},{3,2},{4,5},{5,4},{6,7},{7,6},{8,9},{9,8},{10,11... | collective-permute-start | bytes 294920 | tf_op jit(solution)/shard_map/ppermute | solution.py:452
  50.8 12.5 %all-to-all-start = ((f32[32,3,96]{2,1,0:T(4,128)}), f32[32,3,96]{2,1,0:T(4,128)S(1)}, u32[]{:S(2)}, u32[]{:S(2)}) async-start(f32[32,3,96]{2,1,0:T(4,128)} %get-tuple-element.27), calls=%async_computation | async-start | bytes 131072 | tf_op jit(solution)/shard_map/all_to_all | solution.py:521
  (17 other events, 109.3 us)

commit v6 on v5

--- a/solution.py
+++ b/solution.py
@@ -269,11 +269,7 @@
     *split_tiles, held = more
     rows = out.shape[0]
     for k, block in enumerate(gathered):
-        value = block[...]
-        high, rest = split(value)
-        middle = value - high.astype(F32)
-        held[k, 0:rows], held[k, rows : 2 * rows] = high, rest
-        held[k, 2 * rows : 3 * rows] = (middle - rest.astype(F32)).astype(BF16)
+        held[k, 0:rows], held[k, rows : 2 * rows] = split(block[...])
     held[len(gathered)] = jnp.zeros(held.shape[1:], BF16)
     first = second = None
     work = [(seat, tiles[k]) for k, seat in enumerate(seats(way, cols))]
@@ -286,8 +282,7 @@
         two = lax.dot_general(three[: 2 * rows], low, NT, preferred_element_type=F32)
         first = one if first is None else first + one
         second = two if second is None else second + two
-    small = first[2 * rows :] + second[rows:]
-    out[...] = first[:rows] + (first[rows : 2 * rows] + second[:rows] + small)
+    out[...] = first[:rows] + (first[rows:] + second[:rows] + second[rows:])
 
 
 def half_product(both, pair):
@@ -503,7 +498,7 @@
             [cols],
             [gathered, Far(ndiag), ntiles],
             scratch=[
-                jax.ShapeDtypeStruct((2 * chips + 1, 3 * count, size), BF16)
+                held
             ],
             flops=2 * n * unit,
         )

time: 80.8 us -> 80.7 us (level)
  no operation moved by 1% of the time
where the time goes in v6:
time: 80.7 us; the launch traced here: 80.3 us
  starting transfers between devices  25.5 us (32%)
  waiting for transfers between devices  21.3 us (26%)
  Pallas kernels  18.1 us (22%)
  blocking collectives  13.8 us (17%)
  between operations  0.89 us (1%)
    pallas_call x12, Pallas kernels, call(): pl.pallas_call(kernel, out_shape=outs, in_specs=specs, out_specs=[vmem] *...  18.1 us
    ppermute x9, waiting for transfers between devices, gather(): same[way.source(k)] = lax.ppermute(value, 'chip', way.pairs(k))  14 us
    all_to_all x1, blocking collectives, on_device(): lax.all_to_all(keep + received, ('row', 'chip'), 0, 0, tiled=True)  13.8 us
    ppermute x9, starting transfers between devices, gather(): same[way.source(k)] = lax.ppermute(value, 'chip', way.pairs(k))  11.2 us
    ppermute x6, starting transfers between devices, scatter(): added.append(lax.ppermute(sums[k], 'chip', way.pairs(k)))  7.11 us
    ppermute x6, waiting for transfers between devices, scatter(): added.append(lax.ppermute(sums[k], 'chip', way.pairs(k)))  5.33 us
    all_to_all x1, starting transfers between devices, on_device(): sums = lax.all_to_all(sums, ALL, 0, 0, tiled=True)  5.08 us
  transfers between devices with their start and end apart: 31, of which 13 were waited for; matrix products, arithmetic and copies ran while one was open for 0% of the time, Pallas kernels for 15%

profile of v6, /device:TPU:0, one launch (start us, length us, event | category | flops | bytes accessed | tf_op | source)
XLA Modules:
  0.0 80.3 jit_solution(16242426038405241645)
XLA Ops:
  0.7 2.3 %shard_map.87 = (f32[4,96,256]{2,1,0:T(8,128)S(1)}, f32[4,96,256]{2,1,0:T(8,128)S(1)}, bf16[2,7,256,256]{3,2,1,0:T(8,128)(2,1)S(1)}) custom-call(s32[7]{0:T(128)} %bitcast.41, f32[96,256]{1,0:T(8,128)} %bitcast.32, f32[7,256,256]{2,1,0:T(8,128)} %bitcast.27), custom_call_target="tpu_custom_call" | custom-call | flops 264241152 | bytes 1933340 | tf_op jit(solution)/shard_map/pallas_call | solution.py:121
  3.6 3.5 %collective-permute-start.2 = (f32[96,256]{1,0:T(8,128)S(1)}, f32[96,256]{1,0:T(8,128)S(1)}, u32[]{:S(2)}, u32[]{:S(2)}) collective-permute-start(f32[96,256]{1,0:T(8,128)S(1)} %bitcast.33), channel_id=1, source_target_pairs={{0,6},{2,4},{4,2},{6,0},{1,7},{3,5},{5,3},{7,1},{8,14},{10,12},{12... | collective-permute-start | bytes 294920 | tf_op jit(solution)/shard_map/ppermute | solution.py:443
  7.7 2.8 %collective-permute-done.2.refs_4_ = f32[96,256]{1,0:T(8,128)S(1)} collective-permute-done((f32[96,256]{1,0:T(8,128)S(1)}, f32[96,256]{1,0:T(8,128)S(1)}, u32[]{:S(2)}, u32[]{:S(2)}) %collective-permute-start.2) | collective-permute-done | bytes 98336 | tf_op jit(solution)/shard_map/ppermute | solution.py:443
  10.5 2.0 %collective-permute-done.1.refs_3_ = f32[96,256]{1,0:T(8,128)S(1)} collective-permute-done((f32[96,256]{1,0:T(8,128)S(1)}, f32[96,256]{1,0:T(8,128)S(1)}, u32[]{:S(2)}, u32[]{:S(2)}) %collective-permute-start.1) | collective-permute-done | bytes 98336 | tf_op jit(solution)/shard_map/ppermute | solution.py:443
  13.2 1.8 %collective-permute-start.10 = (f32[96,256]{1,0:T(8,128)S(1)}, f32[96,256]{1,0:T(8,128)S(1)}, u32[]{:S(2)}, u32[]{:S(2)}) collective-permute-start(f32[96,256]{1,0:T(8,128)S(1)} %get-tuple-element.44), channel_id=1, source_target_pairs={{0,6},{2,4},{4,2},{6,0},{1,7},{3,5},{5,3},{7,1},{8,14},{10,12},{12... | collective-permute-start | bytes 294920 | tf_op jit(solution)/shard_map/ppermute | solution.py:454
  15.0 1.4 %collective-permute-start.9 = (f32[96,256]{1,0:T(8,128)S(1)}, f32[96,256]{1,0:T(8,128)S(1)}, u32[]{:S(2)}, u32[]{:S(2)}) collective-permute-start(f32[96,256]{1,0:T(8,128)S(1)} %get-tuple-element.45), channel_id=1, source_target_pairs={{0,4},{2,6},{4,0},{6,2},{1,5},{3,7},{5,1},{7,3},{8,12},{10,14},{12... | collective-permute-start | bytes 294920 | tf_op jit(solution)/shard_map/ppermute | solution.py:454
  19.7 1.5 %collective-permute-done.9.refs_7_ = f32[96,256]{1,0:T(8,128)S(1)} collective-permute-done((f32[96,256]{1,0:T(8,128)S(1)}, f32[96,256]{1,0:T(8,128)S(1)}, u32[]{:S(2)}, u32[]{:S(2)}) %collective-permute-start.9) | collective-permute-done | bytes 98336 | tf_op jit(solution)/shard_map/ppermute | solution.py:454
  22.4 1.6 %collective-permute-start.13 = (f32[96,256]{1,0:T(8,128)S(1)}, f32[96,256]{1,0:T(8,128)S(1)}, u32[]{:S(2)}, u32[]{:S(2)}) collective-permute-start(f32[96,256]{1,0:T(8,128)S(1)} %get-tuple-element.24.refs_0_.refs_1_.refs_2_), channel_id=1, source_target_pairs={{0,6},{2,4},{4,2},{6,0},{1,7},{3,5},{5,3},{7,1},{8,14},{10,12},{12... | collective-permute-start | bytes 294920 | tf_op jit(solution)/shard_map/ppermute | solution.py:443
  24.0 1.5 %collective-permute-start.12 = (f32[96,256]{1,0:T(8,128)S(1)}, f32[96,256]{1,0:T(8,128)S(1)}, u32[]{:S(2)}, u32[]{:S(2)}) collective-permute-start(f32[96,256]{1,0:T(8,128)S(1)} %get-tuple-element.24.refs_0_.refs_1_.refs_2_), channel_id=1, source_target_pairs={{0,4},{2,6},{4,0},{6,2},{1,5},{3,7},{5,1},{7,3},{8,12},{10,14},{12... | collective-permute-start | bytes 294920 | tf_op jit(solution)/shard_map/ppermute | solution.py:443
  26.0 3.1 %collective-permute-done.13.refs_4_ = f32[96,256]{1,0:T(8,128)S(1)} collective-permute-done((f32[96,256]{1,0:T(8,128)S(1)}, f32[96,256]{1,0:T(8,128)S(1)}, u32[]{:S(2)}, u32[]{:S(2)}) %collective-permute-start.13) | collective-permute-done | bytes 98336 | tf_op jit(solution)/shard_map/ppermute | solution.py:443
  29.1 1.6 %collective-permute-done.12.refs_3_ = f32[96,256]{1,0:T(8,128)S(1)} collective-permute-done((f32[96,256]{1,0:T(8,128)S(1)}, f32[96,256]{1,0:T(8,128)S(1)}, u32[]{:S(2)}, u32[]{:S(2)}) %collective-permute-start.12) | collective-permute-done | bytes 98336 | tf_op jit(solution)/shard_map/ppermute | solution.py:443
  31.2 1.6 %collective-permute-start.21 = (f32[96,256]{1,0:T(8,128)S(1)}, f32[96,256]{1,0:T(8,128)S(1)}, u32[]{:S(2)}, u32[]{:S(2)}) collective-permute-start(f32[96,256]{1,0:T(8,128)S(1)} %get-tuple-element.40), channel_id=1, source_target_pairs={{0,6},{2,4},{4,2},{6,0},{1,7},{3,5},{5,3},{7,1},{8,14},{10,12},{12... | collective-permute-start | bytes 294920 | tf_op jit(solution)/shard_map/ppermute | solution.py:454
  32.8 1.5 %collective-permute-start.20 = (f32[96,256]{1,0:T(8,128)S(1)}, f32[96,256]{1,0:T(8,128)S(1)}, u32[]{:S(2)}, u32[]{:S(2)}) collective-permute-start(f32[96,256]{1,0:T(8,128)S(1)} %get-tuple-element.41), channel_id=1, source_target_pairs={{0,4},{2,6},{4,0},{6,2},{1,5},{3,7},{5,1},{7,3},{8,12},{10,14},{12... | collective-permute-start | bytes 294920 | tf_op jit(solution)/shard_map/ppermute | solution.py:454
  35.2 1.3 %shard_map.91.refs_2_ = f32[96,256]{1,0:T(8,128)S(1)} custom-call(s32[7]{0:T(128)S(1)} %bitcast.44, f32[96,256]{1,0:T(8,128)S(1)} %get-tuple-element.24.refs_0_.refs_1_.refs_2_, f32[96,256]{1,0:T(8,128)S(1)} %collective-permute-done.11.refs_2_, f32[96,256]{1,0:T(8,128)S(1)} %collective-permute-done.12.refs_3_, ...), custom_call_target="tpu_custom_call" | custom-call | flops 264241152 | bytes 2621440 | tf_op jit(solution)/shard_map/pallas_call | solution.py:121
  37.5 1.5 %collective-permute-done.20.refs_5_ = f32[96,256]{1,0:T(8,128)S(1)} collective-permute-done((f32[96,256]{1,0:T(8,128)S(1)}, f32[96,256]{1,0:T(8,128)S(1)}, u32[]{:S(2)}, u32[]{:S(2)}) %collective-permute-start.20) | collective-permute-done | bytes 98336 | tf_op jit(solution)/shard_map/ppermute | solution.py:454
  40.0 1.5 %collective-permute-start.24 = (f32[96,256]{1,0:T(8,128)S(1)}, f32[96,256]{1,0:T(8,128)S(1)}, u32[]{:S(2)}, u32[]{:S(2)}) collective-permute-start(f32[96,256]{1,0:T(8,128)S(1)} %get-tuple-element.28.refs_1_.refs_3_), channel_id=1, source_target_pairs={{0,6},{2,4},{4,2},{6,0},{1,7},{3,5},{5,3},{7,1},{8,14},{10,12},{12... | collective-permute-start | bytes 294920 | tf_op jit(solution)/shard_map/ppermute | solution.py:443
  41.5 1.5 %collective-permute-start.23 = (f32[96,256]{1,0:T(8,128)S(1)}, f32[96,256]{1,0:T(8,128)S(1)}, u32[]{:S(2)}, u32[]{:S(2)}) collective-permute-start(f32[96,256]{1,0:T(8,128)S(1)} %get-tuple-element.28.refs_1_.refs_3_), channel_id=1, source_target_pairs={{0,4},{2,6},{4,0},{6,2},{1,5},{3,7},{5,1},{7,3},{8,12},{10,14},{12... | collective-permute-start | bytes 294920 | tf_op jit(solution)/shard_map/ppermute | solution.py:443
  43.5 2.7 %collective-permute-done.24.refs_4_ = f32[96,256]{1,0:T(8,128)S(1)} collective-permute-done((f32[96,256]{1,0:T(8,128)S(1)}, f32[96,256]{1,0:T(8,128)S(1)}, u32[]{:S(2)}, u32[]{:S(2)}) %collective-permute-start.24) | collective-permute-done | bytes 98336 | tf_op jit(solution)/shard_map/ppermute | solution.py:443
  46.2 1.5 %collective-permute-done.23.refs_3_ = f32[96,256]{1,0:T(8,128)S(1)} collective-permute-done((f32[96,256]{1,0:T(8,128)S(1)}, f32[96,256]{1,0:T(8,128)S(1)}, u32[]{:S(2)}, u32[]{:S(2)}) %collective-permute-start.23) | collective-permute-done | bytes 98336 | tf_op jit(solution)/shard_map/ppermute | solution.py:443
  48.3 2.5 %shard_map.95.refs_6_ = f32[96,256]{1,0:T(8,128)S(1)} custom-call(s32[7]{0:T(128)S(1)} %bitcast.45, f32[96,256]{1,0:T(8,128)S(1)} %bitcast.39, f32[96,256]{1,0:T(8,128)S(1)} %collective-permute-done.refs_2_, f32[96,256]{1,0:T(8,128)S(1)} %collective-permute-done.1.refs_3_, f32[96,256]{1,0:T(8,128)S(1)} %collective-permute-done.2.refs_4_, ...), custom_call_target="tpu_custom_call" | custom-call | flops 528482304 | bytes 2883584 | tf_op jit(solution)/shard_map/pallas_call | solution.py:121
  50.7 5.1 %all-to-all-start = ((f32[32,3,96]{2,1,0:T(4,128)}), f32[32,3,96]{2,1,0:T(4,128)S(1)}, u32[]{:S(2)}, u32[]{:S(2)}) async-start(f32[32,3,96]{2,1,0:T(4,128)} %get-tuple-element.27), calls=%async_computation | async-start | bytes 131072 | tf_op jit(solution)/shard_map/all_to_all | solution.py:516
  55.8 2.4 %shard_map.93 = (f32[96,256]{1,0:T(8,128)S(1)}, bf16[2,7,256,256]{3,2,1,0:T(8,128)(2,1)S(1)}) custom-call(s32[7]{0:T(128)S(1)} %bitcast.46, f32[96,256]{1,0:T(8,128)S(1)} %get-tuple-element.24.refs_0_.refs_1_.refs_2_, f32[96,256]{1,0:T(8,128)S(1)} %collective-permute-done.11.refs_2_, f32[96,256]{1,0:T(8,128)S(1)} %collective-permute-done.12.refs_3_, ...), custom_call_target="tpu_custom_call" | custom-call | flops 528482304 | bytes 2883584 | tf_op jit(solution)/shard_map/pallas_call | solution.py:121
  59.0 3.5 %shard_map.94 = (f32[96,256]{1,0:T(8,128)S(1)}, f32[96,256]{1,0:T(8,128)S(1)}) custom-call(s32[7]{0:T(128)S(1)} %bitcast.47, f32[96,256]{1,0:T(8,128)S(1)} %get-tuple-element.28.refs_1_.refs_3_, f32[96,256]{1,0:T(8,128)S(1)} %collective-permute-done.22.refs_2_, f32[96,256]{1,0:T(8,128)S(1)} %collective-permute-done.23.refs_3_, ...), custom_call_target="tpu_custom_call" | custom-call | flops 528482304 | bytes 4980736 | tf_op jit(solution)/shard_map/pallas_call | solution.py:121
  65.7 13.8 %all_to_all.10.refs_0_ = f32[16,16,128]{2,1,0:T(8,128)S(1)} all-to-all(f32[16,16,128]{2,1,0:T(8,128)S(1)} %add.65), channel_id=1, replica_groups=mesh['row'=4,'chip'=4,'core'=2] {'row','chip'}, dimensions={0} | all-to-all | bytes 262144 | tf_op jit(solution)/shard_map/all_to_all | solution.py:552
  (74 shorter events, 16.1 us)
Async XLA Ops:
  3.0 10.1 %collective-permute-start.7 = (f32[4,96,256]{2,1,0:T(8,128)S(1)}, f32[4,96,256]{2,1,0:T(8,128)S(1)}, u32[]{:S(2)}, u32[]{:S(2)}) collective-permute-start(f32[4,96,256]{2,1,0:T(8,128)S(1)} %get-tuple-element.23), channel_id=1, source_target_pairs={{0,1},{1,0},{2,3},{3,2},{4,5},{5,4},{6,7},{7,6},{8,9},{9,8},{10,11... | collective-permute-start | bytes 1179656 | tf_op jit(solution)/shard_map/ppermute | solution.py:450
  3.6 7.0 %collective-permute-start.2 = (f32[96,256]{1,0:T(8,128)S(1)}, f32[96,256]{1,0:T(8,128)S(1)}, u32[]{:S(2)}, u32[]{:S(2)}) collective-permute-start(f32[96,256]{1,0:T(8,128)S(1)} %bitcast.33), channel_id=1, source_target_pairs={{0,6},{2,4},{4,2},{6,0},{1,7},{3,5},{5,3},{7,1},{8,14},{10,12},{12... | collective-permute-start | bytes 294920 | tf_op jit(solution)/shard_map/ppermute | solution.py:443
  7.1 5.5 %collective-permute-start.1 = (f32[96,256]{1,0:T(8,128)S(1)}, f32[96,256]{1,0:T(8,128)S(1)}, u32[]{:S(2)}, u32[]{:S(2)}) collective-permute-start(f32[96,256]{1,0:T(8,128)S(1)} %bitcast.34), channel_id=1, source_target_pairs={{0,4},{2,6},{4,0},{6,2},{1,5},{3,7},{5,1},{7,3},{8,12},{10,14},{12... | collective-permute-start | bytes 294920 | tf_op jit(solution)/shard_map/ppermute | solution.py:443
  7.6 5.2 %collective-permute-start = (f32[96,256]{1,0:T(8,128)S(1)}, f32[96,256]{1,0:T(8,128)S(1)}, u32[]{:S(2)}, u32[]{:S(2)}) collective-permute-start(f32[96,256]{1,0:T(8,128)S(1)} %bitcast.35), channel_id=1, source_target_pairs={{0,2},{2,0},{4,6},{6,4},{1,3},{3,1},{5,7},{7,5},{8,10},{10,8},{12,... | collective-permute-start | bytes 294920 | tf_op jit(solution)/shard_map/ppermute | solution.py:443
  7.7 7.2 %collective-permute-start.3 = (f32[96,256]{1,0:T(8,128)S(1)}, f32[96,256]{1,0:T(8,128)S(1)}, u32[]{:S(2)}, u32[]{:S(2)}) collective-permute-start(f32[96,256]{1,0:T(8,128)S(1)} %bitcast.36), channel_id=1, source_target_pairs={{0,1},{1,0},{2,3},{3,2},{4,5},{5,4},{6,7},{7,6},{8,9},{9,8},{10,11... | collective-permute-start | bytes 294920 | tf_op jit(solution)/shard_map/ppermute | solution.py:447
  10.5 5.8 %collective-permute-start.6 = (f32[96,256]{1,0:T(8,128)S(1)}, f32[96,256]{1,0:T(8,128)S(1)}, u32[]{:S(2)}, u32[]{:S(2)}) collective-permute-start(f32[96,256]{1,0:T(8,128)S(1)} %collective-permute-done.2.refs_4_), channel_id=1, source_target_pairs={{0,1},{1,0},{2,3},{3,2},{4,5},{5,4},{6,7},{7,6},{8,9},{9,8},{10,11... | collective-permute-start | bytes 294920 | tf_op jit(solution)/shard_map/ppermute | solution.py:447
  13.2 6.5 %collective-permute-start.10 = (f32[96,256]{1,0:T(8,128)S(1)}, f32[96,256]{1,0:T(8,128)S(1)}, u32[]{:S(2)}, u32[]{:S(2)}) collective-permute-start(f32[96,256]{1,0:T(8,128)S(1)} %get-tuple-element.44), channel_id=1, source_target_pairs={{0,6},{2,4},{4,2},{6,0},{1,7},{3,5},{5,3},{7,1},{8,14},{10,12},{12... | collective-permute-start | bytes 294920 | tf_op jit(solution)/shard_map/ppermute | solution.py:454
  15.0 6.2 %collective-permute-start.9 = (f32[96,256]{1,0:T(8,128)S(1)}, f32[96,256]{1,0:T(8,128)S(1)}, u32[]{:S(2)}, u32[]{:S(2)}) collective-permute-start(f32[96,256]{1,0:T(8,128)S(1)} %get-tuple-element.45), channel_id=1, source_target_pairs={{0,4},{2,6},{4,0},{6,2},{1,5},{3,7},{5,1},{7,3},{8,12},{10,14},{12... | collective-permute-start | bytes 294920 | tf_op jit(solution)/shard_map/ppermute | solution.py:454
  16.4 4.8 %collective-permute-start.8 = (f32[96,256]{1,0:T(8,128)S(1)}, f32[96,256]{1,0:T(8,128)S(1)}, u32[]{:S(2)}, u32[]{:S(2)}) collective-permute-start(f32[96,256]{1,0:T(8,128)S(1)} %get-tuple-element.46), channel_id=1, source_target_pairs={{0,2},{2,0},{4,6},{6,4},{1,3},{3,1},{5,7},{7,5},{8,10},{10,8},{12,... | collective-permute-start | bytes 294920 | tf_op jit(solution)/shard_map/ppermute | solution.py:454
  22.4 8.8 %collective-permute-start.18 = (f32[4,96,256]{2,1,0:T(8,128)S(1)}, f32[4,96,256]{2,1,0:T(8,128)S(1)}, u32[]{:S(2)}, u32[]{:S(2)}) collective-permute-start(f32[4,96,256]{2,1,0:T(8,128)S(1)} %get-tuple-element.26), channel_id=1, source_target_pairs={{0,1},{1,0},{2,3},{3,2},{4,5},{5,4},{6,7},{7,6},{8,9},{9,8},{10,11... | collective-permute-start | bytes 1179656 | tf_op jit(solution)/shard_map/ppermute | solution.py:450
  22.4 6.6 %collective-permute-start.13 = (f32[96,256]{1,0:T(8,128)S(1)}, f32[96,256]{1,0:T(8,128)S(1)}, u32[]{:S(2)}, u32[]{:S(2)}) collective-permute-start(f32[96,256]{1,0:T(8,128)S(1)} %get-tuple-element.24.refs_0_.refs_1_.refs_2_), channel_id=1, source_target_pairs={{0,6},{2,4},{4,2},{6,0},{1,7},{3,5},{5,3},{7,1},{8,14},{10,12},{12... | collective-permute-start | bytes 294920 | tf_op jit(solution)/shard_map/ppermute | solution.py:443
  24.0 6.6 %collective-permute-start.12 = (f32[96,256]{1,0:T(8,128)S(1)}, f32[96,256]{1,0:T(8,128)S(1)}, u32[]{:S(2)}, u32[]{:S(2)}) collective-permute-start(f32[96,256]{1,0:T(8,128)S(1)} %get-tuple-element.24.refs_0_.refs_1_.refs_2_), channel_id=1, source_target_pairs={{0,4},{2,6},{4,0},{6,2},{1,5},{3,7},{5,1},{7,3},{8,12},{10,14},{12... | collective-permute-start | bytes 294920 | tf_op jit(solution)/shard_map/ppermute | solution.py:443
  25.5 5.2 %collective-permute-start.11 = (f32[96,256]{1,0:T(8,128)S(1)}, f32[96,256]{1,0:T(8,128)S(1)}, u32[]{:S(2)}, u32[]{:S(2)}) collective-permute-start(f32[96,256]{1,0:T(8,128)S(1)} %get-tuple-element.24.refs_0_.refs_1_.refs_2_), channel_id=1, source_target_pairs={{0,2},{2,0},{4,6},{6,4},{1,3},{3,1},{5,7},{7,5},{8,10},{10,8},{12,... | collective-permute-start | bytes 294920 | tf_op jit(solution)/shard_map/ppermute | solution.py:443
  26.0 6.8 %collective-permute-start.14 = (f32[96,256]{1,0:T(8,128)S(1)}, f32[96,256]{1,0:T(8,128)S(1)}, u32[]{:S(2)}, u32[]{:S(2)}) collective-permute-start(f32[96,256]{1,0:T(8,128)S(1)} %get-tuple-element.24.refs_0_.refs_1_.refs_2_), channel_id=1, source_target_pairs={{0,1},{1,0},{2,3},{3,2},{4,5},{5,4},{6,7},{7,6},{8,9},{9,8},{10,11... | collective-permute-start | bytes 294920 | tf_op jit(solution)/shard_map/ppermute | solution.py:447
  29.1 5.2 %collective-permute-start.17 = (f32[96,256]{1,0:T(8,128)S(1)}, f32[96,256]{1,0:T(8,128)S(1)}, u32[]{:S(2)}, u32[]{:S(2)}) collective-permute-start(f32[96,256]{1,0:T(8,128)S(1)} %collective-permute-done.13.refs_4_), channel_id=1, source_target_pairs={{0,1},{1,0},{2,3},{3,2},{4,5},{5,4},{6,7},{7,6},{8,9},{9,8},{10,11... | collective-permute-start | bytes 294920 | tf_op jit(solution)/shard_map/ppermute | solution.py:447
  31.2 6.3 %collective-permute-start.21 = (f32[96,256]{1,0:T(8,128)S(1)}, f32[96,256]{1,0:T(8,128)S(1)}, u32[]{:S(2)}, u32[]{:S(2)}) collective-permute-start(f32[96,256]{1,0:T(8,128)S(1)} %get-tuple-element.40), channel_id=1, source_target_pairs={{0,6},{2,4},{4,2},{6,0},{1,7},{3,5},{5,3},{7,1},{8,14},{10,12},{12... | collective-permute-start | bytes 294920 | tf_op jit(solution)/shard_map/ppermute | solution.py:454
  32.8 6.2 %collective-permute-start.20 = (f32[96,256]{1,0:T(8,128)S(1)}, f32[96,256]{1,0:T(8,128)S(1)}, u32[]{:S(2)}, u32[]{:S(2)}) collective-permute-start(f32[96,256]{1,0:T(8,128)S(1)} %get-tuple-element.41), channel_id=1, source_target_pairs={{0,4},{2,6},{4,0},{6,2},{1,5},{3,7},{5,1},{7,3},{8,12},{10,14},{12... | collective-permute-start | bytes 294920 | tf_op jit(solution)/shard_map/ppermute | solution.py:454
  40.0 6.2 %collective-permute-start.24 = (f32[96,256]{1,0:T(8,128)S(1)}, f32[96,256]{1,0:T(8,128)S(1)}, u32[]{:S(2)}, u32[]{:S(2)}) collective-permute-start(f32[96,256]{1,0:T(8,128)S(1)} %get-tuple-element.28.refs_1_.refs_3_), channel_id=1, source_target_pairs={{0,6},{2,4},{4,2},{6,0},{1,7},{3,5},{5,3},{7,1},{8,14},{10,12},{12... | collective-permute-start | bytes 294920 | tf_op jit(solution)/shard_map/ppermute | solution.py:443
  41.5 6.2 %collective-permute-start.23 = (f32[96,256]{1,0:T(8,128)S(1)}, f32[96,256]{1,0:T(8,128)S(1)}, u32[]{:S(2)}, u32[]{:S(2)}) collective-permute-start(f32[96,256]{1,0:T(8,128)S(1)} %get-tuple-element.28.refs_1_.refs_3_), channel_id=1, source_target_pairs={{0,4},{2,6},{4,0},{6,2},{1,5},{3,7},{5,1},{7,3},{8,12},{10,14},{12... | collective-permute-start | bytes 294920 | tf_op jit(solution)/shard_map/ppermute | solution.py:443
  43.5 15.4 %collective-permute-start.25 = (f32[96,256]{1,0:T(8,128)S(1)}, f32[96,256]{1,0:T(8,128)S(1)}, u32[]{:S(2)}, u32[]{:S(2)}) collective-permute-start(f32[96,256]{1,0:T(8,128)S(1)} %get-tuple-element.28.refs_1_.refs_3_), channel_id=1, source_target_pairs={{0,1},{1,0},{2,3},{3,2},{4,5},{5,4},{6,7},{7,6},{8,9},{9,8},{10,11... | collective-permute-start | bytes 294920 | tf_op jit(solution)/shard_map/ppermute | solution.py:447
  46.2 12.7 %collective-permute-start.28 = (f32[96,256]{1,0:T(8,128)S(1)}, f32[96,256]{1,0:T(8,128)S(1)}, u32[]{:S(2)}, u32[]{:S(2)}) collective-permute-start(f32[96,256]{1,0:T(8,128)S(1)} %collective-permute-done.24.refs_4_), channel_id=1, source_target_pairs={{0,1},{1,0},{2,3},{3,2},{4,5},{5,4},{6,7},{7,6},{8,9},{9,8},{10,11... | collective-permute-start | bytes 294920 | tf_op jit(solution)/shard_map/ppermute | solution.py:447
  47.8 11.2 %collective-permute-start.27 = (f32[96,256]{1,0:T(8,128)S(1)}, f32[96,256]{1,0:T(8,128)}, u32[]{:S(2)}, u32[]{:S(2)}) collective-permute-start(f32[96,256]{1,0:T(8,128)S(1)} %collective-permute-done.23.refs_3_), channel_id=1, source_target_pairs={{0,1},{1,0},{2,3},{3,2},{4,5},{5,4},{6,7},{7,6},{8,9},{9,8},{10,11... | collective-permute-start | bytes 294920 | tf_op jit(solution)/shard_map/ppermute | solution.py:447
  47.8 11.2 %collective-permute-start.26 = (f32[96,256]{1,0:T(8,128)S(1)}, f32[96,256]{1,0:T(8,128)}, u32[]{:S(2)}, u32[]{:S(2)}) collective-permute-start(f32[96,256]{1,0:T(8,128)S(1)} %collective-permute-done.22.refs_2_), channel_id=1, source_target_pairs={{0,1},{1,0},{2,3},{3,2},{4,5},{5,4},{6,7},{7,6},{8,9},{9,8},{10,11... | collective-permute-start | bytes 294920 | tf_op jit(solution)/shard_map/ppermute | solution.py:447
  50.7 12.5 %all-to-all-start = ((f32[32,3,96]{2,1,0:T(4,128)}), f32[32,3,96]{2,1,0:T(4,128)S(1)}, u32[]{:S(2)}, u32[]{:S(2)}) async-start(f32[32,3,96]{2,1,0:T(4,128)} %get-tuple-element.27), calls=%async_computation | async-start | bytes 131072 | tf_op jit(solution)/shard_map/all_to_all | solution.py:516
  (17 other events, 109.4 us)
